TPU v7x, 32 devices: a whole 2x2x4 slice. The times are simulated.
32 devices in a mesh: dp: 8 (over y, x, core), tensor: 4 (over z).
Axes of the slice: x: 2, y: 2, z: 4, core: 2. Of those that a mesh axis runs over, the one named last changes fastest.
Arguments:
- tokens: bfloat16 [8192, 2048], P(('dp', 'tensor')), may hold values from -6 to 6
- cotangent: bfloat16 [8192, 2048], P(('dp', 'tensor')), may hold values from -6 to 6
- routes: int32 [8192, 2], P('dp'), may hold values from 0 to 7, all different within a row
- block_ids: int32 [8, 1024], P('dp'), may hold values from 0 to 7, never falling along the last dimension, each value on 1 to 256 neighbouring positions
- attn_gain: bfloat16 [2048], P('dp'), may hold values from 0.25 to 1.75
- q_gain: bfloat16 [2048], P('dp'), may hold values from 0.25 to 1.75
- k_gain: bfloat16 [2048], P('dp'), may hold values from 0.25 to 1.75
- w_query: bfloat16 [2048, 2048], P('dp', 'tensor'), may hold values from -0.125 to 0.125
- w_key: bfloat16 [2048, 2048], P('dp', 'tensor'), may hold values from -0.125 to 0.125
- w_value: bfloat16 [2048, 2048], P('dp', 'tensor'), may hold values from -0.125 to 0.125
- w_out: bfloat16 [2048, 2048], P('tensor', 'dp'), may hold values from -1.5 to 1.5
- ffn_gain: bfloat16 [2048], P('dp'), may hold values from 0.25 to 1.75
- w_router: bfloat16 [2048, 8], P('dp'), may hold values from -0.25 to 0.25
- w_gate: bfloat16 [8, 2048, 1024], P(None, 'dp', 'tensor'), may hold values from -0.125 to 0.125
- w_up: bfloat16 [8, 2048, 1024], P(None, 'dp', 'tensor'), may hold values from -0.125 to 0.125
- w_down: bfloat16 [8, 1024, 2048], P(None, 'tensor', 'dp'), may hold values from -1.5 to 1.5
Outputs:
- output: bfloat16 [8192, 2048], P(('dp', 'tensor'))
- grad_tokens: float32 [8192, 2048], P(('dp', 'tensor'))
- grad_attn_gain: float32 [2048], P(('dp', 'tensor'))
- grad_q_gain: float32 [2048], P(('dp', 'tensor'))
- grad_k_gain: float32 [2048], P(('dp', 'tensor'))
- grad_query: float32 [2048, 2048], P('dp', 'tensor')
- grad_key: float32 [2048, 2048], P('dp', 'tensor')
- grad_value: float32 [2048, 2048], P('dp', 'tensor')
- grad_out: float32 [2048, 2048], P('tensor', 'dp')
- grad_ffn_gain: float32 [2048], P(('dp', 'tensor'))
- grad_router: float32 [2048, 8], P('dp')
- grad_gate: float32 [8, 2048, 1024], P(None, 'dp', 'tensor')
- grad_up: float32 [8, 2048, 1024], P(None, 'dp', 'tensor')
- grad_down: float32 [8, 1024, 2048], P(None, 'tensor', 'dp')
Inputs may be any that keep to these rules, and one draw needn't show every extreme that they name: `routes`: each row names 2 different experts, and every expert is named by some row. `block_ids`: along each sequence the block ids start at 0, never fall and rise by one at a time; a block holds 1 to 256 positions and one block holds exactly 256.
All inputs are finite; a program needn't handle non-finite values.
Results may differ from a plain program's by a relative error of at most 0.03.
Values may be sent and summed in bfloat16 or wider, within the bound.
A program may use at most 320 MiB of HBM per device.

v0:
```python
import math

import jax
import jax.numpy as jnp
from jax import lax
from jax.sharding import PartitionSpec as P

HEAD_DIM = 128
EXPERTS = 8
TOPK = 2
QROWS = 512
CAP = 320


EPSILON = 1e-05
MASKED = -1e30


def rms_scale(source):
    return source * lax.rsqrt(jnp.mean(source * source, axis=-1, keepdims=True) + EPSILON)


def norm_back(source, gain_vec, grad_out):
    inverse = lax.rsqrt(jnp.mean(source * source, axis=-1, keepdims=True) + EPSILON)
    normed = source * inverse
    grad_gain = jnp.sum(grad_out * normed, axis=0)
    scaled = grad_out * gain_vec
    grad_in = inverse * (scaled - normed * jnp.mean(scaled * normed, axis=-1, keepdims=True))
    return (grad_in, grad_gain)


def rope_tables(seq_len, head_dim):
    half_dim = head_dim // 2
    frequency = jnp.exp(
        -math.log(10000.0) * 2.0 * jnp.arange(half_dim, dtype=jnp.float32) / head_dim
    )
    angles = jnp.arange(seq_len, dtype=jnp.float32)[:, None] * frequency[None, :]
    return (
        jnp.concatenate([jnp.cos(angles)] * 2, axis=1),
        jnp.concatenate([jnp.sin(angles)] * 2, axis=1),
    )


def rotate(heads_in, cosine_table, sine_table):
    half_dim = heads_in.shape[-1] // 2
    turned = jnp.concatenate([-heads_in[..., half_dim:], heads_in[..., :half_dim]], axis=-1)
    return heads_in * cosine_table[:, None, :] + turned * sine_table[:, None, :]


def rotate_back(grad_in, cosine_table, sine_table):
    half_dim = grad_in.shape[-1] // 2
    sined = grad_in * sine_table[:, None, :]
    turned = jnp.concatenate([sined[..., half_dim:], -sined[..., :half_dim]], axis=-1)
    return grad_in * cosine_table[:, None, :] + turned


def claim_slots(route_rows):
    seq_len = route_rows.shape[0]
    flat_routes = route_rows.reshape(-1)
    pair_count = flat_routes.shape[0]
    onehot = (flat_routes[:, None] == jnp.arange(EXPERTS, dtype=jnp.int32)[None, :]).astype(
        jnp.int32
    )
    earlier = jnp.cumsum(onehot, axis=0) - onehot
    place_index = jnp.sum(earlier * onehot, axis=1)
    kept_pair = place_index < CAP
    slot_index = jnp.where(kept_pair, flat_routes * CAP + place_index, EXPERTS * CAP)
    pair_index = jnp.arange(pair_count, dtype=jnp.int32)
    filler = jnp.full((EXPERTS * CAP + 1,), pair_count, jnp.int32).at[slot_index].set(pair_index)
    slot_pair = filler[: EXPERTS * CAP]
    slot_owner = jnp.where(slot_pair < pair_count, slot_pair // TOPK, seq_len)
    return (slot_index, slot_pair, slot_owner)


def attend(q_rot, k_rot, value_heads, block_row):
    seq_len, heads_here, head_dim = q_rot.shape
    blocks = seq_len // QROWS
    score_scale = head_dim ** (-0.5)
    q_blocks = q_rot.reshape(blocks, QROWS, heads_here, head_dim)
    id_blocks = block_row.reshape(blocks, QROWS)

    def per_block(block_item):
        q_block, id_block = block_item
        scores = (
            jnp.einsum("qhd,khd->hqk", q_block, k_rot, preferred_element_type=jnp.float32)
            * score_scale
        )
        allowed = block_row[None, None, :] <= id_block[None, :, None]
        scores = jnp.where(allowed, scores, MASKED)
        row_top = jnp.max(scores, axis=-1, keepdims=True)
        row_sum = jnp.sum(jnp.exp(scores - row_top), axis=-1, keepdims=True)
        log_total = row_top + jnp.log(row_sum)
        weights_low = jnp.exp(scores - log_total).astype(jnp.bfloat16)
        mixed_block = jnp.einsum(
            "hqk,khd->qhd", weights_low, value_heads, preferred_element_type=jnp.float32
        )
        return (mixed_block.reshape(QROWS, heads_here * head_dim), log_total[..., 0])

    mixed_blocks, log_totals = lax.map(per_block, (q_blocks, id_blocks))
    return (mixed_blocks.reshape(seq_len, heads_here * head_dim), log_totals)


def attend_back(q_rot, k_rot, value_heads, block_row, log_totals, grad_mixed):
    seq_len, heads_here, head_dim = q_rot.shape
    blocks = seq_len // QROWS
    score_scale = head_dim ** (-0.5)
    q_blocks = q_rot.reshape(blocks, QROWS, heads_here, head_dim)
    g_blocks = grad_mixed.reshape(blocks, QROWS, heads_here, head_dim)
    id_blocks = block_row.reshape(blocks, QROWS)

    def back_block(running, block_item):
        q_block, g_block, id_block, log_block = block_item
        scores = (
            jnp.einsum("qhd,khd->hqk", q_block, k_rot, preferred_element_type=jnp.float32)
            * score_scale
        )
        allowed = block_row[None, None, :] <= id_block[None, :, None]
        scores = jnp.where(allowed, scores, MASKED)
        weights = jnp.exp(scores - log_block[..., None])
        weights_low = weights.astype(jnp.bfloat16)
        grad_weights = jnp.einsum(
            "qhd,khd->hqk", g_block, value_heads, preferred_element_type=jnp.float32
        )
        grad_scores = weights * (
            grad_weights - jnp.sum(weights * grad_weights, axis=-1, keepdims=True)
        )
        grad_low = grad_scores.astype(jnp.bfloat16)
        grad_query = (
            jnp.einsum("hqk,khd->qhd", grad_low, k_rot, preferred_element_type=jnp.float32)
            * score_scale
        )
        grad_key = (
            running[0]
            + jnp.einsum("hqk,qhd->khd", grad_low, q_block, preferred_element_type=jnp.float32)
            * score_scale
        )
        grad_value = running[1] + jnp.einsum(
            "hqk,qhd->khd", weights_low, g_block, preferred_element_type=jnp.float32
        )
        return ((grad_key, grad_value), grad_query)

    zero_heads = jnp.zeros(k_rot.shape, jnp.float32)
    sums_out, grad_query = lax.scan(
        back_block, (zero_heads, zero_heads), (q_blocks, g_blocks, id_blocks, log_totals)
    )
    return (grad_query.reshape(seq_len, heads_here, head_dim), sums_out[0], sums_out[1])


def local(
    tokens,
    cotangent,
    routes,
    block_ids,
    attn_gain,
    q_gain,
    k_gain,
    w_query,
    w_key,
    w_value,
    w_out,
    ffn_gain,
    w_router,
    w_gate,
    w_up,
    w_down,
):
    gathered = (
        lax.all_gather(attn_gain, "dp", axis=0, tiled=True),
        lax.all_gather(q_gain, "dp", axis=0, tiled=True),
        lax.all_gather(k_gain, "dp", axis=0, tiled=True),
        lax.all_gather(ffn_gain, "dp", axis=0, tiled=True),
        lax.all_gather(w_query, "dp", axis=0, tiled=True),
        lax.all_gather(w_key, "dp", axis=0, tiled=True),
        lax.all_gather(w_value, "dp", axis=0, tiled=True),
        lax.all_gather(w_out, "dp", axis=1, tiled=True),
        lax.all_gather(w_router, "dp", axis=0, tiled=True),
        lax.all_gather(w_gate, "dp", axis=1, tiled=True),
        lax.all_gather(w_up, "dp", axis=1, tiled=True),
        lax.all_gather(w_down, "dp", axis=2, tiled=True),
    )
    full_query = gathered[4]
    full_key = gathered[5]
    full_value = gathered[6]
    full_out = gathered[7]
    full_router = gathered[8]
    full_gate = gathered[9]
    full_up = gathered[10]
    full_down = gathered[11]
    model_width = tokens.shape[1]
    local_rows = tokens.shape[0]
    tensor_rank = lax.axis_index("tensor")
    head_cols = full_query.shape[1]
    heads_here = head_cols // HEAD_DIM
    col_start = tensor_rank * head_cols
    attn_scale = gathered[0].astype(jnp.float32)
    query_scale = lax.dynamic_slice_in_dim(gathered[1].astype(jnp.float32), col_start, head_cols)
    key_scale = lax.dynamic_slice_in_dim(gathered[2].astype(jnp.float32), col_start, head_cols)
    ffn_scale = gathered[3].astype(jnp.float32)
    source = tokens.astype(jnp.float32)
    normed_local = (rms_scale(source) * attn_scale).astype(jnp.bfloat16)
    normed = lax.all_gather(normed_local, "tensor", axis=0, tiled=True)
    seq_len = normed.shape[0]
    block_row = block_ids[0]
    cosine_table, sine_table = rope_tables(seq_len, HEAD_DIM)
    query_proj = jnp.dot(normed, full_query, preferred_element_type=jnp.float32)
    key_proj = jnp.dot(normed, full_key, preferred_element_type=jnp.float32)
    value_low = jnp.dot(normed, full_value, preferred_element_type=jnp.float32).astype(jnp.bfloat16)
    query_sq, key_sq = lax.psum(
        (jnp.sum(query_proj * query_proj, axis=1), jnp.sum(key_proj * key_proj, axis=1)), "tensor"
    )
    query_inv = lax.rsqrt(query_sq / model_width + EPSILON)[:, None]
    key_inv = lax.rsqrt(key_sq / model_width + EPSILON)[:, None]
    query_normed = query_proj * query_inv
    key_normed = key_proj * key_inv
    q_rot = rotate(
        (query_normed * query_scale).reshape(seq_len, heads_here, HEAD_DIM),
        cosine_table,
        sine_table,
    ).astype(jnp.bfloat16)
    k_rot = rotate(
        (key_normed * key_scale).reshape(seq_len, heads_here, HEAD_DIM), cosine_table, sine_table
    ).astype(jnp.bfloat16)
    value_heads = value_low.reshape(seq_len, heads_here, HEAD_DIM)
    mixed, log_totals = attend(q_rot, k_rot, value_heads, block_row)
    mixed_low = mixed.astype(jnp.bfloat16)
    attn_branch = lax.psum_scatter(
        jnp.dot(mixed_low, full_out, preferred_element_type=jnp.float32).astype(jnp.bfloat16),
        "tensor",
        scatter_dimension=0,
        tiled=True,
    ).astype(jnp.float32)
    middle = source + attn_branch
    normed_two_local = (rms_scale(middle) * ffn_scale).astype(jnp.bfloat16)
    normed_two, grad_rows = (
        lax.all_gather(normed_two_local, "tensor", axis=0, tiled=True),
        lax.all_gather(cotangent, "tensor", axis=0, tiled=True),
    )
    logits = jnp.dot(normed_two, full_router, preferred_element_type=jnp.float32)
    router_probs = jax.nn.softmax(logits, axis=-1)
    chosen = jnp.take_along_axis(router_probs, routes, axis=1)
    slot_index, slot_pair, slot_owner = claim_slots(routes)
    gate_slot = jnp.concatenate([chosen.reshape(-1), jnp.zeros((1,), jnp.float32)])[
        slot_pair
    ].reshape(EXPERTS, CAP)
    owner_rows = slot_owner.reshape(EXPERTS, CAP)
    padded = jnp.concatenate([normed_two, jnp.zeros((1, model_width), jnp.bfloat16)])

    def expert_forward(combined, expert_item):
        owners, gates, gate_w, up_w, down_w = expert_item
        rows_in = padded[owners]
        gate_part = jnp.dot(rows_in, gate_w, preferred_element_type=jnp.float32)
        up_part = jnp.dot(rows_in, up_w, preferred_element_type=jnp.float32)
        hidden = (jax.nn.silu(gate_part) * up_part).astype(jnp.bfloat16)
        expert_out = jnp.dot(hidden, down_w, preferred_element_type=jnp.float32)
        return (combined.at[owners].add(expert_out * gates[:, None]), (gate_part, up_part))

    combined, kept_parts = lax.scan(
        expert_forward,
        jnp.zeros((seq_len + 1, model_width), jnp.float32),
        (owner_rows, gate_slot, full_gate, full_up, full_down),
    )
    ffn_branch = lax.psum_scatter(
        combined[:seq_len].astype(jnp.bfloat16), "tensor", scatter_dimension=0, tiled=True
    ).astype(jnp.float32)
    output = (middle + ffn_branch).astype(jnp.bfloat16)
    regathered = (
        lax.all_gather(w_query, "dp", axis=0, tiled=True),
        lax.all_gather(w_key, "dp", axis=0, tiled=True),
        lax.all_gather(w_value, "dp", axis=0, tiled=True),
        lax.all_gather(w_out, "dp", axis=1, tiled=True),
        lax.all_gather(w_router, "dp", axis=0, tiled=True),
        lax.all_gather(w_gate, "dp", axis=1, tiled=True),
        lax.all_gather(w_up, "dp", axis=1, tiled=True),
        lax.all_gather(w_down, "dp", axis=2, tiled=True),
    )
    back_query = regathered[0]
    back_key = regathered[1]
    back_value = regathered[2]
    back_out = regathered[3]
    back_router = regathered[4]
    back_gate = regathered[5]
    back_up = regathered[6]
    back_down = regathered[7]
    grad_pad = jnp.concatenate([grad_rows, jnp.zeros((1, model_width), jnp.bfloat16)])

    def expert_backward(grad_in_rows, expert_item):
        owners, gates, gate_w, up_w, down_w, gate_part, up_part = expert_item
        rows_in = padded[owners]
        rows_grad = grad_pad[owners]
        sigmoid_gate = jax.nn.sigmoid(gate_part)
        silu_gate = jax.nn.silu(gate_part)
        hidden = (silu_gate * up_part).astype(jnp.bfloat16)
        grad_expert = (rows_grad.astype(jnp.float32) * gates[:, None]).astype(jnp.bfloat16)
        grad_down_e = jnp.einsum(
            "cf,cd->fd", hidden, grad_expert, preferred_element_type=jnp.float32
        )
        grad_hidden = jnp.einsum(
            "cd,fd->cf", grad_expert, down_w, preferred_element_type=jnp.float32
        )
        gate_dot = jnp.sum(
            hidden.astype(jnp.float32)
            * jnp.einsum("cd,fd->cf", rows_grad, down_w, preferred_element_type=jnp.float32),
            axis=1,
        )
        grad_gate_part = (
            grad_hidden * up_part * sigmoid_gate * (1.0 + gate_part * (1.0 - sigmoid_gate))
        ).astype(jnp.bfloat16)
        grad_up_part = (grad_hidden * silu_gate).astype(jnp.bfloat16)
        grad_gate_e = jnp.einsum(
            "cd,cf->df", rows_in, grad_gate_part, preferred_element_type=jnp.float32
        )
        grad_up_e = jnp.einsum(
            "cd,cf->df", rows_in, grad_up_part, preferred_element_type=jnp.float32
        )
        grad_rows_in = jnp.einsum(
            "cf,df->cd", grad_gate_part, gate_w, preferred_element_type=jnp.float32
        ) + jnp.einsum("cf,df->cd", grad_up_part, up_w, preferred_element_type=jnp.float32)
        return (
            grad_in_rows.at[owners].add(grad_rows_in),
            (grad_gate_e, grad_up_e, grad_down_e, gate_dot),
        )

    grad_two_part, expert_grads = lax.scan(
        expert_backward,
        jnp.zeros((seq_len + 1, model_width), jnp.float32),
        (owner_rows, gate_slot, back_gate, back_up, back_down, kept_parts[0], kept_parts[1]),
    )
    dot_pad = jnp.concatenate([expert_grads[3].reshape(-1), jnp.zeros((1,), jnp.float32)])
    gate_grad = lax.psum(dot_pad[slot_index].reshape(seq_len, TOPK), "tensor")
    expert_ids = jnp.arange(EXPERTS, dtype=jnp.int32)
    grad_probs = jnp.sum(
        gate_grad[:, :, None]
        * (routes[:, :, None] == expert_ids[None, None, :]).astype(jnp.float32),
        axis=1,
    )
    grad_logits = router_probs * (
        grad_probs - jnp.sum(router_probs * grad_probs, axis=1, keepdims=True)
    )
    logits_low = grad_logits.astype(jnp.bfloat16)
    grad_router = jnp.einsum(
        "sd,se->de", normed_two, logits_low, preferred_element_type=jnp.float32
    )
    own_logits = lax.dynamic_slice_in_dim(logits_low, tensor_rank * local_rows, local_rows)
    grad_two = lax.psum_scatter(
        grad_two_part[:seq_len].astype(jnp.bfloat16), "tensor", scatter_dimension=0, tiled=True
    ).astype(jnp.float32) + jnp.einsum(
        "se,de->sd", own_logits, back_router, preferred_element_type=jnp.float32
    )
    grad_middle_norm, grad_ffn_gain = norm_back(middle, ffn_scale, grad_two)
    grad_middle = cotangent.astype(jnp.float32) + grad_middle_norm
    grad_attn_rows = lax.all_gather(grad_middle.astype(jnp.bfloat16), "tensor", axis=0, tiled=True)
    grad_out_w = jnp.einsum(
        "sf,sd->fd", mixed_low, grad_attn_rows, preferred_element_type=jnp.float32
    )
    grad_mixed = jnp.einsum(
        "sd,fd->sf", grad_attn_rows, back_out, preferred_element_type=jnp.float32
    ).astype(jnp.bfloat16)
    grad_q_rot, grad_k_rot, grad_v = attend_back(
        q_rot,
        k_rot,
        value_heads,
        block_row,
        log_totals,
        grad_mixed.reshape(seq_len, heads_here, HEAD_DIM),
    )
    grad_query_normed = rotate_back(grad_q_rot, cosine_table, sine_table).reshape(
        seq_len, head_cols
    )
    grad_key_normed = rotate_back(grad_k_rot, cosine_table, sine_table).reshape(seq_len, head_cols)
    grad_query_gain = jnp.sum(grad_query_normed * query_normed, axis=0)
    grad_key_gain = jnp.sum(grad_key_normed * key_normed, axis=0)
    query_scaled = grad_query_normed * query_scale
    key_scaled = grad_key_normed * key_scale
    query_dot, key_dot = lax.psum(
        (jnp.sum(query_scaled * query_normed, axis=1), jnp.sum(key_scaled * key_normed, axis=1)),
        "tensor",
    )
    grad_query_proj = (
        query_inv * (query_scaled - query_normed * (query_dot / model_width)[:, None])
    ).astype(jnp.bfloat16)
    grad_key_proj = (key_inv * (key_scaled - key_normed * (key_dot / model_width)[:, None])).astype(
        jnp.bfloat16
    )
    grad_value_low = grad_v.reshape(seq_len, head_cols).astype(jnp.bfloat16)
    grad_query_w = jnp.einsum(
        "sd,sf->df", normed, grad_query_proj, preferred_element_type=jnp.float32
    )
    grad_key_w = jnp.einsum("sd,sf->df", normed, grad_key_proj, preferred_element_type=jnp.float32)
    grad_value_w = jnp.einsum(
        "sd,sf->df", normed, grad_value_low, preferred_element_type=jnp.float32
    )
    grad_normed_part = jnp.einsum(
        "sf,df->sd", grad_query_proj, back_query, preferred_element_type=jnp.float32
    )
    grad_normed_part = grad_normed_part + jnp.einsum(
        "sf,df->sd", grad_key_proj, back_key, preferred_element_type=jnp.float32
    )
    grad_normed_part = grad_normed_part + jnp.einsum(
        "sf,df->sd", grad_value_low, back_value, preferred_element_type=jnp.float32
    )
    grad_normed = lax.psum_scatter(
        grad_normed_part.astype(jnp.bfloat16), "tensor", scatter_dimension=0, tiled=True
    ).astype(jnp.float32)
    grad_source_norm, grad_attn_gain = norm_back(source, attn_scale, grad_normed)
    grad_source = grad_middle + grad_source_norm
    zero_cols = jnp.zeros((model_width,), jnp.float32)
    query_gain_full = lax.dynamic_update_slice_in_dim(zero_cols, grad_query_gain, col_start, 0)
    key_gain_full = lax.dynamic_update_slice_in_dim(zero_cols, grad_key_gain, col_start, 0)
    gain_sums = (
        lax.psum_scatter(grad_attn_gain, ("dp", "tensor"), scatter_dimension=0, tiled=True),
        lax.psum_scatter(query_gain_full, ("dp", "tensor"), scatter_dimension=0, tiled=True),
        lax.psum_scatter(key_gain_full, ("dp", "tensor"), scatter_dimension=0, tiled=True),
        lax.psum_scatter(grad_ffn_gain, ("dp", "tensor"), scatter_dimension=0, tiled=True),
    )
    weight_sums = (
        lax.psum_scatter(
            grad_query_w.astype(jnp.bfloat16), "dp", scatter_dimension=0, tiled=True
        ).astype(jnp.float32),
        lax.psum_scatter(
            grad_key_w.astype(jnp.bfloat16), "dp", scatter_dimension=0, tiled=True
        ).astype(jnp.float32),
        lax.psum_scatter(
            grad_value_w.astype(jnp.bfloat16), "dp", scatter_dimension=0, tiled=True
        ).astype(jnp.float32),
        lax.psum_scatter(
            grad_out_w.astype(jnp.bfloat16), "dp", scatter_dimension=1, tiled=True
        ).astype(jnp.float32),
        lax.psum_scatter(
            grad_router.astype(jnp.bfloat16), "dp", scatter_dimension=0, tiled=True
        ).astype(jnp.float32),
        lax.psum_scatter(
            expert_grads[0].astype(jnp.bfloat16), "dp", scatter_dimension=1, tiled=True
        ).astype(jnp.float32),
        lax.psum_scatter(
            expert_grads[1].astype(jnp.bfloat16), "dp", scatter_dimension=1, tiled=True
        ).astype(jnp.float32),
        lax.psum_scatter(
            expert_grads[2].astype(jnp.bfloat16), "dp", scatter_dimension=2, tiled=True
        ).astype(jnp.float32),
    )
    return (
        output,
        grad_source,
        gain_sums[0],
        gain_sums[1],
        gain_sums[2],
        weight_sums[0],
        weight_sums[1],
        weight_sums[2],
        weight_sums[3],
        gain_sums[3],
        weight_sums[4],
        weight_sums[5],
        weight_sums[6],
        weight_sums[7],
    )


def solution(mesh):
    placed = (
        P(("dp", "tensor"), None),
        P(("dp", "tensor"), None),
        P("dp", None),
        P("dp", None),
        P("dp"),
        P("dp"),
        P("dp"),
        P("dp", "tensor"),
        P("dp", "tensor"),
        P("dp", "tensor"),
        P("tensor", "dp"),
        P("dp"),
        P("dp", None),
        P(None, "dp", "tensor"),
        P(None, "dp", "tensor"),
        P(None, "tensor", "dp"),
    )
    return jax.shard_map(
        local,
        mesh=mesh,
        in_specs=placed,
        out_specs=(
            P(("dp", "tensor"), None),
            P(("dp", "tensor"), None),
            P(("dp", "tensor")),
            P(("dp", "tensor")),
            P(("dp", "tensor")),
            P("dp", "tensor"),
            P("dp", "tensor"),
            P("dp", "tensor"),
            P("tensor", "dp"),
            P(("dp", "tensor")),
            P("dp", None),
            P(None, "dp", "tensor"),
            P(None, "dp", "tensor"),
            P(None, "tensor", "dp"),
        ),
        check_vma=False,
    )
```

profile of v0, /device:TPU:0, one launch (start us, length us, event | category | flops | bytes accessed | tf_op | source)
XLA Modules:
  0.0 1979.5 jit_solution(5476672449387233943)
XLA Ops:
  8.6 10.4 all-gather
  27.0 9.0 all-gather.2
  36.0 8.0 all-gather.1
  51.8 71.5 %all-gather.16.cloned.1.call-done = bf16[1024,2048]{1,0:T(8,128)(2,1)} async-done(((bf16[256,2048]{1,0:T(8,128)(2,1)}), bf16[1024,2048]{1,0:T(8,128)(2,1)}) %all-gather.16.cloned.1.call-update) | async-done | bytes 4194320 | tf_op jit(solution)/shard_map/all_gather | solution.py:201
  129.9 21.6 %all-gather.18.cloned.1.call-done = bf16[2048,512]{1,0:T(8,128)(2,1)} async-done(((bf16[256,512]{1,0:T(8,128)(2,1)}), bf16[2048,512]{1,0:T(8,128)(2,1)}) %all-gather.18.cloned.1.call-update) | async-done | bytes 2097168 | tf_op jit(solution)/shard_map/all_gather | solution.py:172
  156.8 12.1 all-reduce.8
  206.2 16.9 while.59
  231.1 8.5 all-gather.3
  239.5 64.4 %reduce-scatter.13.cloned.1.call-done = bf16[256,2048]{1,0:T(8,128)(2,1)} async-done(((bf16[1024,2048]{1,0:T(8,128)(2,1)}), bf16[256,2048]{1,0:T(8,128)(2,1)}) %reduce-scatter.13.cloned.1.call-update) | async-done | bytes 1048592 | tf_op jit(solution)/shard_map/reduce_scatter | solution.py:226
  315.4 8.1 scatter_custom_fusion.2
  323.5 9.2 all_gather.69
  334.0 52.8 %all-gather.34.cloned.1.call-done = bf16[1024,2048]{1,0:T(8,128)(2,1)} async-done(((bf16[256,2048]{1,0:T(8,128)(2,1)}), bf16[1024,2048]{1,0:T(8,128)(2,1)}) %all-gather.34.cloned.1.call-update) | async-done | bytes 4194320 | tf_op jit(solution)/shard_map/all_gather | solution.py:236
  391.6 76.6 %all-gather.26.cloned.1.call-done = bf16[1024,2048]{1,0:T(8,128)(2,1)} async-done(((bf16[256,2048]{1,0:T(8,128)(2,1)}), bf16[1024,2048]{1,0:T(8,128)(2,1)}) %all-gather.26.cloned.1.call-update) | async-done | bytes 4194320 | tf_op jit(solution)/shard_map/all_gather | solution.py:235
  472.9 12.5 gather_fusion.5
  486.6 13.6 gather_fusion.3
  505.1 17.8 all-gather.28.cloned.1.call-done
  522.9 56.0 %all-gather.30.cloned.1.call-done = bf16[8,2048,256]{2,1,0:T(8,128)(2,1)} async-done(((bf16[8,256,256]{2,1,0:T(8,128)(2,1)}), bf16[8,2048,256]{2,1,0:T(8,128)(2,1)}) %all-gather.30.cloned.1.call-update) | async-done | bytes 8388624 | tf_op jit(solution)/shard_map/all_gather | solution.py:178
  579.0 57.8 %all-gather.32.cloned.1.call-done = bf16[8,256,2048]{2,1,0:T(8,128)(2,1)} async-done(((bf16[8,256,256]{2,1,0:T(8,128)(2,1)}), bf16[8,256,2048]{2,1,0:T(8,128)(2,1)}) %all-gather.32.cloned.1.call-update) | async-done | bytes 8388624 | tf_op jit(solution)/shard_map/all_gather | solution.py:179
  641.1 205.5 %while.60 = (s32[]{:T(128)}, f32[1025,2048]{1,0:T(8,128)}, f32[8,320,256]{2,1,0:T(8,128)}, f32[8,320,256]{2,1,0:T(8,128)}, s32[8,320]{1,0:T(8,128)}, /*index=5*/...) while((s32[]{:T(128)}, f32[1025,2048]{1,0:T(8,128)}, ...), condition=%wide.region_19.20_spmd, body=%wide.region_17.19_spmd.sunk | while | flops 1008437184 | bytes 20856960 | solution.py:257
  641.9 7.1 gather_fusion
  655.7 11.1 scatter_fusion
  667.5 7.1 gather_fusion
  681.4 11.1 scatter_fusion
  693.2 7.1 gather_fusion
  707.0 11.1 scatter_fusion
  718.9 7.1 gather_fusion
  732.7 11.1 scatter_fusion
  744.6 7.1 gather_fusion
  758.4 11.1 scatter_fusion
  770.3 7.1 gather_fusion
  784.1 11.1 scatter_fusion
  796.0 7.1 gather_fusion
  809.8 11.1 scatter_fusion
  821.7 7.1 gather_fusion
  835.5 11.1 scatter_fusion
  851.0 333.6 %while.61 = (s32[]{:T(128)}, f32[1025,2048]{1,0:T(8,128)}, bf16[8,2048,256]{2,1,0:T(8,128)(2,1)}, bf16[8,2048,256]{2,1,0:T(8,128)(2,1)}, bf16[8,256,2048]{2,1,0:...) while((s32[]{:T(128)}, f32[1025,2048]{1,0:T(8,128)}, ...), condition=%wide.region_24.25_spmd, body=%wide.region_21.24_spmd.sunk | while | flops 2355529472 | bytes 40165320 | solution.py:323
  863.0 7.1 gather_fusion.2
  875.2 12.3 scatter_fusion.1
  904.6 7.1 gather_fusion.2
  916.8 12.3 scatter_fusion.1
  946.2 7.1 gather_fusion.2
  958.4 12.3 scatter_fusion.1
  987.8 7.1 gather_fusion.2
  1000.0 12.3 scatter_fusion.1
  1029.5 7.1 gather_fusion.2
  1041.7 12.3 scatter_fusion.1
  1083.3 12.3 scatter_fusion.1
  1124.9 12.3 scatter_fusion.1
  1166.6 12.3 scatter_fusion.1
  1191.4 11.8 gather_fusion.4
  1203.7 46.0 %psum.37 = f32[1024,2]{1,0:T(8,128)S(1)} all-reduce(f32[1024,2]{1,0:T(8,128)S(1)} %reshape.400), channel_id=1, replica_groups=mesh['dp'=8,'tensor'=4] {'tensor'}, use_global_device_ids=true, to_apply=%region_26.27 | all-reduce | flops 2048 | bytes 16384 | tf_op jit(solution)/shard_map/psum | solution.py:329
  1250.0 34.4 %reduce-scatter.17.cloned.1.call-done = bf16[256,2048]{1,0:T(8,128)(2,1)} async-done(((bf16[1024,2048]{1,0:T(8,128)(2,1)}), bf16[256,2048]{1,0:T(8,128)(2,1)}) %reduce-scatter.17.cloned.1.call-update) | async-done | bytes 1048592 | tf_op jit(solution)/shard_map/reduce_scatter | solution.py:344
  1298.6 73.2 %all-gather.36.cloned.1.call-done = bf16[1024,2048]{1,0:T(8,128)(2,1)} async-done(((bf16[256,2048]{1,0:T(8,128)(2,1)}), bf16[1024,2048]{1,0:T(8,128)(2,1)}) %all-gather.36.cloned.1.call-update) | async-done | bytes 4194320 | tf_op jit(solution)/shard_map/all_gather | solution.py:351
  1385.6 37.6 %while.62 = (s32[]{:T(128)}, f32[1024,4,128]{0,2,1:T(8,128)S(1)}, f32[1024,4,128]{0,2,1:T(8,128)}, f32[2,512,4,128]{3,1,2,0:T(8,128)}, bf16[2,512,4,128]{3,1,2,0...) while((s32[]{:T(128)}, f32[1024,4,128]{0,2,1:T(8,128)S(1)}, ...), condition=%wide.region_32.33_spmd.clone, body=%wide.region_30.32_spmd.clone.sunk | while | flops 2719217664 | bytes 105974040 | solution.py:143
  1463.6 9.2 all-reduce.7
  1512.0 42.5 %reduce-scatter.33.cloned.1.call-done = bf16[8,256,256]{2,1,0:T(8,128)(2,1)} async-done(((bf16[8,2048,256]{2,1,0:T(8,128)(2,1)}), bf16[8,256,256]{2,1,0:T(8,128)(2,1)}) %reduce-scatter.33.cloned.1.call-update) | async-done | bytes 1048592 | tf_op jit(solution)/shard_map/reduce_scatter | solution.py:434
  1557.2 72.0 %reduce-scatter.31.cloned.1.call-done = bf16[8,256,256]{2,1,0:T(8,128)(2,1)} async-done(((bf16[8,2048,256]{2,1,0:T(8,128)(2,1)}), bf16[8,256,256]{2,1,0:T(8,128)(2,1)}) %reduce-scatter.31.cloned.1.call-update) | async-done | bytes 1048592 | tf_op jit(solution)/shard_map/reduce_scatter | solution.py:431
  1632.5 41.0 %reduce-scatter.27.cloned.1.call-done = bf16[512,256]{1,0:T(8,128)(2,1)} async-done(((bf16[512,2048]{1,0:T(8,128)(2,1)}), bf16[512,256]{1,0:T(8,128)(2,1)}) %reduce-scatter.27.cloned.1.call-update) | async-done | bytes 262160 | tf_op jit(solution)/shard_map/reduce_scatter | solution.py:425
  1675.3 42.6 %reduce-scatter.25.cloned.1.call-done = bf16[256,512]{1,0:T(8,128)(2,1)} async-done(((bf16[2048,512]{1,0:T(8,128)(2,1)}), bf16[256,512]{1,0:T(8,128)(2,1)}) %reduce-scatter.25.cloned.1.call-update) | async-done | bytes 262160 | tf_op jit(solution)/shard_map/reduce_scatter | solution.py:422
  1719.7 42.5 %reduce-scatter.23.cloned.1.call-done = bf16[256,512]{1,0:T(8,128)(2,1)} async-done(((bf16[2048,512]{1,0:T(8,128)(2,1)}), bf16[256,512]{1,0:T(8,128)(2,1)}) %reduce-scatter.23.cloned.1.call-update) | async-done | bytes 262160 | tf_op jit(solution)/shard_map/reduce_scatter | solution.py:419
  1764.0 43.2 %reduce-scatter.21.cloned.1.call-done = bf16[256,512]{1,0:T(8,128)(2,1)} async-done(((bf16[2048,512]{1,0:T(8,128)(2,1)}), bf16[256,512]{1,0:T(8,128)(2,1)}) %reduce-scatter.21.cloned.1.call-update) | async-done | bytes 262160 | tf_op jit(solution)/shard_map/reduce_scatter | solution.py:416
  1809.0 77.3 %reduce-scatter.19.cloned.1.call-done = bf16[256,2048]{1,0:T(8,128)(2,1)} async-done(((bf16[1024,2048]{1,0:T(8,128)(2,1)}), bf16[256,2048]{1,0:T(8,128)(2,1)}) %reduce-scatter.19.cloned.1.call-update) | async-done | bytes 1048592 | tf_op jit(solution)/shard_map/reduce_scatter | solution.py:401
  1888.4 46.3 %all-reduce.6 = (f32[2048]{0:T(1024)S(1)}, f32[2048]{0:T(1024)S(1)}, f32[2048]{0:T(1024)S(1)}, f32[2048]{0:T(1024)S(1)}) all-reduce(f32[2048]{0:T(1024)S(1)} %get-tuple-element.401, f32[2048]{0:T(1024)S(1)} %dynamic_update_slice.40, f32[2048]{0:T(1024)S(1)} %dynamic_update_slice.41, ...), channel_id=6, replica_groups=mesh['dp'=8,'tensor'=4] {'dp','tensor'}, use_global_device_ids=true, to_apply=%region_40.41.clone | all-reduce | flops 8192 | bytes 65536
  1937.0 30.0 %reduce-scatter.15.cloned.1.call-done = bf16[256,2048]{1,0:T(8,128)(2,1)} async-done(((bf16[1024,2048]{1,0:T(8,128)(2,1)}), bf16[256,2048]{1,0:T(8,128)(2,1)}) %reduce-scatter.15.cloned.1.call-update) | async-done | bytes 1048592 | tf_op jit(solution)/shard_map/reduce_scatter | solution.py:262
  (578 shorter events, 559.7 us)
Async XLA Ops:
  7.2 44.7 %all-gather.20.cloned.1.call-start = ((), (), s32[]{:S(2)}) async-start(), calls=%async_computation.14 | async-start | bytes 2359296 | tf_op jit(solution)/shard_map/all_gather | solution.py:173
  7.9 115.4 %all-gather.16.cloned.1.call-start = ((), (), s32[]{:S(2)}) async-start(), calls=%async_computation.12 | async-start | bytes 5242880 | tf_op jit(solution)/shard_map/all_gather | solution.py:201
  20.6 5.1 copy-start.85
  20.6 5.1 copy-start.86
  20.6 5.7 copy-start.40
  23.7 127.8 %all-gather.18.cloned.1.call-start = ((), (), s32[]{:S(2)}) async-start(), calls=%async_computation.13 | async-start | bytes 2359296 | tf_op jit(solution)/shard_map/all_gather | solution.py:172
  24.4 175.2 %all-gather.22.cloned.1.call-start = ((), (), s32[]{:S(2)}) async-start(), calls=%async_computation.15 | async-start | bytes 2359296 | tf_op jit(solution)/shard_map/all_gather | solution.py:174
  25.0 198.2 %all-gather.24.cloned.1.call-start = ((), (), s32[]{:S(2)}) async-start(), calls=%async_computation.16 | async-start | bytes 2359296 | tf_op jit(solution)/shard_map/all_gather | solution.py:175
  25.6 278.4 %reduce-scatter.13.cloned.1.call-start = ((), (), s32[]{:S(2)}) async-start(), calls=%async_computation.17 | async-start | bytes 5242880 | tf_op jit(solution)/shard_map/reduce_scatter | solution.py:226
  44.1 131.2 %copy-start.65 = (f32[512]{0:T(512)}, f32[512]{0:T(512)S(1)}, u32[]{:S(2)}) copy-start(f32[512]{0:T(512)S(1)} %dynamic_slice.72) | copy-start | bytes 6148
  44.2 124.7 %copy-start.67 = (f32[512]{0:T(512)}, f32[512]{0:T(512)S(1)}, u32[]{:S(2)}) copy-start(f32[512]{0:T(512)S(1)} %dynamic_slice.71) | copy-start | bytes 6148
  50.3 148.5 %copy-start.23 = (f32[1024,128]{1,0:T(8,128)}, f32[1024,128]{1,0:T(8,128)S(1)}, u32[]{:S(2)}) copy-start(f32[1024,128]{1,0:T(8,128)S(1)} %pad_maximum_fusion.3) | copy-start | bytes 1572868
  50.5 148.3 %copy-start.29 = (f32[1024,128]{1,0:T(8,128)}, f32[1024,128]{1,0:T(8,128)S(1)}, u32[]{:S(2)}) copy-start(f32[1024,128]{1,0:T(8,128)S(1)} %pad_maximum_fusion.4) | copy-start | bytes 1572868
  156.8 14.3 copy-start.10
  168.9 6.4 copy-start.60
  183.0 6.3 copy-start.22
  223.2 7.0 copy-start
  223.2 7.0 copy-start.2
  223.2 7.0 copy-start.45
  223.2 7.0 copy-start.56
  230.2 73.8 %copy-start.4 = (bf16[256,2048]{1,0:T(8,128)(2,1)S(1)}, bf16[256,2048]{1,0:T(8,128)(2,1)}, u32[]{:S(2)}) copy-start(bf16[256,2048]{1,0:T(8,128)(2,1)} %param.24) | copy-start | bytes 3145732
  230.2 156.6 %all-gather.34.cloned.1.call-start = ((), (), s32[]{:S(2)}) async-start(), calls=%async_computation.23 | async-start | bytes 5242880 | tf_op jit(solution)/shard_map/all_gather | solution.py:236
  231.0 237.2 %all-gather.26.cloned.1.call-start = ((), (), s32[]{:S(2)}) async-start(), calls=%async_computation.18 | async-start | bytes 5242880 | tf_op jit(solution)/shard_map/all_gather | solution.py:235
  239.5 68.3 %copy-start.49 = (f32[8,1,256]{2,1,0:T(1,128)}, f32[8,1,256]{2,1,0:T(1,128)S(1)}, u32[]{:S(2)}) copy-start(f32[8,1,256]{2,1,0:T(1,128)S(1)} %convert_element_type.218) | copy-start | bytes 24580
  307.8 215.1 %all-gather.28.cloned.1.call-start = ((), (), s32[]{:S(2)}) async-start(), calls=%async_computation.19 | async-start | bytes 9437184 | tf_op jit(solution)/shard_map/all_gather | solution.py:177
  308.5 270.4 %all-gather.30.cloned.1.call-start = ((), (), s32[]{:S(2)}) async-start(), calls=%async_computation.20 | async-start | bytes 9437184 | tf_op jit(solution)/shard_map/all_gather | solution.py:178
  309.1 327.6 %all-gather.32.cloned.1.call-start = ((), (), s32[]{:S(2)}) async-start(), calls=%async_computation.21 | async-start | bytes 9437184 | tf_op jit(solution)/shard_map/all_gather | solution.py:179
  309.9 974.6 %reduce-scatter.17.cloned.1.call-start = ((), (), s32[]{:S(2)}) async-start(), calls=%async_computation.24 | async-start | bytes 5242880 | tf_op jit(solution)/shard_map/reduce_scatter | solution.py:344
  309.9 13.6 copy-start.80
  332.8 135.5 %copy-start.52 = (bf16[2048,8]{0,1:T(8,128)(2,1)}, bf16[2048,8]{0,1:T(8,128)(2,1)S(1)}, u32[]{:S(2)}) copy-start(bf16[2048,8]{0,1:T(8,128)(2,1)S(1)} %all_gather.69) | copy-start | bytes 98308
  472.9 13.2 copy-start.43
  1190.6 181.2 %all-gather.36.cloned.1.call-start = ((), (), s32[]{:S(2)}) async-start(), calls=%async_computation.25 | async-start | bytes 5242880 | tf_op jit(solution)/shard_map/all_gather | solution.py:351
  1191.4 58.5 %copy-start.44 = (s32[1024,2]{0,1:T(2,128)S(1)}, s32[1024,2]{0,1:T(2,128)}, u32[]{:S(2)}) copy-start(s32[1024,2]{0,1:T(2,128)} %param.26) | copy-start | bytes 24580
  1191.4 58.5 %copy-start.55 = (f32[1024]{0:T(1024)S(1)}, f32[1024]{0:T(1024)}, u32[]{:S(2)}) copy-start(f32[1024]{0:T(1024)} %copy-done.54) | copy-start | bytes 12292
  1191.4 58.5 %copy-start.63 = (f32[1024]{0:T(1024)S(1)}, f32[1024]{0:T(1024)}, u32[]{:S(2)}) copy-start(f32[1024]{0:T(1024)} %copy-done.62) | copy-start | bytes 12292
  1203.2 46.8 %copy-start.39 = (f32[1024,8]{0,1:T(8,128)S(1)}, f32[1024,8]{0,1:T(8,128)}, u32[]{:S(2)}) copy-start(f32[1024,8]{0,1:T(8,128)} %copy-done.38) | copy-start | bytes 98308
  1203.2 81.2 %copy-start.5 = (bf16[256,2048]{1,0:T(8,128)(2,1)S(1)}, bf16[256,2048]{1,0:T(8,128)(2,1)}, u32[]{:S(2)}) copy-start(bf16[256,2048]{1,0:T(8,128)(2,1)} %param.24) | copy-start | bytes 3145732
  1203.2 81.2 %copy-start.17 = (bf16[256,2048]{1,0:T(8,128)(2,1)S(1)}, bf16[256,2048]{1,0:T(8,128)(2,1)}, u32[]{:S(2)}) copy-start(bf16[256,2048]{1,0:T(8,128)(2,1)} %reduce-scatter.13.cloned.1.call-done) | copy-start | bytes 3145732
  1203.2 81.2 %copy-start.50 = (f32[8,1,256]{2,1,0:T(1,128)S(1)}, f32[8,1,256]{2,1,0:T(1,128)}, u32[]{:S(2)}) copy-start(f32[8,1,256]{2,1,0:T(1,128)} %copy-done.49) | copy-start | bytes 24580
  1203.2 81.2 %copy-start.53 = (bf16[2048,8]{0,1:T(8,128)(2,1)S(1)}, bf16[2048,8]{0,1:T(8,128)(2,1)}, u32[]{:S(2)}) copy-start(bf16[2048,8]{0,1:T(8,128)(2,1)} %copy-done.52) | copy-start | bytes 98308
  1203.2 81.2 %copy-start.74 = (f32[256]{0:T(256)S(1)}, f32[256]{0:T(256)}, u32[]{:S(2)}) copy-start(f32[256]{0:T(256)} %copy-done.73) | copy-start | bytes 3076
  1250.0 38.6 %copy-start.19 = (bf16[256,2048]{1,0:T(8,128)(2,1)S(1)}, bf16[256,2048]{1,0:T(8,128)(2,1)}, u32[]{:S(2)}) copy-start(bf16[256,2048]{1,0:T(8,128)(2,1)} %param.25) | copy-start | bytes 3145732
  1290.5 217.5 %reduce-scatter.29.cloned.1.call-start = ((), (), s32[]{:S(2)}) async-start(), calls=%async_computation.31 | async-start | bytes 36864 | tf_op jit(solution)/shard_map/reduce_scatter | solution.py:428
  1294.0 215.2 %reduce-scatter.35.cloned.1.call-start = ((), (), s32[]{:S(2)}) async-start(), calls=%async_computation.34 | async-start | bytes 9437184 | tf_op jit(solution)/shard_map/reduce_scatter | solution.py:437
  1294.6 259.8 %reduce-scatter.33.cloned.1.call-start = ((), (), s32[]{:S(2)}) async-start(), calls=%async_computation.33 | async-start | bytes 9437184 | tf_op jit(solution)/shard_map/reduce_scatter | solution.py:434
  1295.2 334.0 %reduce-scatter.31.cloned.1.call-start = ((), (), s32[]{:S(2)}) async-start(), calls=%async_computation.32 | async-start | bytes 9437184 | tf_op jit(solution)/shard_map/reduce_scatter | solution.py:431
  1295.8 377.7 %reduce-scatter.27.cloned.1.call-start = ((), (), s32[]{:S(2)}) async-start(), calls=%async_computation.30 | async-start | bytes 2359296 | tf_op jit(solution)/shard_map/reduce_scatter | solution.py:425
  1384.4 333.5 %reduce-scatter.25.cloned.1.call-start = ((), (), s32[]{:S(2)}) async-start(), calls=%async_computation.29 | async-start | bytes 2359296 | tf_op jit(solution)/shard_map/reduce_scatter | solution.py:422
  1407.5 5.1 copy-start.7
  1441.9 320.3 %reduce-scatter.23.cloned.1.call-start = ((), (), s32[]{:S(2)}) async-start(), calls=%async_computation.28 | async-start | bytes 2359296 | tf_op jit(solution)/shard_map/reduce_scatter | solution.py:419
  1458.5 4.5 copy-start.12
  1458.5 4.5 copy-start.13
  1480.3 326.9 %reduce-scatter.21.cloned.1.call-start = ((), (), s32[]{:S(2)}) async-start(), calls=%async_computation.27 | async-start | bytes 2359296 | tf_op jit(solution)/shard_map/reduce_scatter | solution.py:416
  1487.4 399.0 %reduce-scatter.19.cloned.1.call-start = ((), (), s32[]{:S(2)}) async-start(), calls=%async_computation.26 | async-start | bytes 5242880 | tf_op jit(solution)/shard_map/reduce_scatter | solution.py:401
  1501.8 465.2 %reduce-scatter.15.cloned.1.call-start = ((), (), s32[]{:S(2)}) async-start(), calls=%async_computation.22 | async-start | bytes 5242880 | tf_op jit(solution)/shard_map/reduce_scatter | solution.py:262
  1631.9 254.4 %copy-start.6 = (bf16[256,2048]{1,0:T(8,128)(2,1)S(1)}, bf16[256,2048]{1,0:T(8,128)(2,1)}, u32[]{:S(2)}) copy-start(bf16[256,2048]{1,0:T(8,128)(2,1)} %param.24) | copy-start | bytes 3145732
  1631.9 254.4 %copy-start.48 = (f32[8,1,256]{2,1,0:T(1,128)S(1)}, f32[8,1,256]{2,1,0:T(1,128)}, u32[]{:S(2)}) copy-start(f32[8,1,256]{2,1,0:T(1,128)} %copy-done.47) | copy-start | bytes 24580
  1631.9 254.4 %copy-start.72 = (f32[256]{0:T(256)S(1)}, f32[256]{0:T(256)}, u32[]{:S(2)}) copy-start(f32[256]{0:T(256)} %copy-done.71) | copy-start | bytes 3076
  1675.2 213.2 %copy-start.79 = (f32[2048]{0:T(1024)S(1)}, f32[2048]{0:T(1024)}, u32[]{:S(2)}) copy-start(f32[2048]{0:T(1024)} %get-tuple-element.399) | copy-start | bytes 24580
  1675.2 291.8 %copy-start.18 = (bf16[256,2048]{1,0:T(8,128)(2,1)S(1)}, bf16[256,2048]{1,0:T(8,128)(2,1)}, u32[]{:S(2)}) copy-start(bf16[256,2048]{1,0:T(8,128)(2,1)} %reduce-scatter.13.cloned.1.call-done) | copy-start | bytes 3145732
  1675.2 291.8 %copy-start.20 = (bf16[256,2048]{1,0:T(8,128)(2,1)S(1)}, bf16[256,2048]{1,0:T(8,128)(2,1)}, u32[]{:S(2)}) copy-start(bf16[256,2048]{1,0:T(8,128)(2,1)} %param.25) | copy-start | bytes 3145732
  1675.2 291.8 %copy-start.51 = (f32[8,1,256]{2,1,0:T(1,128)S(1)}, f32[8,1,256]{2,1,0:T(1,128)}, u32[]{:S(2)}) copy-start(f32[8,1,256]{2,1,0:T(1,128)} %copy-done.49) | copy-start | bytes 24580
  1675.2 291.8 %copy-start.75 = (f32[256]{0:T(256)S(1)}, f32[256]{0:T(256)}, u32[]{:S(2)}) copy-start(f32[256]{0:T(256)} %copy-done.73) | copy-start | bytes 3076
  1675.3 291.8 %copy-start.78 = (f32[256]{0:T(256)S(1)}, f32[256]{0:T(256)}, u32[]{:S(2)}) copy-start(f32[256]{0:T(256)} %copy-done.77) | copy-start | bytes 3076
  (52 other events, 111.2 us)
Sparse Core Ops, SparseCore 0:
  9.9 30.4 all-gather.19
  42.5 80.7 all-gather.15
  125.2 26.2 all-gather.17
  153.3 27.7 all-gather.21
  182.8 28.0 all-gather.23
  230.3 73.5 reduce-scatter.12
  305.5 81.2 all-gather.33
  389.0 79.2 all-gather.25
  470.1 52.7 all-gather.27
  524.7 54.2 all-gather.29
  580.9 55.8 all-gather.31
  1190.7 93.6 reduce-scatter.16
  1290.6 81.1 all-gather.35
  1375.2 29.8 reduce-scatter.28
  1408.4 71.2 reduce-scatter.34
  1483.0 71.3 reduce-scatter.32
  1557.7 71.3 reduce-scatter.30
  1632.3 41.0 reduce-scatter.26
  1676.7 41.1 reduce-scatter.24
  1721.0 41.1 reduce-scatter.22
  1766.0 41.1 reduce-scatter.20
  1809.5 76.7 reduce-scatter.18
  1888.6 78.3 reduce-scatter.14
where the time goes:
time: 1990 us; the launch traced here: 1980 us
  waiting for transfers between devices  924 us (46%)
  local copies, waits for them, and re-layouts  315 us (16%)
  other arithmetic  291 us (15%)
  matrix products  272 us (14%)
  blocking collectives  159 us (8%)
    scatter-add x8, other arithmetic, expert_backward(): grad_in_rows.at[owners].add(grad_rows_in)  98.6 us
    scatter-add x8, other arithmetic, expert_forward(): combined.at[owners].add(expert_out * gates[:, None])  88.9 us
    reduce_scatter x1, waiting for transfers between devices, local(): lax.psum_scatter(grad_normed_part.astype(jnp.bfloat16), 'tensor', scatter...  77.3 us
    all_gather x1, waiting for transfers between devices, local(): lax.all_gather(normed_two_local, 'tensor', axis=0, tiled=True)  76.6 us
    all_gather x1, waiting for transfers between devices, local(): lax.all_gather(grad_middle.astype(jnp.bfloat16), 'tensor', axis=0, tiled=...  73.2 us
    reduce_scatter x1, waiting for transfers between devices, local(): lax.psum_scatter(expert_grads[0].astype(jnp.bfloat16), 'dp', scatter_dime...  72 us
    all_gather x1, waiting for transfers between devices, local(): normed = lax.all_gather(normed_local, 'tensor', axis=0, tiled=True)  71.5 us
    reduce_scatter x1, waiting for transfers between devices, local(): lax.psum_scatter(jnp.dot(mixed_low, full_out, preferred_element_type=jnp....  64.4 us
  transfers between devices with their start and end apart: 23, of which 18 were waited for; matrix products, arithmetic and copies ran while one was open for 15% of the time, Pallas kernels for 0%

commit v1 on v0

v1 whole, which is shorter than its diff:
```python
import math

import jax
import jax.numpy as jnp
from jax import lax
from jax.sharding import PartitionSpec as P

HEAD_DIM = 128
EXPERTS = 8
TOPK = 2
QROWS = 512
CAP = 320


EPSILON = 1e-05
MASKED = -1e30


def rms_scale(source):
    return source * lax.rsqrt(jnp.mean(source * source, axis=-1, keepdims=True) + EPSILON)


def norm_back(source, gain_vec, grad_out):
    inverse = lax.rsqrt(jnp.mean(source * source, axis=-1, keepdims=True) + EPSILON)
    normed = source * inverse
    grad_gain = jnp.sum(grad_out * normed, axis=0)
    scaled = grad_out * gain_vec
    grad_in = inverse * (scaled - normed * jnp.mean(scaled * normed, axis=-1, keepdims=True))
    return (grad_in, grad_gain)


def rope_tables(seq_len, head_dim):
    half_dim = head_dim // 2
    frequency = jnp.exp(
        -math.log(10000.0) * 2.0 * jnp.arange(half_dim, dtype=jnp.float32) / head_dim
    )
    angles = jnp.arange(seq_len, dtype=jnp.float32)[:, None] * frequency[None, :]
    return (
        jnp.concatenate([jnp.cos(angles)] * 2, axis=1),
        jnp.concatenate([jnp.sin(angles)] * 2, axis=1),
    )


def rotate(heads_in, cosine_table, sine_table):
    half_dim = heads_in.shape[-1] // 2
    turned = jnp.concatenate([-heads_in[..., half_dim:], heads_in[..., :half_dim]], axis=-1)
    return heads_in * cosine_table[:, None, :] + turned * sine_table[:, None, :]


def rotate_back(grad_in, cosine_table, sine_table):
    half_dim = grad_in.shape[-1] // 2
    sined = grad_in * sine_table[:, None, :]
    turned = jnp.concatenate([sined[..., half_dim:], -sined[..., :half_dim]], axis=-1)
    return grad_in * cosine_table[:, None, :] + turned


def attend(q_rot, k_rot, value_heads, block_row):
    seq_len, heads_here, head_dim = q_rot.shape
    blocks = seq_len // QROWS
    score_scale = head_dim ** (-0.5)
    q_blocks = q_rot.reshape(blocks, QROWS, heads_here, head_dim)
    id_blocks = block_row.reshape(blocks, QROWS)

    def per_block(block_item):
        q_block, id_block = block_item
        scores = (
            jnp.einsum("qhd,khd->hqk", q_block, k_rot, preferred_element_type=jnp.float32)
            * score_scale
        )
        allowed = block_row[None, None, :] <= id_block[None, :, None]
        scores = jnp.where(allowed, scores, MASKED)
        row_top = jnp.max(scores, axis=-1, keepdims=True)
        row_sum = jnp.sum(jnp.exp(scores - row_top), axis=-1, keepdims=True)
        log_total = row_top + jnp.log(row_sum)
        weights_low = jnp.exp(scores - log_total).astype(jnp.bfloat16)
        mixed_block = jnp.einsum(
            "hqk,khd->qhd", weights_low, value_heads, preferred_element_type=jnp.float32
        )
        return (mixed_block.reshape(QROWS, heads_here * head_dim), log_total[..., 0])

    mixed_blocks, log_totals = lax.map(per_block, (q_blocks, id_blocks))
    return (mixed_blocks.reshape(seq_len, heads_here * head_dim), log_totals)


def attend_back(q_rot, k_rot, value_heads, block_row, log_totals, grad_mixed):
    seq_len, heads_here, head_dim = q_rot.shape
    blocks = seq_len // QROWS
    score_scale = head_dim ** (-0.5)
    q_blocks = q_rot.reshape(blocks, QROWS, heads_here, head_dim)
    g_blocks = grad_mixed.reshape(blocks, QROWS, heads_here, head_dim)
    id_blocks = block_row.reshape(blocks, QROWS)

    def back_block(running, block_item):
        q_block, g_block, id_block, log_block = block_item
        scores = (
            jnp.einsum("qhd,khd->hqk", q_block, k_rot, preferred_element_type=jnp.float32)
            * score_scale
        )
        allowed = block_row[None, None, :] <= id_block[None, :, None]
        scores = jnp.where(allowed, scores, MASKED)
        weights = jnp.exp(scores - log_block[..., None])
        weights_low = weights.astype(jnp.bfloat16)
        grad_weights = jnp.einsum(
            "qhd,khd->hqk", g_block, value_heads, preferred_element_type=jnp.float32
        )
        grad_scores = weights * (
            grad_weights - jnp.sum(weights * grad_weights, axis=-1, keepdims=True)
        )
        grad_low = grad_scores.astype(jnp.bfloat16)
        grad_query = (
            jnp.einsum("hqk,khd->qhd", grad_low, k_rot, preferred_element_type=jnp.float32)
            * score_scale
        )
        grad_key = (
            running[0]
            + jnp.einsum("hqk,qhd->khd", grad_low, q_block, preferred_element_type=jnp.float32)
            * score_scale
        )
        grad_value = running[1] + jnp.einsum(
            "hqk,qhd->khd", weights_low, g_block, preferred_element_type=jnp.float32
        )
        return ((grad_key, grad_value), grad_query)

    zero_heads = jnp.zeros(k_rot.shape, jnp.float32)
    sums_out, grad_query = lax.scan(
        back_block, (zero_heads, zero_heads), (q_blocks, g_blocks, id_blocks, log_totals)
    )
    return (grad_query.reshape(seq_len, heads_here, head_dim), sums_out[0], sums_out[1])


def kept_mask(route_rows):
    expert_ids = jnp.arange(EXPERTS, dtype=jnp.int32)
    first = (route_rows[:, 0:1] == expert_ids[None, :]).astype(jnp.int32)
    second = (route_rows[:, 1:2] == expert_ids[None, :]).astype(jnp.int32)
    both = first + second
    earlier = jnp.cumsum(both, axis=0) - both
    return jnp.where((both > 0) & (earlier < CAP), 1.0, 0.0).astype(jnp.float32)


def local(
    tokens,
    cotangent,
    routes,
    block_ids,
    attn_gain,
    q_gain,
    k_gain,
    w_query,
    w_key,
    w_value,
    w_out,
    ffn_gain,
    w_router,
    w_gate,
    w_up,
    w_down,
):
    shard_width = w_query.shape[0]
    head_cols = w_query.shape[1]
    ff_here = w_gate.shape[2]
    hidden_cols = EXPERTS * ff_here
    small = jnp.concatenate(
        [attn_gain[:, None], q_gain[:, None], k_gain[:, None], ffn_gain[:, None], w_router], axis=1
    )
    small = lax.all_gather(small, "dp", axis=0, tiled=True)
    w_qkv = lax.all_gather(
        jnp.concatenate([w_query, w_key, w_value], axis=1), "dp", axis=0, tiled=True
    )
    w_o_t = lax.all_gather(w_out.T, "dp", axis=0, tiled=True)
    gate_local = w_gate.transpose(1, 0, 2).reshape(shard_width, hidden_cols)
    up_local = w_up.transpose(1, 0, 2).reshape(shard_width, hidden_cols)
    down_local = w_down.transpose(2, 0, 1).reshape(shard_width, hidden_cols)
    full_gate = lax.all_gather(gate_local, "dp", axis=0, tiled=True)
    full_up = lax.all_gather(up_local, "dp", axis=0, tiled=True)
    full_down = lax.all_gather(down_local, "dp", axis=0, tiled=True)
    full_router = small[:, 4:]
    model_width = tokens.shape[1]
    local_rows = tokens.shape[0]
    tensor_rank = lax.axis_index("tensor")
    heads_here = head_cols // HEAD_DIM
    col_start = tensor_rank * head_cols
    gains = small[:, :4].astype(jnp.float32).T
    attn_scale = gains[0]
    query_scale = lax.dynamic_slice_in_dim(gains[1], col_start, head_cols)
    key_scale = lax.dynamic_slice_in_dim(gains[2], col_start, head_cols)
    ffn_scale = gains[3]
    source = tokens.astype(jnp.float32)
    normed_local = (rms_scale(source) * attn_scale).astype(jnp.bfloat16)
    normed = lax.all_gather(normed_local, "tensor", axis=0, tiled=True)
    seq_len = normed.shape[0]
    block_row = block_ids[0]
    cosine_table, sine_table = rope_tables(seq_len, HEAD_DIM)
    projected = jnp.dot(normed, w_qkv, preferred_element_type=jnp.float32)
    query_proj = projected[:, :head_cols]
    key_proj = projected[:, head_cols : 2 * head_cols]
    value_low = projected[:, 2 * head_cols :].astype(jnp.bfloat16)
    query_sq, key_sq = lax.psum(
        (jnp.sum(query_proj * query_proj, axis=1), jnp.sum(key_proj * key_proj, axis=1)), "tensor"
    )
    query_inv = lax.rsqrt(query_sq / model_width + EPSILON)[:, None]
    key_inv = lax.rsqrt(key_sq / model_width + EPSILON)[:, None]
    query_normed = query_proj * query_inv
    key_normed = key_proj * key_inv
    q_rot = rotate(
        (query_normed * query_scale).reshape(seq_len, heads_here, HEAD_DIM),
        cosine_table,
        sine_table,
    ).astype(jnp.bfloat16)
    k_rot = rotate(
        (key_normed * key_scale).reshape(seq_len, heads_here, HEAD_DIM), cosine_table, sine_table
    ).astype(jnp.bfloat16)
    value_heads = value_low.reshape(seq_len, heads_here, HEAD_DIM)
    mixed, log_totals = attend(q_rot, k_rot, value_heads, block_row)
    mixed_low = mixed.astype(jnp.bfloat16)
    attn_branch = lax.psum_scatter(
        jnp.einsum("sf,df->sd", mixed_low, w_o_t, preferred_element_type=jnp.float32).astype(
            jnp.bfloat16
        ),
        "tensor",
        scatter_dimension=0,
        tiled=True,
    ).astype(jnp.float32)
    middle = source + attn_branch
    normed_two_local = (rms_scale(middle) * ffn_scale).astype(jnp.bfloat16)
    normed_two = lax.all_gather(normed_two_local, "tensor", axis=0, tiled=True)
    grad_rows = lax.all_gather(cotangent, "tensor", axis=0, tiled=True)
    logits = jnp.dot(normed_two, full_router, preferred_element_type=jnp.float32)
    router_probs = jax.nn.softmax(logits, axis=-1)
    kept = kept_mask(routes)
    gate_values = router_probs * kept
    gates = jnp.repeat(gate_values, ff_here, axis=1)

    gate_part = jnp.dot(normed_two, full_gate, preferred_element_type=jnp.float32)
    up_part = jnp.dot(normed_two, full_up, preferred_element_type=jnp.float32)
    sigmoid_gate = jax.nn.sigmoid(gate_part)
    silu_gate = gate_part * sigmoid_gate
    hidden = silu_gate * up_part
    hidden_gated = (hidden * gates).astype(jnp.bfloat16)
    combined = jnp.einsum(
        "sk,dk->sd", hidden_gated, full_down, preferred_element_type=jnp.float32
    ).astype(jnp.bfloat16)
    back_hidden = jnp.dot(grad_rows, full_down, preferred_element_type=jnp.float32)
    gate_dot = jnp.sum((hidden * back_hidden).reshape(seq_len, EXPERTS, ff_here), axis=2)
    grad_hidden = back_hidden * gates
    grad_gate_part = (
        grad_hidden * up_part * sigmoid_gate * (1.0 + gate_part * (1.0 - sigmoid_gate))
    ).astype(jnp.bfloat16)
    grad_up_part = (grad_hidden * silu_gate).astype(jnp.bfloat16)
    grad_two_part = (
        jnp.einsum("sk,dk->sd", grad_gate_part, full_gate, preferred_element_type=jnp.float32)
        + jnp.einsum("sk,dk->sd", grad_up_part, full_up, preferred_element_type=jnp.float32)
    ).astype(jnp.bfloat16)
    grad_gate_w = jnp.einsum(
        "sd,sk->dk", normed_two, grad_gate_part, preferred_element_type=jnp.float32
    ).astype(jnp.bfloat16)
    grad_up_w = jnp.einsum(
        "sd,sk->dk", normed_two, grad_up_part, preferred_element_type=jnp.float32
    ).astype(jnp.bfloat16)
    grad_down_w = jnp.einsum(
        "sd,sk->dk", grad_rows, hidden_gated, preferred_element_type=jnp.float32
    ).astype(jnp.bfloat16)
    ffn_branch = lax.psum_scatter(
        combined, "tensor", scatter_dimension=0, tiled=True
    ).astype(jnp.float32)
    output = (middle + ffn_branch).astype(jnp.bfloat16)
    grad_probs = lax.psum(gate_dot * kept, "tensor")
    grad_logits = router_probs * (
        grad_probs - jnp.sum(router_probs * grad_probs, axis=1, keepdims=True)
    )
    logits_low = grad_logits.astype(jnp.bfloat16)
    grad_router = jnp.einsum(
        "sd,se->de", normed_two, logits_low, preferred_element_type=jnp.float32
    )
    own_logits = lax.dynamic_slice_in_dim(logits_low, tensor_rank * local_rows, local_rows)
    grad_two = lax.psum_scatter(
        grad_two_part, "tensor", scatter_dimension=0, tiled=True
    ).astype(jnp.float32) + jnp.einsum(
        "se,de->sd", own_logits, full_router, preferred_element_type=jnp.float32
    )
    grad_middle_norm, grad_ffn_gain = norm_back(middle, ffn_scale, grad_two)
    grad_middle = cotangent.astype(jnp.float32) + grad_middle_norm
    grad_attn_rows = lax.all_gather(grad_middle.astype(jnp.bfloat16), "tensor", axis=0, tiled=True)
    grad_out_w = jnp.einsum(
        "sf,sd->df", mixed_low, grad_attn_rows, preferred_element_type=jnp.float32
    ).astype(jnp.bfloat16)
    grad_mixed = jnp.dot(grad_attn_rows, w_o_t, preferred_element_type=jnp.float32).astype(
        jnp.bfloat16
    )
    grad_q_rot, grad_k_rot, grad_v = attend_back(
        q_rot,
        k_rot,
        value_heads,
        block_row,
        log_totals,
        grad_mixed.reshape(seq_len, heads_here, HEAD_DIM),
    )
    grad_query_normed = rotate_back(grad_q_rot, cosine_table, sine_table).reshape(
        seq_len, head_cols
    )
    grad_key_normed = rotate_back(grad_k_rot, cosine_table, sine_table).reshape(seq_len, head_cols)
    grad_query_gain = jnp.sum(grad_query_normed * query_normed, axis=0)
    grad_key_gain = jnp.sum(grad_key_normed * key_normed, axis=0)
    query_scaled = grad_query_normed * query_scale
    key_scaled = grad_key_normed * key_scale
    query_dot, key_dot = lax.psum(
        (jnp.sum(query_scaled * query_normed, axis=1), jnp.sum(key_scaled * key_normed, axis=1)),
        "tensor",
    )
    grad_query_proj = (
        query_inv * (query_scaled - query_normed * (query_dot / model_width)[:, None])
    ).astype(jnp.bfloat16)
    grad_key_proj = (key_inv * (key_scaled - key_normed * (key_dot / model_width)[:, None])).astype(
        jnp.bfloat16
    )
    grad_value_low = grad_v.reshape(seq_len, head_cols).astype(jnp.bfloat16)
    grad_qkv = jnp.concatenate([grad_query_proj, grad_key_proj, grad_value_low], axis=1)
    grad_qkv_w = jnp.einsum(
        "sd,sf->df", normed, grad_qkv, preferred_element_type=jnp.float32
    ).astype(jnp.bfloat16)
    grad_normed_part = jnp.einsum(
        "sf,df->sd", grad_qkv, w_qkv, preferred_element_type=jnp.float32
    ).astype(jnp.bfloat16)
    grad_normed = lax.psum_scatter(
        grad_normed_part, "tensor", scatter_dimension=0, tiled=True
    ).astype(jnp.float32)
    grad_source_norm, grad_attn_gain = norm_back(source, attn_scale, grad_normed)
    grad_source = grad_middle + grad_source_norm
    zero_cols = jnp.zeros((model_width,), jnp.float32)
    query_gain_full = lax.dynamic_update_slice_in_dim(zero_cols, grad_query_gain, col_start, 0)
    key_gain_full = lax.dynamic_update_slice_in_dim(zero_cols, grad_key_gain, col_start, 0)
    gain_sums = lax.psum_scatter(
        jnp.stack([grad_attn_gain, query_gain_full, key_gain_full, grad_ffn_gain], axis=1),
        ("dp", "tensor"),
        scatter_dimension=0,
        tiled=True,
    )
    sum_gate = lax.psum_scatter(grad_gate_w, "dp", scatter_dimension=0, tiled=True)
    sum_up = lax.psum_scatter(grad_up_w, "dp", scatter_dimension=0, tiled=True)
    sum_down = lax.psum_scatter(grad_down_w, "dp", scatter_dimension=0, tiled=True)
    sum_out = lax.psum_scatter(grad_out_w, "dp", scatter_dimension=0, tiled=True)
    sum_qkv = lax.psum_scatter(grad_qkv_w, "dp", scatter_dimension=0, tiled=True).astype(
        jnp.float32
    )
    sum_router = lax.psum_scatter(grad_router, "dp", scatter_dimension=0, tiled=True)
    grad_gate = sum_gate.reshape(shard_width, EXPERTS, ff_here).transpose(1, 0, 2)
    grad_up = sum_up.reshape(shard_width, EXPERTS, ff_here).transpose(1, 0, 2)
    grad_down = sum_down.reshape(shard_width, EXPERTS, ff_here).transpose(1, 2, 0)
    return (
        output,
        grad_source,
        gain_sums[:, 0],
        gain_sums[:, 1],
        gain_sums[:, 2],
        sum_qkv[:, :head_cols],
        sum_qkv[:, head_cols : 2 * head_cols],
        sum_qkv[:, 2 * head_cols :],
        sum_out.T.astype(jnp.float32),
        gain_sums[:, 3],
        sum_router,
        grad_gate.astype(jnp.float32),
        grad_up.astype(jnp.float32),
        grad_down.astype(jnp.float32),
    )


def solution(mesh):
    placed = (
        P(("dp", "tensor"), None),
        P(("dp", "tensor"), None),
        P("dp", None),
        P("dp", None),
        P("dp"),
        P("dp"),
        P("dp"),
        P("dp", "tensor"),
        P("dp", "tensor"),
        P("dp", "tensor"),
        P("tensor", "dp"),
        P("dp"),
        P("dp", None),
        P(None, "dp", "tensor"),
        P(None, "dp", "tensor"),
        P(None, "tensor", "dp"),
    )
    return jax.shard_map(
        local,
        mesh=mesh,
        in_specs=placed,
        out_specs=(
            P(("dp", "tensor"), None),
            P(("dp", "tensor"), None),
            P(("dp", "tensor")),
            P(("dp", "tensor")),
            P(("dp", "tensor")),
            P("dp", "tensor"),
            P("dp", "tensor"),
            P("dp", "tensor"),
            P("tensor", "dp"),
            P(("dp", "tensor")),
            P("dp", None),
            P(None, "dp", "tensor"),
            P(None, "dp", "tensor"),
            P(None, "tensor", "dp"),
        ),
        check_vma=False,
    )
```

time: 1990 us -> 1700 us (0.85)
  waiting for transfers between devices: 924 us -> 1200 us
  local copies, waits for them, and re-layouts: 315 us -> 90.3 us
  other arithmetic: 291 us -> 103 us
  blocking collectives: 159 us -> 50.7 us
  matrix products: 272 us -> 236 us
    gather x31 -> x0, local copies, waits for them, and re-layouts: 210 us -> none  [the longest x8 56.9 us: expert_forward(): rows_in = padded[owners]]
    scatter-add x16 -> x0, other arithmetic: 188 us -> none  [the longest x8 98.6 us: expert_backward(): grad_in_rows.at[owners].add(grad_rows_in)]
    unnamed x23 -> x21, waiting for transfers between devices: 6.77 us -> 136 us
    reduce_scatter x12 -> x10, waiting for transfers between devices: 490 us -> 567 us  [the longest x1 75.1 us: local(): lax.psum_scatter(combined, 'tensor', scatter_dimension=0, tiled=True)]
    all_gather x9 -> x7, waiting for transfers between devices: 283 us -> 344 us  [the longest x1 82.8 us: local(): normed_two = lax.all_gather(normed_two_local, 'tensor', axis=0, tiled=True)]
    unnamed x1 -> x0, blocking collectives: 46.3 us -> none
    dot_general x93 -> x16, matrix products: 231 us -> 188 us  [the longest x1 20.4 us: local(): jnp.dot(grad_rows, full_down, preferred_element_type=jnp.float32)]
    all_gather x5 -> x1, blocking collectives: 45.1 us -> 10.6 us  [local(): small = lax.all_gather(small, 'dp', axis=0, tiled=True)]
  transfers between devices with their start and end apart: 23 -> 20, of which waited for: 18 -> 19; matrix products, arithmetic and copies ran while one was open for 15% -> 13% of each run, Pallas kernels for 0% -> 0%
where the time goes in v1:
time: 1700 us; the launch traced here: 1690 us
  waiting for transfers between devices  1200 us (71%)
  matrix products  236 us (14%)
  other arithmetic  103 us (6%)
  local copies, waits for them, and re-layouts  90.3 us (5%)
  blocking collectives  50.7 us (3%)
    unnamed x21, waiting for transfers between devices  136 us
    all_gather x1, waiting for transfers between devices, local(): normed_two = lax.all_gather(normed_two_local, 'tensor', axis=0, tiled=True)  82.8 us
    all_gather x1, waiting for transfers between devices, local(): lax.all_gather(grad_middle.astype(jnp.bfloat16), 'tensor', axis=0, tiled=...  78.6 us
    reduce_scatter x1, waiting for transfers between devices, local(): lax.psum_scatter(combined, 'tensor', scatter_dimension=0, tiled=True)  75.1 us
    reduce_scatter x1, waiting for transfers between devices, local(): lax.psum_scatter(grad_two_part, 'tensor', scatter_dimension=0, tiled=True)  74.2 us
    reduce_scatter x1, waiting for transfers between devices, local(): lax.psum_scatter(grad_gate_w, 'dp', scatter_dimension=0, tiled=True)  71.9 us
    reduce_scatter x1, waiting for transfers between devices, local(): lax.psum_scatter(grad_down_w, 'dp', scatter_dimension=0, tiled=True)  71.7 us
    reduce_scatter x1, waiting for transfers between devices, local(): lax.psum_scatter(jnp.einsum('sf,df->sd', mixed_low, w_o_t, preferred_elem...  71.6 us
  transfers between devices with their start and end apart: 20, of which 19 were waited for; matrix products, arithmetic and copies ran while one was open for 13% of the time, Pallas kernels for 0%

profile of v1, /device:TPU:0, one launch (start us, length us, event | category | flops | bytes accessed | tf_op | source)
XLA Modules:
  0.0 1693.1 jit_solution(1426367260879998874)
XLA Ops:
  10.7 10.6 all_gather.30
  29.9 4.0 multiply_cosine_fusion
  37.5 69.8 %all-gather.10.cloned.1.call-done = bf16[1024,2048]{1,0:T(8,128)(2,1)} async-done(((bf16[256,2048]{1,0:T(8,128)(2,1)}), bf16[1024,2048]{1,0:T(8,128)(2,1)}) %all-gather.10.cloned.1.call-update) | async-done | bytes 4194320 | tf_op jit(solution)/shard_map/all_gather | solution.py:189
  107.3 46.4 %all-gather.12.cloned.1.call-done = bf16[2048,1536]{1,0:T(8,128)(2,1)} async-done(((bf16[256,1536]{1,0:T(8,128)(2,1)}), bf16[2048,1536]{1,0:T(8,128)(2,1)}) %all-gather.12.cloned.1.call-update) | async-done | bytes 6291472 | tf_op jit(solution)/shard_map/all_gather | solution.py:166
  153.7 10.0 fusion.76
  166.7 12.0 all-reduce.1
  178.8 4.0 multiply_bitcast_fusion
  196.1 3.1 copy.80
  199.2 3.8 fusion.45
  206.9 3.5 fusion.47
  210.4 18.3 %while.27 = (s32[]{:T(128)}, bf16[2,512,512]{2,1,0:T(8,128)(2,1)}, f32[2,4,512]{2,1,0:T(4,128)S(1)}, s32[1,1024]{1,0:T(1,128)}, s32[2,512]{1,0:T(2,128)S(1)}, /*...) while((s32[]{:T(128)}, bf16[2,512,512]{2,1,0:T(8,128)(2,1)}, ...), condition=%wide.region_8.9_spmd, body=%wide.region_5.8_spmd.sunk | while | flops 1097332736 | bytes 36776580 | solution.py:81
  228.8 6.6 convolution_convert_fusion.5
  237.9 71.6 %reduce-scatter.14.cloned.1.call-done = bf16[256,2048]{1,0:T(8,128)(2,1)} async-done(((bf16[1024,2048]{1,0:T(8,128)(2,1)}), bf16[256,2048]{1,0:T(8,128)(2,1)}) %reduce-scatter.14.cloned.1.call-update) | async-done | bytes 1048592 | tf_op jit(solution)/shard_map/reduce_scatter | solution.py:215
  319.5 48.9 %all-gather.18.cloned.1.call-done = bf16[2048,2048]{0,1:T(8,128)(2,1)} async-done(((bf16[256,2048]{0,1:T(8,128)(2,1)}), bf16[2048,2048]{0,1:T(8,128)(2,1)}) %all-gather.18.cloned.1.call-update) | async-done | bytes 8388624 | tf_op jit(solution)/shard_map/all_gather | solution.py:173
  368.4 82.8 %all-gather.16.cloned.1.call-done = bf16[1024,2048]{1,0:T(8,128)(2,1)} async-done(((bf16[256,2048]{1,0:T(8,128)(2,1)}), bf16[1024,2048]{1,0:T(8,128)(2,1)}) %all-gather.16.cloned.1.call-update) | async-done | bytes 4194320 | tf_op jit(solution)/shard_map/all_gather | solution.py:225
  451.2 14.7 fusion.77
  465.9 42.2 %all-gather.20.cloned.1.call-done = bf16[2048,2048]{0,1:T(8,128)(2,1)} async-done(((bf16[256,2048]{0,1:T(8,128)(2,1)}), bf16[2048,2048]{0,1:T(8,128)(2,1)}) %all-gather.20.cloned.1.call-update) | async-done | bytes 8388624 | tf_op jit(solution)/shard_map/all_gather | solution.py:174
  508.0 14.6 fusion.78
  522.7 67.7 %all-gather.24.cloned.1.call-done = bf16[1024,2048]{1,0:T(8,128)(2,1)} async-done(((bf16[256,2048]{1,0:T(8,128)(2,1)}), bf16[1024,2048]{1,0:T(8,128)(2,1)}) %all-gather.24.cloned.1.call-update) | async-done | bytes 4194320 | tf_op jit(solution)/shard_map/all_gather | solution.py:226
  590.4 56.3 %all-gather.22.cloned.1.call-done = bf16[2048,2048]{0,1:T(8,128)(2,1)} async-done(((bf16[256,2048]{0,1:T(8,128)(2,1)}), bf16[2048,2048]{0,1:T(8,128)(2,1)}) %all-gather.22.cloned.1.call-update) | async-done | bytes 8388624 | tf_op jit(solution)/shard_map/all_gather | solution.py:175
  646.7 20.4 %multiply_multiply_fusion = (f32[1024,2048]{1,0:T(8,128)}, f32[1024,2048]{1,0:T(8,128)}) fusion(f32[1024,2048]{1,0:T(8,128)} %fusion.78, f32[1024,2048]{1,0:T(8,128)} %fusion.77, bf16[1024,2048]{1,0:T(8,128)(2,1)} %all-gather.24.cloned.1.call-done, bf16[2048,2048]{0,1:T(8,128)(2,1)} %all-gather.22.cloned.1.call-done), kind=kOutput, calls=%fused_computation.59 | convolution fusion | flops 8602517504 | bytes 46137344 | tf_op jit(solution)/shard_map/dot_general | solution.py:242
  667.1 10.7 copy.144
  677.8 5.4 reduce_sum.166
  684.4 19.0 %psum.37 = f32[1024,8]{0,1:T(8,128)S(1)} all-reduce(f32[1024,8]{0,1:T(8,128)S(1)} %get-tuple-element.313), channel_id=1, replica_groups=mesh['dp'=8,'tensor'=4] {'tensor'}, use_global_device_ids=true, to_apply=%region_18.19 | all-reduce | flops 8192 | bytes 65536 | tf_op jit(solution)/shard_map/psum | solution.py:266
  703.4 3.4 fusion.75
  710.1 4.1 copy.143
  714.2 13.6 multiply_convert_fusion.1
  727.8 14.2 fusion.79
  742.0 13.1 add_convert_fusion
  755.2 74.2 %reduce-scatter.18.cloned.1.call-done = bf16[256,2048]{1,0:T(8,128)(2,1)} async-done(((bf16[1024,2048]{1,0:T(8,128)(2,1)}), bf16[256,2048]{1,0:T(8,128)(2,1)}) %reduce-scatter.18.cloned.1.call-update) | async-done | bytes 1048592 | tf_op jit(solution)/shard_map/reduce_scatter | solution.py:275
  829.3 2.9 multiply_reduce_fusion.1
  838.2 78.6 %all-gather.26.cloned.1.call-done = bf16[1024,2048]{1,0:T(8,128)(2,1)} async-done(((bf16[256,2048]{1,0:T(8,128)(2,1)}), bf16[1024,2048]{1,0:T(8,128)(2,1)}) %all-gather.26.cloned.1.call-update) | async-done | bytes 4194320 | tf_op jit(solution)/shard_map/all_gather | solution.py:282
  916.9 6.2 convolution_convert_fusion.7
  925.4 45.9 %while.28 = (s32[]{:T(128)}, f32[1024,4,128]{0,2,1:T(8,128)S(1)}, f32[1024,4,128]{0,2,1:T(8,128)}, f32[2,512,4,128]{3,1,2,0:T(8,128)}, bf16[2,512,4,128]{3,1,2,0...) while((s32[]{:T(128)}, f32[1024,4,128]{0,2,1:T(8,128)S(1)}, ...), condition=%wide.region_23.24_spmd.clone, body=%wide.region_21.23_spmd.clone.sunk | while | flops 2719217664 | bytes 181473200 | solution.py:125
  929.8 3.5 multiply_reduce_fusion.11
  933.3 3.7 multiply_convert_fusion.9
  937.0 3.8 bitcast_add_fusion.4
  943.9 3.8 bitcast_add_fusion.5
  952.1 3.5 multiply_reduce_fusion.11
  955.6 3.7 multiply_convert_fusion.9
  959.3 3.8 bitcast_add_fusion.4
  966.2 5.0 bitcast_add_fusion.5
  971.2 3.2 copy.98
  987.4 4.1 multiply_reduce_fusion.2
  991.5 9.1 all-reduce
  1005.6 4.9 multiply_convert_fusion.5
  1011.8 11.0 convolution_convert_fusion.3
  1022.9 14.0 convolution_convert_fusion
  1037.0 14.5 convolution_convert_fusion.1
  1051.6 14.0 convert_bitcast_fusion
  1066.8 5.9 convolution_convert_fusion.6
  1072.8 14.1 convolution_convert_fusion.4
  1087.1 11.7 reduce-scatter.20.cloned.1.call-done
  1102.3 11.5 convolution_convert_fusion.2
  1114.5 4.2 fusion.80
  1118.8 55.5 %reduce-scatter.30.cloned.1.call-done = bf16[256,2048]{1,0:T(8,128)(2,1)} async-done(((bf16[2048,2048]{1,0:T(8,128)(2,1)}), bf16[256,2048]{1,0:T(8,128)(2,1)}) %reduce-scatter.30.cloned.1.call-update) | async-done | bytes 1048592 | tf_op jit(solution)/shard_map/reduce_scatter | solution.py:338
  1177.2 71.9 %reduce-scatter.28.cloned.1.call-done = bf16[256,2048]{1,0:T(8,128)(2,1)} async-done(((bf16[2048,2048]{1,0:T(8,128)(2,1)}), bf16[256,2048]{1,0:T(8,128)(2,1)}) %reduce-scatter.28.cloned.1.call-update) | async-done | bytes 1048592 | tf_op jit(solution)/shard_map/reduce_scatter | solution.py:337
  1252.1 71.7 %reduce-scatter.32.cloned.1.call-done = bf16[256,2048]{0,1:T(8,128)(2,1)} async-done(((bf16[2048,2048]{0,1:T(8,128)(2,1)}), bf16[256,2048]{0,1:T(8,128)(2,1)}) %reduce-scatter.32.cloned.1.call-update) | async-done | bytes 1048592 | tf_op jit(solution)/shard_map/reduce_scatter | solution.py:339
  1326.7 41.9 %reduce-scatter.24.cloned.1.call-done = bf16[256,512]{1,0:T(8,128)(2,1)} async-done(((bf16[2048,512]{1,0:T(8,128)(2,1)}), bf16[256,512]{1,0:T(8,128)(2,1)}) %reduce-scatter.24.cloned.1.call-update) | async-done | bytes 262160 | tf_op jit(solution)/shard_map/reduce_scatter | solution.py:340
  1372.4 75.1 %reduce-scatter.16.cloned.1.call-done = bf16[256,2048]{1,0:T(8,128)(2,1)} async-done(((bf16[1024,2048]{1,0:T(8,128)(2,1)}), bf16[256,2048]{1,0:T(8,128)(2,1)}) %reduce-scatter.16.cloned.1.call-update) | async-done | bytes 1048592 | tf_op jit(solution)/shard_map/reduce_scatter | solution.py:262
  1447.6 5.4 fusion.37
  1453.0 134.2 %reduce-scatter.34.cloned.1.call-done = f32[64,4]{1,0:T(8,128)} async-done(((f32[2048,4]{1,0:T(8,128)}), f32[64,4]{1,0:T(8,128)}) %reduce-scatter.34.cloned.1.call-update) | async-done | bytes 1040
  1590.5 58.6 %reduce-scatter.22.cloned.1.call-done = bf16[256,1536]{1,0:T(8,128)(2,1)} async-done(((bf16[2048,1536]{1,0:T(8,128)(2,1)}), bf16[256,1536]{1,0:T(8,128)(2,1)}) %reduce-scatter.22.cloned.1.call-update) | async-done | bytes 786448 | tf_op jit(solution)/shard_map/reduce_scatter | solution.py:341
  1651.4 34.7 %reduce-scatter.26.cloned.1.call-done = f32[256,8]{0,1:T(8,128)} async-done(((f32[2048,8]{0,1:T(8,128)}), f32[256,8]{0,1:T(8,128)}) %reduce-scatter.26.cloned.1.call-update) | async-done | bytes 8208 | tf_op jit(solution)/shard_map/reduce_scatter | solution.py:344
  (326 shorter events, 137.0 us)
Async XLA Ops:
  7.2 100.1 %all-gather.10.cloned.1.call-start = ((), (), s32[]{:S(2)}) async-start(), calls=%async_computation.11 | async-start | bytes 5242880 | tf_op jit(solution)/shard_map/all_gather | solution.py:189
  21.9 810.3 %copy-start.46 = (f32[1,2048]{1,0:T(1,128)}, f32[1,2048]{1,0:T(1,128)S(1)}, u32[]{:S(2)}) copy-start(f32[1,2048]{1,0:T(1,128)S(1)} %get-tuple-element.347) | copy-start | bytes 24580
  21.9 4.2 copy-start.39
  21.9 4.2 copy-start.40
  21.9 4.2 copy-start.41
  26.1 127.6 %all-gather.12.cloned.1.call-start = ((), (), s32[]{:S(2)}) async-start(), calls=%async_computation.12 | async-start | bytes 7077888 | tf_op jit(solution)/shard_map/all_gather | solution.py:166
  27.1 201.6 %all-gather.14.cloned.1.call-start = ((), (), s32[]{:S(2)}) async-start(), calls=%async_computation.13 | async-start | bytes 2359296 | tf_op jit(solution)/shard_map/all_gather | solution.py:169
  27.9 281.7 %reduce-scatter.14.cloned.1.call-start = ((), (), s32[]{:S(2)}) async-start(), calls=%async_computation.14 | async-start | bytes 5242880 | tf_op jit(solution)/shard_map/reduce_scatter | solution.py:215
  36.2 170.8 %copy-start.18 = (f32[1024,128]{1,0:T(8,128)}, f32[1024,128]{1,0:T(8,128)S(1)}, u32[]{:S(2)}) copy-start(f32[1024,128]{1,0:T(8,128)S(1)} %get-tuple-element.368) | copy-start | bytes 1572868
  36.2 170.8 %copy-start.27 = (f32[1024,128]{1,0:T(8,128)}, f32[1024,128]{1,0:T(8,128)S(1)}, u32[]{:S(2)}) copy-start(f32[1024,128]{1,0:T(8,128)S(1)} %get-tuple-element.369) | copy-start | bytes 1572868
  37.5 141.4 %copy-start.58 = (f32[1,512]{1,0:T(1,128)}, f32[1,512]{1,0:T(1,128)S(1)}, u32[]{:S(2)}) copy-start(f32[1,512]{1,0:T(1,128)S(1)} %get-tuple-element.362) | copy-start | bytes 6148
  37.5 141.4 %copy-start.60 = (f32[1,512]{1,0:T(1,128)}, f32[1,512]{1,0:T(1,128)S(1)}, u32[]{:S(2)}) copy-start(f32[1,512]{1,0:T(1,128)S(1)} %get-tuple-element.363) | copy-start | bytes 6148
  228.7 6.6 copy-start.5
  228.7 6.6 copy-start.44
  228.7 6.6 copy-start.50
  235.4 74.2 %copy-start.9 = (bf16[256,2048]{1,0:T(8,128)(2,1)S(1)}, bf16[256,2048]{1,0:T(8,128)(2,1)}, u32[]{:S(2)}) copy-start(bf16[256,2048]{1,0:T(8,128)(2,1)} %param.20) | copy-start | bytes 3145732
  235.4 133.1 %all-gather.18.cloned.1.call-start = ((), (), s32[]{:S(2)}) async-start(), calls=%async_computation.16 | async-start | bytes 9437184 | tf_op jit(solution)/shard_map/all_gather | solution.py:173
  237.9 213.3 %all-gather.16.cloned.1.call-start = ((), (), s32[]{:S(2)}) async-start(), calls=%async_computation.15 | async-start | bytes 5242880 | tf_op jit(solution)/shard_map/all_gather | solution.py:225
  311.3 521.0 %copy-start.64 = (f32[256]{0:T(256)}, f32[256]{0:T(256)S(1)}, u32[]{:S(2)}) copy-start(f32[256]{0:T(256)S(1)} %add_rsqrt_fusion.2) | copy-start | bytes 3076
  312.8 195.2 %all-gather.20.cloned.1.call-start = ((), (), s32[]{:S(2)}) async-start(), calls=%async_computation.17 | async-start | bytes 9437184 | tf_op jit(solution)/shard_map/all_gather | solution.py:174
  315.2 275.2 %all-gather.24.cloned.1.call-start = ((), (), s32[]{:S(2)}) async-start(), calls=%async_computation.20 | async-start | bytes 5242880 | tf_op jit(solution)/shard_map/all_gather | solution.py:226
  315.9 330.8 %all-gather.22.cloned.1.call-start = ((), (), s32[]{:S(2)}) async-start(), calls=%async_computation.18 | async-start | bytes 9437184 | tf_op jit(solution)/shard_map/all_gather | solution.py:175
  316.7 512.7 %reduce-scatter.18.cloned.1.call-start = ((), (), s32[]{:S(2)}) async-start(), calls=%async_computation.21 | async-start | bytes 5242880 | tf_op jit(solution)/shard_map/reduce_scatter | solution.py:275
  677.8 25.6 %copy-start.43 = (bf16[2048,12]{0,1:T(8,128)(2,1)S(1)}, bf16[2048,12]{0,1:T(8,128)(2,1)}, u32[]{:S(2)}) copy-start(bf16[2048,12]{0,1:T(8,128)(2,1)} %copy-done.42) | copy-start | bytes 147460
  706.9 122.4 %copy-start.52 = (bf16[1024,8]{0,1:T(8,128)(2,1)}, bf16[1024,8]{0,1:T(8,128)(2,1)S(1)}, u32[]{:S(2)}) copy-start(bf16[1024,8]{0,1:T(8,128)(2,1)S(1)} %get-tuple-element.341) | copy-start | bytes 49156
  727.8 14.2 copy-start.30
  727.8 14.2 copy-start.31
  755.1 161.7 %all-gather.26.cloned.1.call-start = ((), (), s32[]{:S(2)}) async-start(), calls=%async_computation.22 | async-start | bytes 5242880 | tf_op jit(solution)/shard_map/all_gather | solution.py:282
  829.3 4.3 copy-start.21
  835.4 263.3 %reduce-scatter.20.cloned.1.call-start = ((), (), s32[]{:S(2)}) async-start(), calls=%async_computation.23 | async-start | bytes 5242880 | tf_op jit(solution)/shard_map/reduce_scatter | solution.py:323
  927.8 5.5 copy-start
  929.0 4.3 copy-start.3
  937.0 6.1 copy-start.1
  950.1 5.5 copy-start
  951.3 4.3 copy-start.3
  959.3 6.1 copy-start.1
  982.2 4.6 copy-start.26
  982.9 8.6 copy-start.14
  982.9 8.6 copy-start.15
  982.9 4.5 copy-start.12
  982.9 4.5 copy-start.55
  982.9 4.5 copy-start.57
  982.9 4.5 copy-start.59
  982.9 4.5 copy-start.61
  1005.6 6.2 copy-start.37
  1022.8 151.5 %reduce-scatter.30.cloned.1.call-start = ((), (), s32[]{:S(2)}) async-start(), calls=%async_computation.28 | async-start | bytes 9437184 | tf_op jit(solution)/shard_map/reduce_scatter | solution.py:338
  1036.9 212.2 %reduce-scatter.28.cloned.1.call-start = ((), (), s32[]{:S(2)}) async-start(), calls=%async_computation.27 | async-start | bytes 9437184 | tf_op jit(solution)/shard_map/reduce_scatter | solution.py:337
  1051.5 272.3 %reduce-scatter.32.cloned.1.call-start = ((), (), s32[]{:S(2)}) async-start(), calls=%async_computation.29 | async-start | bytes 9437184 | tf_op jit(solution)/shard_map/reduce_scatter | solution.py:339
  1065.6 303.0 %reduce-scatter.24.cloned.1.call-start = ((), (), s32[]{:S(2)}) async-start(), calls=%async_computation.25 | async-start | bytes 2359296 | tf_op jit(solution)/shard_map/reduce_scatter | solution.py:340
  1072.8 374.8 %reduce-scatter.16.cloned.1.call-start = ((), (), s32[]{:S(2)}) async-start(), calls=%async_computation.19 | async-start | bytes 5242880 | tf_op jit(solution)/shard_map/reduce_scatter | solution.py:262
  1086.9 11.9 copy-start.10
  1086.9 11.9 copy-start.49
  1086.9 11.9 copy-start.63
  1086.9 13.9 copy-start.69
  1087.0 500.2 %reduce-scatter.34.cloned.1.call-start = ((), (), s32[]{:S(2)}) async-start(), calls=%async_computation.30 | async-start | bytes 1081344
  1087.1 15.3 copy-start.33
  1087.1 15.3 copy-start.35
  1102.3 546.8 %reduce-scatter.22.cloned.1.call-start = ((), (), s32[]{:S(2)}) async-start(), calls=%async_computation.24 | async-start | bytes 7077888 | tf_op jit(solution)/shard_map/reduce_scatter | solution.py:341
  1113.8 572.3 %reduce-scatter.26.cloned.1.call-start = ((), (), s32[]{:S(2)}) async-start(), calls=%async_computation.26 | async-start | bytes 73728 | tf_op jit(solution)/shard_map/reduce_scatter | solution.py:344
  1323.8 123.8 %copy-start.17 = (bf16[256,2048]{1,0:T(8,128)(2,1)S(1)}, bf16[256,2048]{1,0:T(8,128)(2,1)}, u32[]{:S(2)}) copy-start(bf16[256,2048]{1,0:T(8,128)(2,1)} %reduce-scatter.14.cloned.1.call-done) | copy-start | bytes 3145732
  1323.8 123.8 %copy-start.22 = (bf16[256,2048]{1,0:T(8,128)(2,1)S(1)}, bf16[256,2048]{1,0:T(8,128)(2,1)}, u32[]{:S(2)}) copy-start(bf16[256,2048]{1,0:T(8,128)(2,1)} %param.21) | copy-start | bytes 3145732
  1323.8 123.8 %copy-start.47 = (f32[1,2048]{1,0:T(1,128)S(1)}, f32[1,2048]{1,0:T(1,128)}, u32[]{:S(2)}) copy-start(f32[1,2048]{1,0:T(1,128)} %copy-done.46) | copy-start | bytes 24580
  1323.8 123.8 %copy-start.65 = (f32[256]{0:T(256)S(1)}, f32[256]{0:T(256)}, u32[]{:S(2)}) copy-start(f32[256]{0:T(256)} %copy-done.64) | copy-start | bytes 3076
  1323.8 123.8 %copy-start.67 = (f32[256]{0:T(256)S(1)}, f32[256]{0:T(256)}, u32[]{:S(2)}) copy-start(f32[256]{0:T(256)} %copy-done.66) | copy-start | bytes 3076
  (39 other events, 101.9 us)
Sparse Core Ops, SparseCore 0:
  26.2 81.0 all-gather.9
  109.8 43.8 all-gather.11
  155.5 28.0 all-gather.13
  235.5 74.0 reduce-scatter.13
  311.9 56.5 all-gather.17
  370.4 80.7 all-gather.15
  453.7 54.3 all-gather.19
  509.6 80.7 all-gather.23
  592.3 54.3 all-gather.21
  755.2 74.0 reduce-scatter.17
  835.6 81.2 all-gather.25
  1022.9 75.7 reduce-scatter.19
  1102.2 72.0 reduce-scatter.29
  1177.6 71.4 reduce-scatter.27
  1252.4 71.2 reduce-scatter.31
  1327.5 41.0 reduce-scatter.23
  1370.7 76.7 reduce-scatter.15
  1449.7 137.4 reduce-scatter.33
  1590.6 58.5 reduce-scatter.21
  1652.5 33.5 reduce-scatter.25

commit v2 on v1

--- a/solution.py
+++ b/solution.py
@@ -3,6 +3,8 @@
 import jax
 import jax.numpy as jnp
 from jax import lax
+from jax.experimental import pallas as pl
+from jax.experimental.pallas import tpu as pltpu
 from jax.sharding import PartitionSpec as P
 
 HEAD_DIM = 128
@@ -14,6 +16,8 @@
 
 EPSILON = 1e-05
 MASKED = -1e30
+MESH = pl.DeviceIdType.MESH
+CHUNKS = 8
 
 
 def rms_scale(source):
@@ -137,6 +141,415 @@
     return jnp.where((both > 0) & (earlier < CAP), 1.0, 0.0).astype(jnp.float32)
 
 
+def neighbour_barrier(me, count):
+    barrier = pltpu.get_barrier_semaphore()
+
+    @pl.when(me > 0)
+    def _():
+        pl.semaphore_signal(barrier, inc=1, device_id={"tensor": me - 1}, device_id_type=MESH)
+
+    @pl.when(me < count - 1)
+    def _():
+        pl.semaphore_signal(barrier, inc=1, device_id={"tensor": me + 1}, device_id_type=MESH)
+
+    pl.semaphore_wait(
+        barrier, jnp.minimum(me, 1).astype(jnp.int32) + jnp.minimum(count - 1 - me, 1)
+    )
+
+
+def line_exchange(
+    count, chunks, rows, width, part, extras, out_shapes, epilogue, gather, collective_id, prologue=None
+):
+    reduce = part is not None
+    n_extra = len(extras)
+    n_out = len(out_shapes)
+    last = count - 1
+    back_lag = 2 if reduce else 0
+    pass_lag = (back_lag + 1) if reduce else chunks
+
+    def kernel(*refs):
+        refs = list(refs)
+        part_ref = refs.pop(0) if reduce else None
+        extra_refs = [refs.pop(0) for _ in range(n_extra)]
+        full_ref = refs.pop(0) if gather else None
+        out_refs = [refs.pop(0) for _ in range(n_out)]
+        if reduce:
+            sum_right, sum_left, acc = refs.pop(0), refs.pop(0), refs.pop(0)
+            rs_send_r, rs_recv_r, rs_send_l, rs_recv_l = [refs.pop(0) for _ in range(4)]
+        if gather:
+            ag_send_r, ag_recv_r, ag_send_l, ag_recv_l = [refs.pop(0) for _ in range(4)]
+        me = lax.axis_index("tensor")
+        right, left = jnp.minimum(me + 1, last), jnp.maximum(me - 1, 0)
+
+        def remote(source, target, send_sem, recv_sem, device):
+            return pltpu.make_async_remote_copy(
+                src_ref=source,
+                dst_ref=target,
+                send_sem=send_sem,
+                recv_sem=recv_sem,
+                device_id={"tensor": device},
+                device_id_type=MESH,
+            )
+
+        def rs_right(block, chunk, source=None):
+            here = sum_right.at[block, chunk]
+            return remote(
+                here if source is None else source,
+                here,
+                rs_send_r.at[block, chunk],
+                rs_recv_r.at[block, chunk],
+                right,
+            )
+
+        def rs_left(block, chunk, source=None):
+            here = sum_left.at[block, chunk]
+            return remote(
+                here if source is None else source,
+                here,
+                rs_send_l.at[block, chunk],
+                rs_recv_l.at[block, chunk],
+                left,
+            )
+
+        def ag_right(block, chunk):
+            here = full_ref.at[block, chunk]
+            return remote(
+                here, here, ag_send_r.at[block, chunk], ag_recv_r.at[block, chunk], right
+            )
+
+        def ag_left(block, chunk):
+            here = full_ref.at[block, chunk]
+            return remote(here, here, ag_send_l.at[block, chunk], ag_recv_l.at[block, chunk], left)
+
+        neighbour_barrier(me, count)
+        if prologue is not None:
+            prologue(extra_refs, out_refs)
+
+        def send_sums(chunk):
+            for step in range(last):
+                far = last - step
+
+                @pl.when(jnp.logical_and(me < far, me == 0))
+                def _():
+                    rs_right(far, chunk, part_ref.at[far, chunk]).start()
+
+                @pl.when(jnp.logical_and(me < far, me > 0))
+                def _():
+                    rs_right(far, chunk).wait_recv()
+                    sum_right[far, chunk] = sum_right[far, chunk] + part_ref[far, chunk]
+                    rs_right(far, chunk).start()
+
+                @pl.when(jnp.logical_and(me > step, me == last))
+                def _():
+                    rs_left(step, chunk, part_ref.at[step, chunk]).start()
+
+                @pl.when(jnp.logical_and(me > step, me < last))
+                def _():
+                    rs_left(step, chunk).wait_recv()
+                    sum_left[step, chunk] = sum_left[step, chunk] + part_ref[step, chunk]
+                    rs_left(step, chunk).start()
+
+        def finish(chunk):
+            if reduce:
+                acc[...] = part_ref[me, chunk].astype(jnp.float32)
+
+                @pl.when(me > 0)
+                def _():
+                    rs_right(me, chunk).wait_recv()
+                    acc[...] = acc[...] + sum_right[me, chunk].astype(jnp.float32)
+
+                @pl.when(me < last)
+                def _():
+                    rs_left(me, chunk).wait_recv()
+                    acc[...] = acc[...] + sum_left[me, chunk].astype(jnp.float32)
+
+                made = epilogue(chunk, acc[...], extra_refs, out_refs)
+            else:
+                made = epilogue(chunk, None, extra_refs, out_refs)
+            if gather:
+                full_ref[me, chunk] = made
+
+                @pl.when(me < last)
+                def _():
+                    ag_right(me, chunk).start()
+
+                @pl.when(me > 0)
+                def _():
+                    ag_left(me, chunk).start()
+
+        def forward(chunk):
+            for step in range(1, count):
+
+                @pl.when(me - step >= 0)
+                def _():
+                    ag_right(jnp.maximum(me - step, 0), chunk).wait_recv()
+
+                @pl.when(jnp.logical_and(me - step >= 0, me < last))
+                def _():
+                    ag_right(jnp.maximum(me - step, 0), chunk).start()
+
+                @pl.when(me + step <= last)
+                def _():
+                    ag_left(jnp.minimum(me + step, last), chunk).wait_recv()
+
+                @pl.when(jnp.logical_and(me + step <= last, me > 0))
+                def _():
+                    ag_left(jnp.minimum(me + step, last), chunk).start()
+
+        def tick(time, carry):
+            if reduce:
+
+                @pl.when(time < chunks)
+                def _():
+                    send_sums(time)
+
+            @pl.when(jnp.logical_and(time >= back_lag, time < back_lag + chunks))
+            def _():
+                finish(time - back_lag)
+
+            if gather:
+
+                @pl.when(time >= pass_lag)
+                def _():
+                    forward(time - pass_lag)
+
+            return carry
+
+        ticks = chunks + (pass_lag if gather else back_lag)
+        lax.fori_loop(0, ticks, tick, 0)
+
+        def drain(chunk, carry):
+            for block in range(count):
+                if reduce:
+
+                    @pl.when(me < block)
+                    def _():
+                        rs_right(block, chunk).wait_send()
+
+                    @pl.when(me > block)
+                    def _():
+                        rs_left(block, chunk).wait_send()
+
+                if gather:
+
+                    @pl.when(jnp.logical_and(block <= me, me < last))
+                    def _():
+                        ag_right(block, chunk).wait_send()
+
+                    @pl.when(jnp.logical_and(block >= me, me > 0))
+                    def _():
+                        ag_left(block, chunk).wait_send()
+
+            return carry
+
+        lax.fori_loop(0, chunks, drain, 0)
+
+    block = (count, chunks, rows, width)
+    shapes = []
+    if gather:
+        shapes.append(jax.ShapeDtypeStruct(block, jnp.bfloat16))
+    shapes.extend(out_shapes)
+    scratch = []
+    if reduce:
+        scratch += [
+            pltpu.VMEM(block, jnp.bfloat16),
+            pltpu.VMEM(block, jnp.bfloat16),
+            pltpu.VMEM((rows, width), jnp.float32),
+        ]
+        scratch += [pltpu.SemaphoreType.DMA((count, chunks))] * 4
+    if gather:
+        scratch += [pltpu.SemaphoreType.DMA((count, chunks))] * 4
+    operands = ([part] if reduce else []) + list(extras)
+    block_bytes = count * chunks * rows * width * 2
+    results = pl.pallas_call(
+        kernel,
+        out_shape=tuple(shapes),
+        in_specs=[pl.BlockSpec(memory_space=pltpu.VMEM)] * len(operands),
+        out_specs=tuple([pl.BlockSpec(memory_space=pltpu.VMEM)] * len(shapes)),
+        scratch_shapes=scratch,
+        compiler_params=pltpu.CompilerParams(
+            collective_id=collective_id, has_side_effects=True, vmem_limit_bytes=56 * 1024 * 1024
+        ),
+        cost_estimate=pl.CostEstimate(
+            flops=0,
+            bytes_accessed=block_bytes * (60 if reduce and gather else 45),
+            transcendentals=0,
+        ),
+    )(*operands)
+    return results
+
+
+def small_sum(count, values, collective_id):
+    def kernel(in_ref, out_ref, slots, send_sems, recv_sems):
+        me = lax.axis_index("tensor")
+        barrier = pltpu.get_barrier_semaphore()
+        for offset in range(1, count):
+            peer = lax.rem(me + offset, count)
+            pl.semaphore_signal(barrier, inc=1, device_id={"tensor": peer}, device_id_type=MESH)
+        pl.semaphore_wait(barrier, count - 1)
+
+        def send(offset):
+            return pltpu.make_async_remote_copy(
+                src_ref=in_ref,
+                dst_ref=slots.at[offset - 1],
+                send_sem=send_sems.at[offset - 1],
+                recv_sem=recv_sems.at[offset - 1],
+                device_id={"tensor": lax.rem(me + offset, count)},
+                device_id_type=MESH,
+            )
+
+        for offset in range(1, count):
+            send(offset).start()
+        total = in_ref[...]
+        for offset in range(1, count):
+            send(offset).wait_recv()
+            total = total + slots[offset - 1]
+        out_ref[...] = total
+        for offset in range(1, count):
+            send(offset).wait_send()
+
+    return pl.pallas_call(
+        kernel,
+        out_shape=jax.ShapeDtypeStruct(values.shape, jnp.float32),
+        in_specs=[pl.BlockSpec(memory_space=pltpu.VMEM)],
+        out_specs=pl.BlockSpec(memory_space=pltpu.VMEM),
+        scratch_shapes=[
+            pltpu.VMEM((count - 1,) + values.shape, jnp.float32),
+            pltpu.SemaphoreType.DMA((count - 1,)),
+            pltpu.SemaphoreType.DMA((count - 1,)),
+        ],
+        compiler_params=pltpu.CompilerParams(collective_id=collective_id, has_side_effects=True),
+    )(values)
+
+
+def start_gather(count, tokens, gain_row):
+    rows, width = tokens.shape
+    step = rows // CHUNKS
+
+    def epilogue(chunk, total, extra_refs, out_refs):
+        value = extra_refs[0][chunk].astype(jnp.float32)
+        return (rms_scale(value) * extra_refs[1][...]).astype(jnp.bfloat16)
+
+    (full,) = line_exchange(
+        count,
+        CHUNKS,
+        step,
+        width,
+        None,
+        [tokens.reshape(CHUNKS, step, width), gain_row],
+        [],
+        epilogue,
+        True,
+        1,
+    )
+    return full.reshape(count * rows, width)
+
+
+def middle_exchange(count, branch_part, tokens, gain_row):
+    rows, width = tokens.shape
+    step = rows // CHUNKS
+
+    def epilogue(chunk, total, extra_refs, out_refs):
+        value = extra_refs[0][chunk].astype(jnp.float32) + total
+        out_refs[0][chunk] = value
+        return (rms_scale(value) * extra_refs[1][...]).astype(jnp.bfloat16)
+
+    full, middle = line_exchange(
+        count,
+        CHUNKS,
+        step,
+        width,
+        branch_part.reshape(count, CHUNKS, step, width),
+        [tokens.reshape(CHUNKS, step, width), gain_row],
+        [jax.ShapeDtypeStruct((CHUNKS, step, width), jnp.float32)],
+        epilogue,
+        True,
+        2,
+    )
+    return full.reshape(count * rows, width), middle.reshape(rows, width)
+
+
+def norm_back_rows(value, gain_row, grad_out):
+    inverse = lax.rsqrt(jnp.mean(value * value, axis=-1, keepdims=True) + EPSILON)
+    normed = value * inverse
+    scaled = grad_out * gain_row
+    grad_in = inverse * (scaled - normed * jnp.mean(scaled * normed, axis=-1, keepdims=True))
+    return grad_in, jnp.sum(grad_out * normed, axis=0, keepdims=True)
+
+
+def zero_gain(extra_refs, out_refs):
+    out_refs[1][...] = jnp.zeros_like(out_refs[1])
+
+
+def middle_back_exchange(count, grad_part, router_part, middle, cotangent, gain_row):
+    rows, width = middle.shape
+    step = rows // CHUNKS
+
+    def epilogue(chunk, total, extra_refs, out_refs):
+        grad_out = total + extra_refs[0][chunk]
+        grad_in, grad_gain = norm_back_rows(extra_refs[1][chunk], extra_refs[3][...], grad_out)
+        out_refs[1][...] = out_refs[1][...] + grad_gain
+        grad_middle = extra_refs[2][chunk].astype(jnp.float32) + grad_in
+        out_refs[0][chunk] = grad_middle
+        return grad_middle.astype(jnp.bfloat16)
+
+    full, grad_middle, grad_gain = line_exchange(
+        count,
+        CHUNKS,
+        step,
+        width,
+        grad_part.reshape(count, CHUNKS, step, width),
+        [
+            router_part.reshape(CHUNKS, step, width),
+            middle.reshape(CHUNKS, step, width),
+            cotangent.reshape(CHUNKS, step, width),
+            gain_row,
+        ],
+        [
+            jax.ShapeDtypeStruct((CHUNKS, step, width), jnp.float32),
+            jax.ShapeDtypeStruct((1, width), jnp.float32),
+        ],
+        epilogue,
+        True,
+        3,
+        zero_gain,
+    )
+    return full.reshape(count * rows, width), grad_middle.reshape(rows, width), grad_gain[0]
+
+
+def end_exchange(count, grad_part, grad_middle, tokens, gain_row):
+    rows, width = tokens.shape
+    step = rows // CHUNKS
+
+    def epilogue(chunk, total, extra_refs, out_refs):
+        value = extra_refs[1][chunk].astype(jnp.float32)
+        grad_in, grad_gain = norm_back_rows(value, extra_refs[2][...], total)
+        out_refs[1][...] = out_refs[1][...] + grad_gain
+        out_refs[0][chunk] = extra_refs[0][chunk] + grad_in
+
+    grad_source, grad_gain = line_exchange(
+        count,
+        CHUNKS,
+        step,
+        width,
+        grad_part.reshape(count, CHUNKS, step, width),
+        [
+            grad_middle.reshape(CHUNKS, step, width),
+            tokens.reshape(CHUNKS, step, width),
+            gain_row,
+        ],
+        [
+            jax.ShapeDtypeStruct((CHUNKS, step, width), jnp.float32),
+            jax.ShapeDtypeStruct((1, width), jnp.float32),
+        ],
+        epilogue,
+        False,
+        4,
+        zero_gain,
+    )
+    return grad_source.reshape(rows, width), grad_gain[0]
+
+
 def local(
     tokens,
     cotangent,
@@ -184,9 +597,8 @@
     query_scale = lax.dynamic_slice_in_dim(gains[1], col_start, head_cols)
     key_scale = lax.dynamic_slice_in_dim(gains[2], col_start, head_cols)
     ffn_scale = gains[3]
-    source = tokens.astype(jnp.float32)
-    normed_local = (rms_scale(source) * attn_scale).astype(jnp.bfloat16)
-    normed = lax.all_gather(normed_local, "tensor", axis=0, tiled=True)
+    count = lax.axis_size("tensor")
+    normed = start_gather(count, tokens, attn_scale[None, :])
     seq_len = normed.shape[0]
     block_row = block_ids[0]
     cosine_table, sine_table = rope_tables(seq_len, HEAD_DIM)
@@ -194,9 +606,10 @@
     query_proj = projected[:, :head_cols]
     key_proj = projected[:, head_cols : 2 * head_cols]
     value_low = projected[:, 2 * head_cols :].astype(jnp.bfloat16)
-    query_sq, key_sq = lax.psum(
-        (jnp.sum(query_proj * query_proj, axis=1), jnp.sum(key_proj * key_proj, axis=1)), "tensor"
-    )
+    squares = jnp.stack(
+        [jnp.sum(query_proj * query_proj, axis=1), jnp.sum(key_proj * key_proj, axis=1)]
+    )
+    query_sq, key_sq = small_sum(count, squares, 5)
     query_inv = lax.rsqrt(query_sq / model_width + EPSILON)[:, None]
     key_inv = lax.rsqrt(key_sq / model_width + EPSILON)[:, None]
     query_normed = query_proj * query_inv
@@ -212,17 +625,10 @@
     value_heads = value_low.reshape(seq_len, heads_here, HEAD_DIM)
     mixed, log_totals = attend(q_rot, k_rot, value_heads, block_row)
     mixed_low = mixed.astype(jnp.bfloat16)
-    attn_branch = lax.psum_scatter(
-        jnp.einsum("sf,df->sd", mixed_low, w_o_t, preferred_element_type=jnp.float32).astype(
-            jnp.bfloat16
-        ),
-        "tensor",
-        scatter_dimension=0,
-        tiled=True,
-    ).astype(jnp.float32)
-    middle = source + attn_branch
-    normed_two_local = (rms_scale(middle) * ffn_scale).astype(jnp.bfloat16)
-    normed_two = lax.all_gather(normed_two_local, "tensor", axis=0, tiled=True)
+    branch_part = jnp.einsum(
+        "sf,df->sd", mixed_low, w_o_t, preferred_element_type=jnp.float32
+    ).astype(jnp.bfloat16)
+    normed_two, middle = middle_exchange(count, branch_part, tokens, ffn_scale[None, :])
     grad_rows = lax.all_gather(cotangent, "tensor", axis=0, tiled=True)
     logits = jnp.dot(normed_two, full_router, preferred_element_type=jnp.float32)
     router_probs = jax.nn.softmax(logits, axis=-1)
@@ -263,7 +669,7 @@
         combined, "tensor", scatter_dimension=0, tiled=True
     ).astype(jnp.float32)
     output = (middle + ffn_branch).astype(jnp.bfloat16)
-    grad_probs = lax.psum(gate_dot * kept, "tensor")
+    grad_probs = small_sum(count, (gate_dot * kept).T, 6).T
     grad_logits = router_probs * (
         grad_probs - jnp.sum(router_probs * grad_probs, axis=1, keepdims=True)
     )
@@ -272,14 +678,12 @@
         "sd,se->de", normed_two, logits_low, preferred_element_type=jnp.float32
     )
     own_logits = lax.dynamic_slice_in_dim(logits_low, tensor_rank * local_rows, local_rows)
-    grad_two = lax.psum_scatter(
-        grad_two_part, "tensor", scatter_dimension=0, tiled=True
-    ).astype(jnp.float32) + jnp.einsum(
+    router_part = jnp.einsum(
         "se,de->sd", own_logits, full_router, preferred_element_type=jnp.float32
     )
-    grad_middle_norm, grad_ffn_gain = norm_back(middle, ffn_scale, grad_two)
-    grad_middle = cotangent.astype(jnp.float32) + grad_middle_norm
-    grad_attn_rows = lax.all_gather(grad_middle.astype(jnp.bfloat16), "tensor", axis=0, tiled=True)
+    grad_attn_rows, grad_middle, grad_ffn_gain = middle_back_exchange(
+        count, grad_two_part, router_part, middle, cotangent, ffn_scale[None, :]
+    )
     grad_out_w = jnp.einsum(
         "sf,sd->df", mixed_low, grad_attn_rows, preferred_element_type=jnp.float32
     ).astype(jnp.bfloat16)
@@ -302,10 +706,10 @@
     grad_key_gain = jnp.sum(grad_key_normed * key_normed, axis=0)
     query_scaled = grad_query_normed * query_scale
     key_scaled = grad_key_normed * key_scale
-    query_dot, key_dot = lax.psum(
-        (jnp.sum(query_scaled * query_normed, axis=1), jnp.sum(key_scaled * key_normed, axis=1)),
-        "tensor",
-    )
+    dots = jnp.stack(
+        [jnp.sum(query_scaled * query_normed, axis=1), jnp.sum(key_scaled * key_normed, axis=1)]
+    )
+    query_dot, key_dot = small_sum(count, dots, 7)
     grad_query_proj = (
         query_inv * (query_scaled - query_normed * (query_dot / model_width)[:, None])
     ).astype(jnp.bfloat16)
@@ -320,19 +724,20 @@
     grad_normed_part = jnp.einsum(
         "sf,df->sd", grad_qkv, w_qkv, preferred_element_type=jnp.float32
     ).astype(jnp.bfloat16)
-    grad_normed = lax.psum_scatter(
-        grad_normed_part, "tensor", scatter_dimension=0, tiled=True
-    ).astype(jnp.float32)
-    grad_source_norm, grad_attn_gain = norm_back(source, attn_scale, grad_normed)
-    grad_source = grad_middle + grad_source_norm
+    grad_source, grad_attn_gain = end_exchange(
+        count, grad_normed_part, grad_middle, tokens, attn_scale[None, :]
+    )
     zero_cols = jnp.zeros((model_width,), jnp.float32)
     query_gain_full = lax.dynamic_update_slice_in_dim(zero_cols, grad_query_gain, col_start, 0)
     key_gain_full = lax.dynamic_update_slice_in_dim(zero_cols, grad_key_gain, col_start, 0)
-    gain_sums = lax.psum_scatter(
-        jnp.stack([grad_attn_gain, query_gain_full, key_gain_full, grad_ffn_gain], axis=1),
+    gain_rows = lax.psum(
+        jnp.stack([grad_attn_gain, query_gain_full, key_gain_full, grad_ffn_gain]),
         ("dp", "tensor"),
-        scatter_dimension=0,
-        tiled=True,
+    )
+    dp_rank = lax.axis_index("dp")
+    gain_width = model_width // (lax.axis_size("dp") * count)
+    gain_sums = lax.dynamic_slice_in_dim(
+        gain_rows, (dp_rank * count + tensor_rank) * gain_width, gain_width, 1
     )
     sum_gate = lax.psum_scatter(grad_gate_w, "dp", scatter_dimension=0, tiled=True)
     sum_up = lax.psum_scatter(grad_up_w, "dp", scatter_dimension=0, tiled=True)
@@ -341,21 +746,24 @@
     sum_qkv = lax.psum_scatter(grad_qkv_w, "dp", scatter_dimension=0, tiled=True).astype(
         jnp.float32
     )
-    sum_router = lax.psum_scatter(grad_router, "dp", scatter_dimension=0, tiled=True)
+    router_rows = lax.psum(grad_router.T, "dp")
+    sum_router = lax.dynamic_slice_in_dim(
+        router_rows, dp_rank * shard_width, shard_width, 1
+    ).T
     grad_gate = sum_gate.reshape(shard_width, EXPERTS, ff_here).transpose(1, 0, 2)
     grad_up = sum_up.reshape(shard_width, EXPERTS, ff_here).transpose(1, 0, 2)
     grad_down = sum_down.reshape(shard_width, EXPERTS, ff_here).transpose(1, 2, 0)
     return (
         output,
         grad_source,
-        gain_sums[:, 0],
-        gain_sums[:, 1],
-        gain_sums[:, 2],
+        gain_sums[0],
+        gain_sums[1],
+        gain_sums[2],
         sum_qkv[:, :head_cols],
         sum_qkv[:, head_cols : 2 * head_cols],
         sum_qkv[:, 2 * head_cols :],
         sum_out.T.astype(jnp.float32),
-        gain_sums[:, 3],
+        gain_sums[3],
         sum_router,
         grad_gate.astype(jnp.float32),
         grad_up.astype(jnp.float32),

time: 1700 us -> 1170 us (0.69)
  waiting for transfers between devices: 1200 us -> 90.7 us
  Pallas kernels: 0 us -> 594 us
  other arithmetic: 103 us -> 73.9 us
    pallas_call x0 -> x7, Pallas kernels: none -> 594 us  [the longest x4 572 us: line_exchange(): pl.pallas_call(kernel, out_shape=tuple(shapes), in_specs=[pl.BlockSpec(me...]
    all_gather x3 -> x0, waiting for transfers between devices: 231 us -> none  [the longest x1 82.8 us: local(): normed_two = lax.all_gather(normed_two_local, 'tensor', axis=0, tiled=True)]
    reduce_scatter x4 -> x0, waiting for transfers between devices: 192 us -> none  [the longest x1 74.2 us: local(): lax.psum_scatter(grad_two_part, 'tensor', scatter_dimension=0, tiled=True)]
    unnamed x21 -> x13, waiting for transfers between devices: 136 us -> 1.92 us
    reduce_scatter x1, waiting for transfers between devices: 75.1 us -> 0.01 us  [local(): lax.psum_scatter(combined, 'tensor', scatter_dimension=0, tiled=True)]
    reduce_scatter x1, waiting for transfers between devices: 71.9 us -> 0.01 us  [local(): lax.psum_scatter(grad_gate_w, 'dp', scatter_dimension=0, tiled=True)]
    all_gather x1, waiting for transfers between devices: 67.7 us -> 0.01 us  [local(): grad_rows = lax.all_gather(cotangent, 'tensor', axis=0, tiled=True)]
    reduce_scatter x1, waiting for transfers between devices: 58.6 us -> 0.01 us  [local(): lax.psum_scatter(grad_qkv_w, 'dp', scatter_dimension=0, tiled=True)]
  transfers between devices with their start and end apart: 20 -> 13, of which waited for: 19 -> 2; matrix products, arithmetic and copies ran while one was open for 13% -> 28% of each run, Pallas kernels for 0% -> 51%
where the time goes in v2:
time: 1170 us; the launch traced here: 1160 us
  Pallas kernels  594 us (51%)
  matrix products  233 us (20%)
  local copies, waits for them, and re-layouts  91.5 us (8%)
  waiting for transfers between devices  90.7 us (8%)
  other arithmetic  73.9 us (6%)
  blocking collectives  60.7 us (5%)
  between operations  15 us (1%)
    pallas_call x4, Pallas kernels, line_exchange(): pl.pallas_call(kernel, out_shape=tuple(shapes), in_specs=[pl.BlockSpec(me...  572 us
    reduce_scatter x1, waiting for transfers between devices, local(): lax.psum_scatter(grad_down_w, 'dp', scatter_dimension=0, tiled=True)  71.8 us
    psum x1, blocking collectives, local(): lax.psum(jnp.stack([grad_attn_gain, query_gain_full, key_gain_full, grad_...  49.6 us
    unnamed x114, local copies, waits for them, and re-layouts  39.5 us
    dot_general x1, matrix products, local(): jnp.dot(grad_rows, full_down, preferred_element_type=jnp.float32)  26.4 us
  transfers between devices with their start and end apart: 13, of which 2 were waited for; matrix products, arithmetic and copies ran while one was open for 28% of the time, Pallas kernels for 51%

profile of v2, /device:TPU:0, one launch (start us, length us, event | category | flops | bytes accessed | tf_op | source)
XLA Modules:
  0.0 1159.7 jit_solution(18304810069696116441)
XLA Ops:
  16.6 11.0 all_gather.21
  30.2 4.0 multiply_cosine_fusion
  37.1 78.4 %shard_map.263 = bf16[4,8,32,2048]{3,2,1,0:T(8,128)(2,1)} custom-call(bf16[8,32,2048]{2,1,0:T(8,128)(2,1)} %bitcast.296, f32[1,2048]{1,0:T(1,128)} %get-tuple-element.347.refs_1_.refs_3_), custom_call_target="tpu_custom_call" | custom-call | bytes 188743680 | tf_op jit(solution)/shard_map/pallas_call | solution.py:364
  118.1 10.5 fusion.69
  128.7 2.7 copy-done.8
  132.3 6.8 shard_map.264
  139.9 3.9 multiply_bitcast_fusion
  147.4 2.8 slice.169
  150.1 2.9 slice_negate_fusion.3
  153.0 3.1 concatenate.44
  158.0 2.3 copy.80
  160.3 4.1 fusion.34
  164.4 2.5 copy.86
  168.4 2.4 copy.152
  173.4 16.7 %while.27 = (s32[]{:T(128)}, bf16[2,512,512]{2,1,0:T(8,128)(2,1)}, f32[2,4,512]{2,1,0:T(4,128)S(1)}, s32[1,1024]{1,0:T(1,128)S(1)}, s32[2,512]{1,0:T(2,128)S(1)}...) while((s32[]{:T(128)}, bf16[2,512,512]{2,1,0:T(8,128)(2,1)}, ...), condition=%wide.region_5.6_spmd, body=%wide.region_2.5_spmd.sunk | while | flops 1097332736 | bytes 36776080 | solution.py:85
  175.7 2.5 exponential_reduce_fusion.2
  178.2 2.6 fusion.131
  184.0 2.5 exponential_reduce_fusion.2
  186.5 2.6 fusion.131
  190.1 7.1 convolution_convert_fusion.5
  197.2 227.1 %shard_map.265 = (bf16[4,8,32,2048]{3,2,1,0:T(8,128)(2,1)}, f32[8,32,2048]{2,1,0:T(8,128)}) custom-call(bf16[4,8,32,2048]{3,2,1,0:T(8,128)(2,1)} %bitcast.309, bf16[8,32,2048]{2,1,0:T(8,128)(2,1)} %bitcast.297, f32[1,2048]{1,0:T(1,128)} %get-tuple-element.344.refs_2_.refs_4_), custom_call_target="tpu_custom_call" | custom-call | bytes 251658240 | tf_op jit(solution)/shard_map/pallas_call | solution.py:364
  424.4 3.4 fusion.68
  429.3 7.4 copy.131
  436.6 14.5 %fusion.71 = f32[1024,2048]{1,0:T(8,128)} fusion(bf16[1024,2048]{1,0:T(8,128)(2,1)} %bitcast.289, bf16[2048,2048]{0,1:T(8,128)(2,1)} %all-gather.13.cloned.1.call-done), kind=kOutput, calls=%fused_computation.180 | convolution fusion | flops 8589934592 | bytes 20971520 | tf_op jit(solution)/shard_map/dot_general | solution.py:640
  451.2 15.0 %fusion.70 = f32[1024,2048]{1,0:T(8,128)} fusion(bf16[1024,2048]{1,0:T(8,128)(2,1)} %bitcast.290, bf16[2048,2048]{0,1:T(8,128)(2,1)} %all-gather.11.cloned.1.call-done), kind=kOutput, calls=%fused_computation.179 | convolution fusion | flops 8589934592 | bytes 20971520 | tf_op jit(solution)/shard_map/dot_general | solution.py:639
  466.2 26.4 %multiply_multiply_fusion = (f32[1024,2048]{1,0:T(8,128)}, bf16[1024,2048]{1,0:T(8,128)(2,1)}, bf16[1024,2048]{1,0:T(8,128)(2,1)}, bf16[1024,2048]{1,0:T(8,128)(2,1)}) fusion(f32[1024,2048]{1,0:T(8,128)} %fusion.71, f32[1024,2048]{1,0:T(8,128)} %fusion.70, f32[1024,2048]{1,0:T(8,128)} %bitcast.299, bf16[1024,2048]{1,0:T(8,128)(2,1)} %all-gather.17.cloned.1.call-done, ...), kind=kOutput, calls=%fused_computation.59 | convolution fusion | flops 8627683328 | bytes 58720256 | tf_op jit(solution)/shard_map/dot_general | solution.py:648
  492.6 10.8 copy.132
  503.3 4.6 reduce_sum.104
  508.7 7.7 shard_map.266
  518.0 3.5 fusion.73
  523.3 12.8 %fusion.72 = f32[1024,2048]{1,0:T(8,128)S(1)} fusion(bf16[1024,2048]{1,0:T(8,128)(2,1)} %get-tuple-element.324, bf16[2048,2048]{0,1:T(8,128)(2,1)} %all-gather.11.cloned.1.call-done), kind=kOutput, calls=%fused_computation.181 | convolution fusion | flops 8589934592 | bytes 20971520 | tf_op jit(solution)/shard_map/sk,dk->sd/dot_general | solution.py:656
  536.1 12.6 %add_convert_fusion = bf16[1024,2048]{1,0:T(8,128)(2,1)} fusion(f32[1024,2048]{1,0:T(8,128)S(1)} %fusion.72, bf16[1024,2048]{1,0:T(8,128)(2,1)S(1)} %copy-done.64, bf16[2048,2048]{0,1:T(8,128)(2,1)} %all-gather.13.cloned.1.call-done), kind=kOutput, calls=%fused_computation.47 | convolution fusion | flops 8594128896 | bytes 25165824 | tf_op jit(solution)/shard_map/sk,dk->sd/dot_general | solution.py:657
  548.8 173.0 %shard_map.267 = (bf16[4,8,32,2048]{3,2,1,0:T(8,128)(2,1)}, f32[8,32,2048]{2,1,0:T(8,128)}, f32[1,2048]{1,0:T(1,128)}) custom-call(bf16[4,8,32,2048]{3,2,1,0:T(8,128)(2,1)} %bitcast.314, f32[8,32,2048]{2,1,0:T(8,128)} %bitcast.304, f32[8,32,2048]{2,1,0:T(8,128)} %get-tuple-element.124.refs_2_, bf16[8,32,2048]{2,1,0:T(8,128)(2,1)} %bitcast.315, ...), custom_call_target="tpu_custom_call" | custom-call | bytes 251658240 | tf_op jit(solution)/shard_map/pallas_call | solution.py:364
  721.8 5.9 convolution_convert_fusion.6
  727.8 2.7 copy_bitcast_fusion.4
  730.5 5.2 convolution_convert_fusion.7
  737.1 13.9 %convolution_convert_fusion.4 = bf16[1024,2048]{1,0:T(8,128)(2,1)} fusion(bf16[1024,2048]{1,0:T(8,128)(2,1)} %get-tuple-element.325, bf16[2048,2048]{0,1:T(8,128)(2,1)} %all-gather.15.cloned.1.call-done), kind=kOutput, calls=%fused_computation.57 | convolution fusion | flops 8592031744 | bytes 16777216 | tf_op jit(solution)/shard_map/sk,dk->sd/dot_general | solution.py:645
  752.2 44.0 %while.28 = (s32[]{:T(128)}, f32[1024,4,128]{0,2,1:T(8,128)S(1)}, f32[1024,4,128]{0,2,1:T(8,128)}, f32[2,512,4,128]{3,1,2,0:T(8,128)}, bf16[2,512,4,128]{3,1,2,0...) while((s32[]{:T(128)}, f32[1024,4,128]{0,2,1:T(8,128)S(1)}, ...), condition=%wide.region_15.16_spmd.clone, body=%wide.region_13.15_spmd.clone.sunk | while | flops 2719217664 | bytes 215026224 | solution.py:129
  752.2 2.4 fusion.140
  755.3 3.5 multiply_reduce_fusion.7
  758.8 3.7 multiply_convert_fusion.7
  762.5 3.8 bitcast_add_fusion.5
  768.4 2.7 bitcast_add_fusion.6
  773.9 2.4 fusion.140
  777.0 3.5 multiply_reduce_fusion.7
  780.5 3.7 multiply_convert_fusion.7
  784.2 3.8 bitcast_add_fusion.5
  790.7 2.7 bitcast_add_fusion.6
  796.2 4.4 copy.96
  807.6 2.5 bitcast_multiply_fusion.3
  816.1 3.9 multiply_reduce_fusion.1
  820.5 8.2 shard_map.268
  829.5 5.0 multiply_convert_fusion.5
  835.9 9.5 convolution_convert_fusion.2
  845.4 14.4 %convolution_convert_fusion.1 = bf16[2048,2048]{1,0:T(8,128)(2,1)} fusion(bf16[1024,2048]{1,0:T(8,128)(2,1)} %bitcast.292, bf16[1024,2048]{1,0:T(8,128)(2,1)} %get-tuple-element.324), kind=kOutput, calls=%fused_computation.54 | convolution fusion | flops 8594128896 | bytes 16777216 | tf_op jit(solution)/shard_map/sd,sk->dk/dot_general | solution.py:659
  859.9 14.1 %convolution_convert_fusion = bf16[2048,2048]{1,0:T(8,128)(2,1)} fusion(bf16[1024,2048]{1,0:T(8,128)(2,1)} %bitcast.293, bf16[1024,2048]{1,0:T(8,128)(2,1)} %get-tuple-element.326), kind=kOutput, calls=%fused_computation.53 | convolution fusion | flops 8594128896 | bytes 16777216 | tf_op jit(solution)/shard_map/sd,sk->dk/dot_general | solution.py:662
  874.1 14.9 %convert_bitcast_fusion = bf16[2048,2048]{0,1:T(8,128)(2,1)} fusion(bf16[1024,2048]{1,0:T(8,128)(2,1)} %get-tuple-element.325, bf16[1024,2048]{1,0:T(8,128)(2,1)} %all-gather.17.cloned.1.call-done), kind=kOutput, calls=%fused_computation.46 | convolution fusion | flops 8594128896 | bytes 16777216 | tf_op jit(solution)/shard_map/sd,sk->dk/dot_general | solution.py:665
  890.9 11.0 convolution_convert_fusion.3
  901.9 93.0 %shard_map.269 = (f32[8,32,2048]{2,1,0:T(8,128)}, f32[1,2048]{1,0:T(1,128)}) custom-call(bf16[4,8,32,2048]{3,2,1,0:T(8,128)(2,1)} %bitcast.311, f32[8,32,2048]{2,1,0:T(8,128)} %get-tuple-element.131.refs_1_, bf16[8,32,2048]{2,1,0:T(8,128)(2,1)} %bitcast.298, f32[1,2048]{1,0:T(1,128)} %get-tuple-element.347.refs_1_.refs_3_), custom_call_target="tpu_custom_call" | custom-call | bytes 188743680 | tf_op jit(solution)/shard_map/pallas_call | solution.py:364
  995.7 49.6 %psum.14 = f32[4,2048]{1,0:T(4,128)S(1)} all-reduce(f32[4,2048]{1,0:T(4,128)S(1)} %pad_maximum_fusion.8), channel_id=1, replica_groups=mesh['dp'=8,'tensor'=4] {'dp','tensor'}, use_global_device_ids=true, to_apply=%region_20.21 | all-reduce | flops 8192 | bytes 65536 | tf_op jit(solution)/shard_map/psum | solution.py:733
  1049.3 2.6 fusion.38
  1057.2 16.9 %reduce-scatter.15.cloned.1.call-done = bf16[256,2048]{1,0:T(8,128)(2,1)} async-done(((bf16[2048,2048]{1,0:T(8,128)(2,1)}), bf16[256,2048]{1,0:T(8,128)(2,1)}) %reduce-scatter.15.cloned.1.call-update) | async-done | bytes 1048592 | tf_op jit(solution)/shard_map/reduce_scatter | solution.py:743
  1077.0 71.8 %reduce-scatter.17.cloned.1.call-done = bf16[256,2048]{0,1:T(8,128)(2,1)} async-done(((bf16[2048,2048]{0,1:T(8,128)(2,1)}), bf16[256,2048]{0,1:T(8,128)(2,1)}) %reduce-scatter.17.cloned.1.call-update) | async-done | bytes 1048592 | tf_op jit(solution)/shard_map/reduce_scatter | solution.py:744
  1148.9 2.7 convert_bitcast_fusion.1
  (295 shorter events, 86.1 us)
Async XLA Ops:
  7.2 5.4 copy-start.38
  7.2 110.9 %all-gather.7.cloned.1.call-start = ((), (), s32[]{:S(2)}) async-start(), calls=%async_computation.6 | async-start | bytes 7077888 | tf_op jit(solution)/shard_map/all_gather | solution.py:579
  9.4 180.7 %all-gather.9.cloned.1.call-start = ((), (), s32[]{:S(2)}) async-start(), calls=%async_computation.7 | async-start | bytes 2359296 | tf_op jit(solution)/shard_map/all_gather | solution.py:582
  10.1 5.6 copy-start.42
  10.1 6.3 copy-start.60
  10.2 6.3 copy-start.61
  10.2 6.3 copy-start.62
  10.2 6.3 copy-start.63
  10.2 6.3 copy-start.58
  10.2 426.4 %all-gather.13.cloned.1.call-start = ((), (), s32[]{:S(2)}) async-start(), calls=%async_computation.9 | async-start | bytes 9437184 | tf_op jit(solution)/shard_map/all_gather | solution.py:587
  12.5 21.7 %copy-start.56 = (s32[1024,2]{0,1:T(2,128)S(1)}, s32[1024,2]{0,1:T(2,128)}, u32[]{:S(2)}) copy-start(s32[1024,2]{0,1:T(2,128)} %param.22) | copy-start | bytes 24580
  12.5 438.6 %all-gather.11.cloned.1.call-start = ((), (), s32[]{:S(2)}) async-start(), calls=%async_computation.8 | async-start | bytes 9437184 | tf_op jit(solution)/shard_map/all_gather | solution.py:586
  13.9 452.3 %all-gather.17.cloned.1.call-start = ((), (), s32[]{:S(2)}) async-start(), calls=%async_computation.12 | async-start | bytes 5242880 | tf_op jit(solution)/shard_map/all_gather | solution.py:632
  14.5 451.7 %all-gather.15.cloned.1.call-start = ((), (), s32[]{:S(2)}) async-start(), calls=%async_computation.10 | async-start | bytes 9437184 | tf_op jit(solution)/shard_map/all_gather | solution.py:588
  15.1 1030.9 %all-reduce.2.cloned.1.call-start = ((), (), s32[]{:S(2)}) async-start(), calls=%async_computation.15 | async-start | bytes 131072 | tf_op jit(solution)/shard_map/psum | solution.py:749
  118.1 21.8 %copy-start.52 = (f32[1,512]{1,0:T(1,128)}, f32[1,512]{1,0:T(1,128)S(1)}, u32[]{:S(2)}) copy-start(f32[1,512]{1,0:T(1,128)S(1)} %get-tuple-element.364) | copy-start | bytes 6148
  118.1 21.8 %copy-start.54 = (f32[1,512]{1,0:T(1,128)}, f32[1,512]{1,0:T(1,128)S(1)}, u32[]{:S(2)}) copy-start(f32[1,512]{1,0:T(1,128)S(1)} %get-tuple-element.365) | copy-start | bytes 6148
  139.9 4.0 copy-start.48
  139.9 4.0 copy-start.50
  150.1 7.8 copy-start.24
  160.3 6.7 copy-start.13
  190.1 7.1 copy-start.3
  190.1 7.1 copy-start.7
  190.1 7.1 copy-start.44
  190.1 7.1 copy-start.46
  523.3 524.0 %reduce-scatter.11.cloned.1.call-start = ((), (), s32[]{:S(2)}) async-start(), calls=%async_computation.14 | async-start | bytes 2359296 | tf_op jit(solution)/shard_map/reduce_scatter | solution.py:745
  523.3 12.8 %copy-start.64 = (bf16[1024,2048]{1,0:T(8,128)(2,1)S(1)}, bf16[1024,2048]{1,0:T(8,128)(2,1)}, u32[]{:S(2)}) copy-start(bf16[1024,2048]{1,0:T(8,128)(2,1)} %get-tuple-element.326) | copy-start | bytes 12582916
  548.7 173.0 %copy-start.59 = (bf16[2,512,512]{2,1,0:T(8,128)(2,1)S(1)}, bf16[2,512,512]{2,1,0:T(8,128)(2,1)}, u32[]{:S(2)}) copy-start(bf16[2,512,512]{2,1,0:T(8,128)(2,1)} %get-tuple-element.123) | copy-start | bytes 3145732
  727.8 321.5 %reduce-scatter.7.cloned.1.call-start = ((), (), s32[]{:S(2)}) async-start(), calls=%async_computation.11 | async-start | bytes 5242880 | tf_op jit(solution)/shard_map/reduce_scatter | solution.py:668
  751.0 300.9 %reduce-scatter.9.cloned.1.call-start = ((), (), s32[]{:S(2)}) async-start(), calls=%async_computation.13 | async-start | bytes 7077888 | tf_op jit(solution)/shard_map/reduce_scatter | solution.py:746
  752.2 3.1 copy-start.11
  754.7 4.1 copy-start
  755.1 3.7 copy-start.5
  755.3 3.5 copy-start.9
  762.5 5.0 copy-start.1
  762.5 5.0 copy-start.6
  762.5 5.2 copy-start.10
  762.5 5.9 copy-start.30
  776.3 4.2 copy-start
  776.8 3.7 copy-start.5
  777.0 3.5 copy-start.9
  784.2 5.6 copy-start.1
  784.2 5.6 copy-start.6
  784.2 5.8 copy-start.10
  784.2 6.5 copy-start.30
  796.2 4.4 copy-start.23
  796.2 5.9 copy-start.32
  802.0 5.6 copy-start.28
  810.9 4.3 copy-start.12
  810.9 5.1 copy-start.26
  810.9 5.1 copy-start.49
  810.9 5.1 copy-start.51
  810.9 5.1 copy-start.53
  810.9 5.1 copy-start.55
  812.3 7.7 copy-start.16
  812.3 7.7 copy-start.17
  829.5 6.4 copy-start.29
  829.5 6.4 copy-start.39
  845.4 208.9 %reduce-scatter.13.cloned.1.call-start = ((), (), s32[]{:S(2)}) async-start(), calls=%async_computation.16 | async-start | bytes 9437184 | tf_op jit(solution)/shard_map/reduce_scatter | solution.py:742
  859.9 214.2 %reduce-scatter.15.cloned.1.call-start = ((), (), s32[]{:S(2)}) async-start(), calls=%async_computation.17 | async-start | bytes 9437184 | tf_op jit(solution)/shard_map/reduce_scatter | solution.py:743
  874.1 274.8 %reduce-scatter.17.cloned.1.call-start = ((), (), s32[]{:S(2)}) async-start(), calls=%async_computation.18 | async-start | bytes 9437184 | tf_op jit(solution)/shard_map/reduce_scatter | solution.py:744
  901.9 93.1 %copy-start.57 = (f32[1,2048]{1,0:T(1,128)S(1)}, f32[1,2048]{1,0:T(1,128)}, u32[]{:S(2)}) copy-start(f32[1,2048]{1,0:T(1,128)} %get-tuple-element.134) | copy-start | bytes 24580
  901.9 147.4 %copy-start.25 = (f32[8,32,2048]{2,1,0:T(8,128)S(1)}, f32[8,32,2048]{2,1,0:T(8,128)}, u32[]{:S(2)}) copy-start(f32[8,32,2048]{2,1,0:T(8,128)} %get-tuple-element.124.refs_2_) | copy-start | bytes 6291460
  1075.5 76.1 %copy-start.33 = (f32[8,32,2048]{2,1,0:T(8,128)S(1)}, f32[8,32,2048]{2,1,0:T(8,128)}, u32[]{:S(2)}) copy-start(f32[8,32,2048]{2,1,0:T(8,128)} %get-tuple-element.132) | copy-start | bytes 6291460
  (30 other events, 58.8 us)
Sparse Core Ops, SparseCore 0:
  10.5 48.2 all-gather.6
  60.6 28.1 all-gather.8
  90.6 55.8 all-gather.12
  148.2 55.8 all-gather.10
  205.6 103.4 all-gather.16
  310.7 53.8 all-gather.14
  523.4 57.3 all-reduce.1
  727.9 50.5 reduce-scatter.10
  780.8 77.0 reduce-scatter.6
  861.1 62.3 reduce-scatter.8
  927.0 71.4 reduce-scatter.12
  1001.9 72.1 reduce-scatter.14
  1077.5 71.2 reduce-scatter.16

commit v3 on v2

--- a/solution.py
+++ b/solution.py
@@ -17,7 +17,7 @@
 EPSILON = 1e-05
 MASKED = -1e30
 MESH = pl.DeviceIdType.MESH
-CHUNKS = 8
+CHUNK_ROWS = 16
 
 
 def rms_scale(source):
@@ -164,8 +164,8 @@
     n_extra = len(extras)
     n_out = len(out_shapes)
     last = count - 1
-    back_lag = 2 if reduce else 0
-    pass_lag = (back_lag + 1) if reduce else chunks
+    back_lag = last if reduce else 0
+    pass_lag = back_lag if reduce else chunks
 
     def kernel(*refs):
         refs = list(refs)
@@ -225,7 +225,7 @@
         if prologue is not None:
             prologue(extra_refs, out_refs)
 
-        def send_sums(chunk):
+        def send_right(chunk):
             for step in range(last):
                 far = last - step
 
@@ -239,6 +239,9 @@
                     sum_right[far, chunk] = sum_right[far, chunk] + part_ref[far, chunk]
                     rs_right(far, chunk).start()
 
+        def send_left(chunk):
+            for step in range(last):
+
                 @pl.when(jnp.logical_and(me > step, me == last))
                 def _():
                     rs_left(step, chunk, part_ref.at[step, chunk]).start()
@@ -277,45 +280,39 @@
                 def _():
                     ag_left(me, chunk).start()
 
-        def forward(chunk):
-            for step in range(1, count):
-
-                @pl.when(me - step >= 0)
-                def _():
-                    ag_right(jnp.maximum(me - step, 0), chunk).wait_recv()
-
-                @pl.when(jnp.logical_and(me - step >= 0, me < last))
-                def _():
-                    ag_right(jnp.maximum(me - step, 0), chunk).start()
-
-                @pl.when(me + step <= last)
-                def _():
-                    ag_left(jnp.minimum(me + step, last), chunk).wait_recv()
-
-                @pl.when(jnp.logical_and(me + step <= last, me > 0))
-                def _():
-                    ag_left(jnp.minimum(me + step, last), chunk).start()
+        def forward(chunk, step):
+            @pl.when(me - step >= 0)
+            def _():
+                ag_right(jnp.maximum(me - step, 0), chunk).wait_recv()
+
+            @pl.when(jnp.logical_and(me - step >= 0, me < last))
+            def _():
+                ag_right(jnp.maximum(me - step, 0), chunk).start()
+
+            @pl.when(me + step <= last)
+            def _():
+                ag_left(jnp.minimum(me + step, last), chunk).wait_recv()
+
+            @pl.when(jnp.logical_and(me + step <= last, me > 0))
+            def _():
+                ag_left(jnp.minimum(me + step, last), chunk).start()
+
+        def at_chunk(chunk, work):
+            @pl.when(jnp.logical_and(chunk >= 0, chunk < chunks))
+            def _():
+                work(jnp.clip(chunk, 0, chunks - 1))
 
         def tick(time, carry):
             if reduce:
-
-                @pl.when(time < chunks)
-                def _():
-                    send_sums(time)
-
-            @pl.when(jnp.logical_and(time >= back_lag, time < back_lag + chunks))
-            def _():
-                finish(time - back_lag)
-
+                at_chunk(time - me, send_right)
+                at_chunk(time - (last - me), send_left)
+            at_chunk(time - back_lag, finish)
             if gather:
-
-                @pl.when(time >= pass_lag)
-                def _():
-                    forward(time - pass_lag)
-
+                for step in range(1, count):
+                    at_chunk(time - pass_lag - step, lambda chunk: forward(chunk, step))
             return carry
 
-        ticks = chunks + (pass_lag if gather else back_lag)
+        ticks = chunks + (pass_lag + last if gather else back_lag)
         lax.fori_loop(0, ticks, tick, 0)
 
         def drain(chunk, carry):
@@ -424,7 +421,7 @@
 
 def start_gather(count, tokens, gain_row):
     rows, width = tokens.shape
-    step = rows // CHUNKS
+    step, chunks = CHUNK_ROWS, rows // CHUNK_ROWS
 
     def epilogue(chunk, total, extra_refs, out_refs):
         value = extra_refs[0][chunk].astype(jnp.float32)
@@ -432,11 +429,11 @@
 
     (full,) = line_exchange(
         count,
-        CHUNKS,
+        chunks,
         step,
         width,
         None,
-        [tokens.reshape(CHUNKS, step, width), gain_row],
+        [tokens.reshape(chunks, step, width), gain_row],
         [],
         epilogue,
         True,
@@ -447,7 +444,7 @@
 
 def middle_exchange(count, branch_part, tokens, gain_row):
     rows, width = tokens.shape
-    step = rows // CHUNKS
+    step, chunks = CHUNK_ROWS, rows // CHUNK_ROWS
 
     def epilogue(chunk, total, extra_refs, out_refs):
         value = extra_refs[0][chunk].astype(jnp.float32) + total
@@ -456,12 +453,12 @@
 
     full, middle = line_exchange(
         count,
-        CHUNKS,
+        chunks,
         step,
         width,
-        branch_part.reshape(count, CHUNKS, step, width),
-        [tokens.reshape(CHUNKS, step, width), gain_row],
-        [jax.ShapeDtypeStruct((CHUNKS, step, width), jnp.float32)],
+        branch_part.reshape(count, chunks, step, width),
+        [tokens.reshape(chunks, step, width), gain_row],
+        [jax.ShapeDtypeStruct((chunks, step, width), jnp.float32)],
         epilogue,
         True,
         2,
@@ -483,7 +480,7 @@
 
 def middle_back_exchange(count, grad_part, router_part, middle, cotangent, gain_row):
     rows, width = middle.shape
-    step = rows // CHUNKS
+    step, chunks = CHUNK_ROWS, rows // CHUNK_ROWS
 
     def epilogue(chunk, total, extra_refs, out_refs):
         grad_out = total + extra_refs[0][chunk]
@@ -495,18 +492,18 @@
 
     full, grad_middle, grad_gain = line_exchange(
         count,
-        CHUNKS,
+        chunks,
         step,
         width,
-        grad_part.reshape(count, CHUNKS, step, width),
+        grad_part.reshape(count, chunks, step, width),
         [
-            router_part.reshape(CHUNKS, step, width),
-            middle.reshape(CHUNKS, step, width),
-            cotangent.reshape(CHUNKS, step, width),
+            router_part.reshape(chunks, step, width),
+            middle.reshape(chunks, step, width),
+            cotangent.reshape(chunks, step, width),
             gain_row,
         ],
         [
-            jax.ShapeDtypeStruct((CHUNKS, step, width), jnp.float32),
+            jax.ShapeDtypeStruct((chunks, step, width), jnp.float32),
             jax.ShapeDtypeStruct((1, width), jnp.float32),
         ],
         epilogue,
@@ -519,7 +516,7 @@
 
 def end_exchange(count, grad_part, grad_middle, tokens, gain_row):
     rows, width = tokens.shape
-    step = rows // CHUNKS
+    step, chunks = CHUNK_ROWS, rows // CHUNK_ROWS
 
     def epilogue(chunk, total, extra_refs, out_refs):
         value = extra_refs[1][chunk].astype(jnp.float32)
@@ -529,17 +526,17 @@
 
     grad_source, grad_gain = line_exchange(
         count,
-        CHUNKS,
+        chunks,
         step,
         width,
-        grad_part.reshape(count, CHUNKS, step, width),
+        grad_part.reshape(count, chunks, step, width),
         [
-            grad_middle.reshape(CHUNKS, step, width),
-            tokens.reshape(CHUNKS, step, width),
+            grad_middle.reshape(chunks, step, width),
+            tokens.reshape(chunks, step, width),
             gain_row,
         ],
         [
-            jax.ShapeDtypeStruct((CHUNKS, step, width), jnp.float32),
+            jax.ShapeDtypeStruct((chunks, step, width), jnp.float32),
             jax.ShapeDtypeStruct((1, width), jnp.float32),
         ],
         epilogue,
@@ -548,6 +545,11 @@
         zero_gain,
     )
     return grad_source.reshape(rows, width), grad_gain[0]
+
+
+def after(value, *others):
+    zero = sum(other[0, 0].astype(jnp.float32) * 0.0 for other in others)
+    return value + zero.astype(value.dtype)
 
 
 def local(
@@ -581,11 +583,7 @@
     )
     w_o_t = lax.all_gather(w_out.T, "dp", axis=0, tiled=True)
     gate_local = w_gate.transpose(1, 0, 2).reshape(shard_width, hidden_cols)
-    up_local = w_up.transpose(1, 0, 2).reshape(shard_width, hidden_cols)
-    down_local = w_down.transpose(2, 0, 1).reshape(shard_width, hidden_cols)
     full_gate = lax.all_gather(gate_local, "dp", axis=0, tiled=True)
-    full_up = lax.all_gather(up_local, "dp", axis=0, tiled=True)
-    full_down = lax.all_gather(down_local, "dp", axis=0, tiled=True)
     full_router = small[:, 4:]
     model_width = tokens.shape[1]
     local_rows = tokens.shape[0]
@@ -599,6 +597,7 @@
     ffn_scale = gains[3]
     count = lax.axis_size("tensor")
     normed = start_gather(count, tokens, attn_scale[None, :])
+    grad_rows = lax.all_gather(after(cotangent, normed), "tensor", axis=0, tiled=True)
     seq_len = normed.shape[0]
     block_row = block_ids[0]
     cosine_table, sine_table = rope_tables(seq_len, HEAD_DIM)
@@ -610,6 +609,10 @@
         [jnp.sum(query_proj * query_proj, axis=1), jnp.sum(key_proj * key_proj, axis=1)]
     )
     query_sq, key_sq = small_sum(count, squares, 5)
+    up_local = after(w_up, query_sq[None]).transpose(1, 0, 2).reshape(shard_width, hidden_cols)
+    down_local = after(w_down, query_sq[None]).transpose(2, 0, 1).reshape(shard_width, hidden_cols)
+    full_up = lax.all_gather(up_local, "dp", axis=0, tiled=True)
+    full_down = lax.all_gather(down_local, "dp", axis=0, tiled=True)
     query_inv = lax.rsqrt(query_sq / model_width + EPSILON)[:, None]
     key_inv = lax.rsqrt(key_sq / model_width + EPSILON)[:, None]
     query_normed = query_proj * query_inv
@@ -629,7 +632,7 @@
         "sf,df->sd", mixed_low, w_o_t, preferred_element_type=jnp.float32
     ).astype(jnp.bfloat16)
     normed_two, middle = middle_exchange(count, branch_part, tokens, ffn_scale[None, :])
-    grad_rows = lax.all_gather(cotangent, "tensor", axis=0, tiled=True)
+    full_router = after(full_router, grad_rows, normed_two)
     logits = jnp.dot(normed_two, full_router, preferred_element_type=jnp.float32)
     router_probs = jax.nn.softmax(logits, axis=-1)
     kept = kept_mask(routes)
@@ -652,10 +655,6 @@
         grad_hidden * up_part * sigmoid_gate * (1.0 + gate_part * (1.0 - sigmoid_gate))
     ).astype(jnp.bfloat16)
     grad_up_part = (grad_hidden * silu_gate).astype(jnp.bfloat16)
-    grad_two_part = (
-        jnp.einsum("sk,dk->sd", grad_gate_part, full_gate, preferred_element_type=jnp.float32)
-        + jnp.einsum("sk,dk->sd", grad_up_part, full_up, preferred_element_type=jnp.float32)
-    ).astype(jnp.bfloat16)
     grad_gate_w = jnp.einsum(
         "sd,sk->dk", normed_two, grad_gate_part, preferred_element_type=jnp.float32
     ).astype(jnp.bfloat16)
@@ -664,6 +663,13 @@
     ).astype(jnp.bfloat16)
     grad_down_w = jnp.einsum(
         "sd,sk->dk", grad_rows, hidden_gated, preferred_element_type=jnp.float32
+    ).astype(jnp.bfloat16)
+    grad_two_part = after(
+        jnp.einsum("sk,dk->sd", grad_gate_part, full_gate, preferred_element_type=jnp.float32)
+        + jnp.einsum("sk,dk->sd", grad_up_part, full_up, preferred_element_type=jnp.float32),
+        grad_gate_w,
+        grad_up_w,
+        grad_down_w,
     ).astype(jnp.bfloat16)
     ffn_branch = lax.psum_scatter(
         combined, "tensor", scatter_dimension=0, tiled=True
@@ -678,6 +684,9 @@
         "sd,se->de", normed_two, logits_low, preferred_element_type=jnp.float32
     )
     own_logits = lax.dynamic_slice_in_dim(logits_low, tensor_rank * local_rows, local_rows)
+    sum_gate = lax.psum_scatter(grad_gate_w, "dp", scatter_dimension=0, tiled=True)
+    sum_up = lax.psum_scatter(grad_up_w, "dp", scatter_dimension=0, tiled=True)
+    sum_down = lax.psum_scatter(grad_down_w, "dp", scatter_dimension=0, tiled=True)
     router_part = jnp.einsum(
         "se,de->sd", own_logits, full_router, preferred_element_type=jnp.float32
     )
@@ -687,6 +696,13 @@
     grad_out_w = jnp.einsum(
         "sf,sd->df", mixed_low, grad_attn_rows, preferred_element_type=jnp.float32
     ).astype(jnp.bfloat16)
+    grad_router_wide = jnp.pad(grad_router, ((0, 0), (0, 128 - EXPERTS))).astype(jnp.bfloat16)
+    sum_out_router = lax.psum_scatter(
+        jnp.concatenate([grad_out_w, grad_router_wide], axis=1),
+        "dp",
+        scatter_dimension=0,
+        tiled=True,
+    ).astype(jnp.float32)
     grad_mixed = jnp.dot(grad_attn_rows, w_o_t, preferred_element_type=jnp.float32).astype(
         jnp.bfloat16
     )
@@ -695,7 +711,7 @@
         k_rot,
         value_heads,
         block_row,
-        log_totals,
+        after(log_totals, ffn_branch),
         grad_mixed.reshape(seq_len, heads_here, HEAD_DIM),
     )
     grad_query_normed = rotate_back(grad_q_rot, cosine_table, sine_table).reshape(
@@ -709,7 +725,7 @@
     dots = jnp.stack(
         [jnp.sum(query_scaled * query_normed, axis=1), jnp.sum(key_scaled * key_normed, axis=1)]
     )
-    query_dot, key_dot = small_sum(count, dots, 7)
+    query_dot, key_dot = small_sum(count, after(dots, sum_gate, sum_up), 7)
     grad_query_proj = (
         query_inv * (query_scaled - query_normed * (query_dot / model_width)[:, None])
     ).astype(jnp.bfloat16)
@@ -725,31 +741,27 @@
         "sf,df->sd", grad_qkv, w_qkv, preferred_element_type=jnp.float32
     ).astype(jnp.bfloat16)
     grad_source, grad_attn_gain = end_exchange(
-        count, grad_normed_part, grad_middle, tokens, attn_scale[None, :]
-    )
+        count, grad_normed_part, grad_middle, tokens, after(attn_scale[None, :], sum_down)
+    )
+    sum_out_router = after(sum_out_router, grad_attn_gain[None])
+    sum_out = sum_out_router[:, :head_cols]
+    sum_router = sum_out_router[:, head_cols : head_cols + EXPERTS]
     zero_cols = jnp.zeros((model_width,), jnp.float32)
     query_gain_full = lax.dynamic_update_slice_in_dim(zero_cols, grad_query_gain, col_start, 0)
     key_gain_full = lax.dynamic_update_slice_in_dim(zero_cols, grad_key_gain, col_start, 0)
-    gain_rows = lax.psum(
-        jnp.stack([grad_attn_gain, query_gain_full, key_gain_full, grad_ffn_gain]),
+    gain_stack = jnp.stack([grad_attn_gain, query_gain_full, key_gain_full, grad_ffn_gain])
+    total_rows = lax.psum(
+        gain_stack,
         ("dp", "tensor"),
     )
     dp_rank = lax.axis_index("dp")
     gain_width = model_width // (lax.axis_size("dp") * count)
     gain_sums = lax.dynamic_slice_in_dim(
-        gain_rows, (dp_rank * count + tensor_rank) * gain_width, gain_width, 1
-    )
-    sum_gate = lax.psum_scatter(grad_gate_w, "dp", scatter_dimension=0, tiled=True)
-    sum_up = lax.psum_scatter(grad_up_w, "dp", scatter_dimension=0, tiled=True)
-    sum_down = lax.psum_scatter(grad_down_w, "dp", scatter_dimension=0, tiled=True)
-    sum_out = lax.psum_scatter(grad_out_w, "dp", scatter_dimension=0, tiled=True)
+        total_rows, (dp_rank * count + tensor_rank) * gain_width, gain_width, 1
+    )
     sum_qkv = lax.psum_scatter(grad_qkv_w, "dp", scatter_dimension=0, tiled=True).astype(
         jnp.float32
     )
-    router_rows = lax.psum(grad_router.T, "dp")
-    sum_router = lax.dynamic_slice_in_dim(
-        router_rows, dp_rank * shard_width, shard_width, 1
-    ).T
     grad_gate = sum_gate.reshape(shard_width, EXPERTS, ff_here).transpose(1, 0, 2)
     grad_up = sum_up.reshape(shard_width, EXPERTS, ff_here).transpose(1, 0, 2)
     grad_down = sum_down.reshape(shard_width, EXPERTS, ff_here).transpose(1, 2, 0)

time: 1170 us -> 951 us (0.81)
  Pallas kernels: 594 us -> 414 us
  waiting for transfers between devices: 90.7 us -> 39.1 us
  local copies, waits for them, and re-layouts: 91.5 us -> 107 us
    pallas_call x4, Pallas kernels: 572 us -> 389 us  [line_exchange(): pl.pallas_call(kernel, out_shape=tuple(shapes), in_specs=[pl.BlockSpec(me...]
    reduce_scatter x1, waiting for transfers between devices: 71.8 us -> 0.01 us  [local(): lax.psum_scatter(grad_down_w, 'dp', scatter_dimension=0, tiled=True)]
    all_gather x1, waiting for transfers between devices: 0.01 us -> 38.1 us  [local(): lax.all_gather(after(cotangent, normed), 'tensor', axis=0, tiled=True)]
    reduce_scatter x1, waiting for transfers between devices: 16.9 us -> 0.01 us  [local(): sum_up = lax.psum_scatter(grad_up_w, 'dp', scatter_dimension=0, tiled=True)]
    slice x1 -> x14, local copies, waits for them, and re-layouts: 0.29 us -> 15.1 us  [the longest x12 14.2 us: after(): zero = sum((other[0, 0].astype(jnp.float32) * 0.0 for other in others))]
    unnamed x114 -> x142, local copies, waits for them, and re-layouts: 39.5 us -> 36.7 us
  transfers between devices with their start and end apart: 13 -> 12, of which waited for: 2 -> 1; matrix products, arithmetic and copies ran while one was open for 28% -> 37% of each run, Pallas kernels for 51% -> 44%
where the time goes in v3:
time: 951 us; the launch traced here: 944 us
  Pallas kernels  414 us (44%)
  matrix products  233 us (25%)
  local copies, waits for them, and re-layouts  107 us (11%)
  other arithmetic  72.3 us (8%)
  blocking collectives  52.9 us (6%)
  waiting for transfers between devices  39.1 us (4%)
  between operations  23.3 us (2%)
    pallas_call x4, Pallas kernels, line_exchange(): pl.pallas_call(kernel, out_shape=tuple(shapes), in_specs=[pl.BlockSpec(me...  389 us
    psum x1, blocking collectives, local(): total_rows = lax.psum(gain_stack, ('dp', 'tensor'))  42.4 us
    all_gather x1, waiting for transfers between devices, local(): lax.all_gather(after(cotangent, normed), 'tensor', axis=0, tiled=True)  38.1 us
    unnamed x142, local copies, waits for them, and re-layouts  36.7 us
    dot_general x1, matrix products, local(): jnp.dot(grad_rows, full_down, preferred_element_type=jnp.float32)  26.5 us
    pallas_call x3, Pallas kernels, small_sum(): pl.pallas_call(kernel, out_shape=jax.ShapeDtypeStruct(values.shape, jnp.f...  24.7 us
  transfers between devices with their start and end apart: 12, of which 1 were waited for; matrix products, arithmetic and copies ran while one was open for 37% of the time, Pallas kernels for 44%

profile of v3, /device:TPU:0, one launch (start us, length us, event | category | flops | bytes accessed | tf_op | source)
XLA Modules:
  0.0 943.7 jit_solution(255157742916135552)
XLA Ops:
  12.9 10.6 %all_gather.21 = bf16[2048,12]{0,1:T(8,128)(2,1)S(1)} all-gather(bf16[256,12]{0,1:T(8,128)(2,1)S(1)} %concatenate.43), channel_id=1, replica_groups=mesh['dp'=8,'tensor'=4] {'dp'}, dimensions={0}, use_global_device_ids=true | all-gather | bytes 55296 | tf_op jit(solution)/shard_map/all_gather | solution.py:580
  24.1 78.0 %shard_map.263 = bf16[4,16,16,2048]{3,2,1,0:T(8,128)(2,1)} custom-call(bf16[16,16,2048]{2,1,0:T(8,128)(2,1)} %bitcast.302, f32[1,2048]{1,0:T(1,128)} %get-tuple-element.324.refs_1_), custom_call_target="tpu_custom_call" | custom-call | bytes 188743680 | tf_op jit(solution)/shard_map/pallas_call | solution.py:361
  107.8 10.3 %fusion.71 = f32[1024,1536]{1,0:T(8,128)S(1)} fusion(bf16[1024,2048]{1,0:T(8,128)(2,1)} %bitcast.314, bf16[2048,1536]{1,0:T(8,128)(2,1)} %all-gather.7.cloned.1.call-done), kind=kOutput, calls=%fused_computation.187 | convolution fusion | flops 6442450944 | bytes 16777216 | tf_op jit(solution)/shard_map/dot_general | solution.py:604
  118.1 2.6 copy-done.8
  121.7 7.4 shard_map.264
  141.7 4.0 multiply_cosine_fusion
  147.1 38.1 %all-gather.15.cloned.1.call-done = bf16[1024,2048]{1,0:T(8,128)(2,1)} async-done(((bf16[256,2048]{1,0:T(8,128)(2,1)}), bf16[1024,2048]{1,0:T(8,128)(2,1)}) %all-gather.15.cloned.1.call-update) | async-done | bytes 4194320 | tf_op jit(solution)/shard_map/all_gather | solution.py:600
  186.5 3.9 multiply_bitcast_fusion
  193.9 2.8 slice.240
  202.1 3.1 concatenate.47
  205.2 4.1 copy.111
  209.3 3.9 fusion.36
  213.3 2.5 copy.117
  220.6 17.1 %while.27 = (s32[]{:T(128)}, bf16[2,512,512]{2,1,0:T(8,128)(2,1)}, f32[2,4,512]{2,1,0:T(4,128)S(1)}, s32[1,1024]{1,0:T(1,128)S(1)}, s32[2,512]{1,0:T(2,128)S(1)}...) while((s32[]{:T(128)}, bf16[2,512,512]{2,1,0:T(8,128)(2,1)}, ...), condition=%wide.region_5.6_spmd, body=%wide.region_2.5_spmd.sunk | while | flops 1097332736 | bytes 36776580 | solution.py:85
  223.3 2.5 exponential_reduce_fusion.2
  225.8 2.6 fusion.132
  231.5 2.5 exponential_reduce_fusion.2
  234.0 2.6 fusion.132
  237.7 7.0 convolution_convert_fusion.6
  244.7 116.8 %shard_map.265 = (bf16[4,16,16,2048]{3,2,1,0:T(8,128)(2,1)}, f32[16,16,2048]{2,1,0:T(8,128)}) custom-call(bf16[4,16,16,2048]{3,2,1,0:T(8,128)(2,1)} %bitcast.316, bf16[16,16,2048]{2,1,0:T(8,128)(2,1)} %bitcast.303, f32[1,2048]{1,0:T(1,128)} %get-tuple-element.321.refs_2_.refs_4_), custom_call_target="tpu_custom_call" | custom-call | bytes 251658240 | tf_op jit(solution)/shard_map/pallas_call | solution.py:361
  364.0 3.4 fusion.70
  369.5 7.4 copy.165
  376.9 14.5 %fusion.72 = f32[1024,2048]{1,0:T(8,128)} fusion(bf16[1024,2048]{1,0:T(8,128)(2,1)} %bitcast.295, bf16[2048,2048]{0,1:T(8,128)(2,1)} %all-gather.11.cloned.1.call-done), kind=kOutput, calls=%fused_computation.188 | convolution fusion | flops 8589934592 | bytes 20971520 | tf_op jit(solution)/shard_map/dot_general | solution.py:642
  391.3 14.7 %fusion.73 = f32[1024,2048]{1,0:T(8,128)} fusion(bf16[1024,2048]{1,0:T(8,128)(2,1)} %bitcast.296, bf16[2048,2048]{0,1:T(8,128)(2,1)} %all-gather.13.cloned.1.call-done), kind=kOutput, calls=%fused_computation.189 | convolution fusion | flops 8589934592 | bytes 20971520 | tf_op jit(solution)/shard_map/dot_general | solution.py:643
  406.0 26.5 %multiply_multiply_fusion = (f32[1024,2048]{1,0:T(8,128)}, bf16[1024,2048]{1,0:T(8,128)(2,1)}, bf16[1024,2048]{1,0:T(8,128)(2,1)}, bf16[1024,2048]{1,0:T(8,128)(2,1)}) fusion(f32[1024,2048]{1,0:T(8,128)} %fusion.73, f32[1024,2048]{1,0:T(8,128)} %fusion.72, f32[1024,2048]{1,0:T(8,128)} %bitcast.306, bf16[1024,2048]{1,0:T(8,128)(2,1)} %all-gather.15.cloned.1.call-done, ...), kind=kOutput, calls=%fused_computation.61 | convolution fusion | flops 8627683328 | bytes 58720256 | tf_op jit(solution)/shard_map/dot_general | solution.py:651
  432.5 13.8 %convolution_convert_fusion.5 = bf16[1024,2048]{1,0:T(8,128)(2,1)} fusion(bf16[1024,2048]{1,0:T(8,128)(2,1)} %get-tuple-element.302, bf16[2048,2048]{0,1:T(8,128)(2,1)} %all-gather.17.cloned.1.call-done), kind=kOutput, calls=%fused_computation.59 | convolution fusion | flops 8592031744 | bytes 16777216 | tf_op jit(solution)/shard_map/sk,dk->sd/dot_general | solution.py:648
  446.4 14.5 %convolution_convert_fusion.2 = bf16[2048,2048]{1,0:T(8,128)(2,1)} fusion(bf16[1024,2048]{1,0:T(8,128)(2,1)} %bitcast.297, bf16[1024,2048]{1,0:T(8,128)(2,1)} %get-tuple-element.303), kind=kOutput, calls=%fused_computation.54 | convolution fusion | flops 8594128896 | bytes 16777216 | tf_op jit(solution)/shard_map/sd,sk->dk/dot_general | solution.py:661
  460.9 14.0 %convolution_convert_fusion.3 = bf16[2048,2048]{1,0:T(8,128)(2,1)} fusion(bf16[1024,2048]{1,0:T(8,128)(2,1)} %bitcast.298, bf16[1024,2048]{1,0:T(8,128)(2,1)} %get-tuple-element.301), kind=kOutput, calls=%fused_computation.55 | convolution fusion | flops 8594128896 | bytes 16777216 | tf_op jit(solution)/shard_map/sd,sk->dk/dot_general | solution.py:658
  475.0 14.3 %convolution_convert_fusion.1 = bf16[2048,2048]{1,0:T(8,128)(2,1)} fusion(bf16[1024,2048]{1,0:T(8,128)(2,1)} %all-gather.15.cloned.1.call-done, bf16[1024,2048]{1,0:T(8,128)(2,1)} %get-tuple-element.302), kind=kOutput, calls=%fused_computation.53 | convolution fusion | flops 8594128896 | bytes 16777216 | tf_op jit(solution)/shard_map/sd,sk->dk/dot_general | solution.py:664
  489.5 2.7 copy_bitcast_fusion.4
  495.8 10.9 %copy.166 = f32[128,8,8,256]{3,2,1,0:T(8,128)} copy(f32[128,8,8,256]{3,1,2,0:T(8,128)} %bitcast.305) | data formatting | bytes 16777216
  506.7 4.6 reduce_sum.104
  512.1 9.9 %shard_map.266 = f32[8,1024]{1,0:T(8,128)} custom-call(f32[8,1024]{1,0:T(8,128)} %bitcast_multiply_fusion.5.in_ref), custom_call_target="tpu_custom_call" | custom-call | tf_op jit(solution)/shard_map/pallas_call | solution.py:408
  527.4 12.8 %fusion.74 = f32[1024,2048]{1,0:T(8,128)S(1)} fusion(bf16[1024,2048]{1,0:T(8,128)(2,1)} %get-tuple-element.301, bf16[2048,2048]{0,1:T(8,128)(2,1)} %all-gather.11.cloned.1.call-done), kind=kOutput, calls=%fused_computation.190 | convolution fusion | flops 8589934592 | bytes 20971520 | tf_op jit(solution)/shard_map/sk,dk->sd/dot_general | solution.py:668
  540.2 13.3 %add_convert_fusion = bf16[1024,2048]{1,0:T(8,128)(2,1)} fusion(f32[1024,2048]{1,0:T(8,128)S(1)} %fusion.74, f32[]{:T(128)} %bitcast.35, bf16[1024,2048]{1,0:T(8,128)(2,1)S(1)} %copy-done.74, bf16[2048,2048]{0,1:T(8,128)(2,1)} %all-gather.13.cloned.1.call-done), kind=kOutput, calls=%fused_computation.46 | convolution fusion | flops 8596226048 | bytes 25165828 | tf_op jit(solution)/shard_map/sk,dk->sd/dot_general | solution.py:669
  553.5 117.3 %shard_map.267 = (bf16[4,16,16,2048]{3,2,1,0:T(8,128)(2,1)}, f32[16,16,2048]{2,1,0:T(8,128)}, f32[1,2048]{1,0:T(1,128)}) custom-call(bf16[4,16,16,2048]{3,2,1,0:T(8,128)(2,1)} %bitcast.322, f32[16,16,2048]{2,1,0:T(8,128)} %bitcast.310, f32[16,16,2048]{2,1,0:T(8,128)} %get-tuple-element.124.refs_2_, bf16[16,16,2048]{2,1,0:T(8,128)(2,1)} %bitcast.323, ...), custom_call_target="tpu_custom_call" | custom-call | bytes 251658240 | tf_op jit(solution)/shard_map/pallas_call | solution.py:361
  670.7 4.6 convolution_convert_fusion.9
  676.5 3.0 convolution_convert_fusion.8
  680.2 2.5 convolution_convert_fusion.7
  686.6 45.0 %while.28 = (s32[]{:T(128)}, f32[1024,4,128]{0,2,1:T(8,128)S(1)}, f32[1024,4,128]{0,2,1:T(8,128)}, f32[2,512,4,128]{3,1,2,0:T(8,128)}, bf16[2,512,4,128]{3,1,2,0...) while((s32[]{:T(128)}, f32[1024,4,128]{0,2,1:T(8,128)S(1)}, ...), condition=%wide.region_15.16_spmd.clone, body=%wide.region_13.15_spmd.clone.sunk | while | flops 2719217664 | bytes 181473200 | solution.py:129
  687.1 2.6 fusion.141
  690.3 3.5 multiply_reduce_fusion.7
  694.3 3.7 multiply_convert_fusion.7
  698.0 3.8 bitcast_add_fusion.5
  705.3 3.8 bitcast_add_fusion.6
  709.1 2.4 fusion.141
  712.2 3.5 multiply_reduce_fusion.7
  715.7 3.7 multiply_convert_fusion.7
  719.4 3.8 bitcast_add_fusion.5
  726.5 5.1 bitcast_add_fusion.6
  731.5 3.2 copy.131
  734.8 2.7 copy.129
  739.2 2.9 convert_element_type.235
  742.1 2.3 copy.142
  751.7 4.0 multiply_reduce_fusion.1
  760.0 7.4 shard_map.268
  768.2 5.0 multiply_convert_fusion.5
  774.5 9.5 %convolution_convert_fusion = bf16[2048,1536]{1,0:T(8,128)(2,1)} fusion(bf16[1024,2048]{1,0:T(8,128)(2,1)S(1)} %bitcast.315, bf16[1024,512]{1,0:T(8,128)(2,1)S(1)} %copy-done.36, bf16[1024,512]{1,0:T(8,128)(2,1)S(1)} %get-tuple-element.305, bf16[1024,512]{1,0:T(8,128)(2,1)S(1)} %get-tuple-element.304), kind=kOutput, calls=%fused_computation.52 | convolution fusion | flops 6455033856 | bytes 13631488 | tf_op jit(solution)/shard_map/sd,sf->df/dot_general | solution.py:737
  785.6 2.6 fusion.40
  791.4 10.8 %convolution_convert_fusion.4 = bf16[1024,2048]{1,0:T(8,128)(2,1)} fusion(bf16[2048,1536]{1,0:T(8,128)(2,1)} %all-gather.7.cloned.1.call-done, bf16[1024,512]{1,0:T(8,128)(2,1)} %copy.142, bf16[1024,512]{1,0:T(8,128)(2,1)} %copy-done.32, bf16[1024,512]{1,0:T(8,128)(2,1)S(1)} %copy-done.31), kind=kOutput, calls=%fused_computation.58 | convolution fusion | flops 6453985280 | bytes 13631488 | tf_op jit(solution)/shard_map/sf,df->sd/dot_general | solution.py:740
  802.2 77.2 %shard_map.269 = (f32[16,16,2048]{2,1,0:T(8,128)}, f32[1,2048]{1,0:T(1,128)}) custom-call(bf16[4,16,16,2048]{3,2,1,0:T(8,128)(2,1)} %bitcast.319, f32[16,16,2048]{2,1,0:T(8,128)} %get-tuple-element.131.refs_1_, bf16[16,16,2048]{2,1,0:T(8,128)(2,1)} %bitcast.304, f32[1,2048]{1,0:T(1,128)} %broadcast_add_fusion.3.refs_3_), custom_call_target="tpu_custom_call" | custom-call | bytes 188743680 | tf_op jit(solution)/shard_map/pallas_call | solution.py:361
  886.5 2.7 copy.143
  889.2 42.4 %psum.7 = f32[4,2048]{1,0:T(4,128)S(1)} all-reduce(f32[4,2048]{1,0:T(4,128)S(1)} %pad_maximum_fusion.8), channel_id=1, replica_groups=mesh['dp'=8,'tensor'=4] {'dp','tensor'}, use_global_device_ids=true, to_apply=%region_23.24 | all-reduce | flops 8192 | bytes 65536 | tf_op jit(solution)/shard_map/psum | solution.py:753
  933.0 2.3 fusion.67
  (324 shorter events, 98.4 us)
Async XLA Ops:
  7.2 96.8 %copy-start.26 = (bf16[256,2048]{1,0:T(8,128)(2,1)S(1)}, bf16[256,2048]{1,0:T(8,128)(2,1)}, u32[]{:S(2)}) copy-start(bf16[256,2048]{1,0:T(8,128)(2,1)} %param.21) | copy-start | bytes 3145732
  7.2 100.6 %all-gather.7.cloned.1.call-start = ((), (), s32[]{:S(2)}) async-start(), calls=%async_computation.6 | async-start | bytes 7077888 | tf_op jit(solution)/shard_map/all_gather | solution.py:581
  9.4 175.8 %all-gather.15.cloned.1.call-start = ((), (), s32[]{:S(2)}) async-start(), calls=%async_computation.10 | async-start | bytes 5242880 | tf_op jit(solution)/shard_map/all_gather | solution.py:600
  23.4 340.5 %copy-start.42 = (bf16[2048,12]{0,1:T(8,128)(2,1)}, bf16[2048,12]{0,1:T(8,128)(2,1)S(1)}, u32[]{:S(2)}) copy-start(bf16[2048,12]{0,1:T(8,128)(2,1)S(1)} %all_gather.21) | copy-start | bytes 147460
  24.1 81.8 %copy-start.33 = (bf16[8,256,256]{2,1,0:T(8,128)(2,1)S(1)}, bf16[8,256,256]{2,1,0:T(8,128)(2,1)}, u32[]{:S(2)}) copy-start(bf16[8,256,256]{2,1,0:T(8,128)(2,1)} %param.33) | copy-start | bytes 3145732
  102.1 5.2 copy-start.34
  105.1 132.6 %all-gather.9.cloned.1.call-start = ((), (), s32[]{:S(2)}) async-start(), calls=%async_computation.7 | async-start | bytes 2359296 | tf_op jit(solution)/shard_map/all_gather | solution.py:584
  105.8 271.0 %all-gather.11.cloned.1.call-start = ((), (), s32[]{:S(2)}) async-start(), calls=%async_computation.8 | async-start | bytes 9437184 | tf_op jit(solution)/shard_map/all_gather | solution.py:586
  107.2 284.1 %all-gather.13.cloned.1.call-start = ((), (), s32[]{:S(2)}) async-start(), calls=%async_computation.9 | async-start | bytes 9437184 | tf_op jit(solution)/shard_map/all_gather | solution.py:614
  120.7 11.3 %copy-start.35 = (bf16[8,256,256]{2,1,0:T(8,128)(2,1)S(1)}, bf16[8,256,256]{2,1,0:T(8,128)(2,1)}, u32[]{:S(2)}) copy-start(bf16[8,256,256]{2,1,0:T(8,128)(2,1)} %param.35) | copy-start | bytes 3145732
  132.0 274.0 %all-gather.17.cloned.1.call-start = ((), (), s32[]{:S(2)}) async-start(), calls=%async_computation.11 | async-start | bytes 9437184 | tf_op jit(solution)/shard_map/all_gather | solution.py:615
  132.7 53.7 %copy-start.65 = (f32[2,1024]{1,0:T(2,128)S(1)}, f32[2,1024]{1,0:T(2,128)}, u32[]{:S(2)}) copy-start(f32[2,1024]{1,0:T(2,128)} %shard_map.264) | copy-start | bytes 24580
  134.1 550.6 %reduce-scatter.7.cloned.1.call-start = ((), (), s32[]{:S(2)}) async-start(), calls=%async_computation.12 | async-start | bytes 5242880 | tf_op jit(solution)/shard_map/reduce_scatter | solution.py:674
  135.7 231.8 %copy-start.53 = (s32[1024,1]{0,1:T(1,128)}, s32[1024,1]{0,1:T(1,128)S(1)}, u32[]{:S(2)}) copy-start(s32[1024,1]{0,1:T(1,128)S(1)} %get-tuple-element.327) | copy-start | bytes 12292
  135.7 231.8 %copy-start.55 = (s32[1024,1]{0,1:T(1,128)}, s32[1024,1]{0,1:T(1,128)S(1)}, u32[]{:S(2)}) copy-start(s32[1024,1]{0,1:T(1,128)S(1)} %get-tuple-element.328) | copy-start | bytes 12292
  138.5 51.9 %copy-start.61 = (f32[1,512]{1,0:T(1,128)}, f32[1,512]{1,0:T(1,128)S(1)}, u32[]{:S(2)}) copy-start(f32[1,512]{1,0:T(1,128)S(1)} %get-tuple-element.341) | copy-start | bytes 6148
  138.5 51.9 %copy-start.63 = (f32[1,512]{1,0:T(1,128)}, f32[1,512]{1,0:T(1,128)S(1)}, u32[]{:S(2)}) copy-start(f32[1,512]{1,0:T(1,128)S(1)} %get-tuple-element.342) | copy-start | bytes 6148
  147.1 220.4 %copy-start.44 = (s32[1,8,8,128]{3,2,1,0:T(8,128)}, s32[1,8,8,128]{3,2,1,0:T(8,128)S(1)}, u32[]{:S(2)}) copy-start(s32[1,8,8,128]{3,2,1,0:T(8,128)S(1)} %add_bitcast_fusion.1) | copy-start | bytes 98308
  186.4 4.0 copy-start.57
  186.4 4.0 copy-start.59
  193.9 4.6 copy-start.20
  237.7 7.0 copy-start.3
  237.7 7.0 copy-start.7
  237.7 7.0 copy-start.47
  237.7 7.0 copy-start.66
  446.3 309.4 %reduce-scatter.11.cloned.1.call-start = ((), (), s32[]{:S(2)}) async-start(), calls=%async_computation.14 | async-start | bytes 9437184 | tf_op jit(solution)/shard_map/reduce_scatter | solution.py:688
  460.9 296.1 %reduce-scatter.9.cloned.1.call-start = ((), (), s32[]{:S(2)}) async-start(), calls=%async_computation.13 | async-start | bytes 9437184 | tf_op jit(solution)/shard_map/reduce_scatter | solution.py:687
  475.0 313.3 %reduce-scatter.13.cloned.1.call-start = ((), (), s32[]{:S(2)}) async-start(), calls=%async_computation.15 | async-start | bytes 9437184 | tf_op jit(solution)/shard_map/reduce_scatter | solution.py:689
  489.4 392.0 %reduce-scatter.17.cloned.1.call-start = ((), (), s32[]{:S(2)}) async-start(), calls=%async_computation.17 | async-start | bytes 2949120 | tf_op jit(solution)/shard_map/reduce_scatter | solution.py:700
  506.6 4.8 copy-start.45
  506.6 4.8 copy-start.54
  506.6 4.8 copy-start.56
  506.6 17.3 %copy-start.39 = (f32[1024,8]{0,1:T(8,128)S(1)}, f32[1024,8]{0,1:T(8,128)}, u32[]{:S(2)}) copy-start(f32[1024,8]{0,1:T(8,128)} %copy-done.38) | copy-start | bytes 98308
  506.6 17.3 %copy-start.50 = (f32[1024]{0:T(1024)S(1)}, f32[1024]{0:T(1024)}, u32[]{:S(2)}) copy-start(f32[1024]{0:T(1024)} %copy-done.49) | copy-start | bytes 12292
  506.7 17.3 %copy-start.52 = (f32[1024]{0:T(1024)S(1)}, f32[1024]{0:T(1024)}, u32[]{:S(2)}) copy-start(f32[1024]{0:T(1024)} %copy-done.51) | copy-start | bytes 12292
  506.7 18.9 %copy-start.43 = (bf16[2048,12]{0,1:T(8,128)(2,1)S(1)}, bf16[2048,12]{0,1:T(8,128)(2,1)}, u32[]{:S(2)}) copy-start(bf16[2048,12]{0,1:T(8,128)(2,1)} %copy-done.42) | copy-start | bytes 147460
  527.4 12.8 %copy-start.74 = (bf16[1024,2048]{1,0:T(8,128)(2,1)S(1)}, bf16[1024,2048]{1,0:T(8,128)(2,1)}, u32[]{:S(2)}) copy-start(bf16[1024,2048]{1,0:T(8,128)(2,1)} %get-tuple-element.303) | copy-start | bytes 12582916
  553.5 117.3 %copy-start.72 = (bf16[2048,512]{0,1:T(8,128)(2,1)S(1)}, bf16[2048,512]{0,1:T(8,128)(2,1)}, u32[]{:S(2)}) copy-start(bf16[2048,512]{0,1:T(8,128)(2,1)} %all-gather.9.cloned.1.call-done) | copy-start | bytes 6291460
  682.7 3.8 copy-start.4
  682.8 3.8 copy-start.41
  682.8 3.8 copy-start.48
  684.6 248.5 %reduce-scatter.15.cloned.1.call-start = ((), (), s32[]{:S(2)}) async-start(), calls=%async_computation.16 | async-start | bytes 7077888 | tf_op jit(solution)/shard_map/reduce_scatter | solution.py:762
  689.7 4.4 copy-start
  690.1 4.2 copy-start.5
  698.0 6.7 copy-start.1
  711.5 4.2 copy-start
  719.4 3.9 copy-start.2
  719.4 6.5 copy-start.1
  737.4 7.0 copy-start.24
  739.2 5.2 copy-start.12
  747.0 4.0 slice-start.1
  747.0 4.6 copy-start.22
  747.0 4.6 copy-start.58
  747.1 4.6 copy-start.60
  747.1 4.6 copy-start.62
  747.1 4.6 copy-start.64
  768.2 6.3 copy-start.25
  768.2 6.3 copy-start.36
  784.0 7.4 copy-start.31
  802.2 80.8 %copy-start.28 = (bf16[256,2048]{1,0:T(8,128)(2,1)S(1)}, bf16[256,2048]{1,0:T(8,128)(2,1)}, u32[]{:S(2)}) copy-start(bf16[256,2048]{1,0:T(8,128)(2,1)} %reduce-scatter.11.cloned.1.call-done) | copy-start | bytes 3145732
  879.4 5.3 copy-start.29
  885.0 4.2 copy-start.69
  885.0 4.2 copy-start.70
  886.5 48.9 %copy-start.27 = (f32[16,16,2048]{2,1,0:T(8,128)S(1)}, f32[16,16,2048]{2,1,0:T(8,128)}, u32[]{:S(2)}) copy-start(f32[16,16,2048]{2,1,0:T(8,128)} %get-tuple-element.132) | copy-start | bytes 6291460
  (35 other events, 91.4 us)
Sparse Core Ops, SparseCore 0:
  10.5 48.1 all-gather.6
  105.2 79.9 all-gather.14
  187.1 26.4 all-gather.8
  215.3 55.8 all-gather.10
  273.0 55.8 all-gather.12
  330.6 55.8 all-gather.16
  446.5 77.9 reduce-scatter.6
  527.9 71.9 reduce-scatter.10
  603.4 71.4 reduce-scatter.8
  678.2 71.4 reduce-scatter.12
  753.1 43.4 reduce-scatter.16
  799.8 61.7 reduce-scatter.14

commit v4 on v3

--- a/solution.py
+++ b/solution.py
@@ -376,13 +376,13 @@
     return results
 
 
-def small_sum(count, values, collective_id):
+def small_sum(count, values, collective_id, axis="tensor"):
     def kernel(in_ref, out_ref, slots, send_sems, recv_sems):
-        me = lax.axis_index("tensor")
+        me = lax.axis_index(axis)
         barrier = pltpu.get_barrier_semaphore()
         for offset in range(1, count):
             peer = lax.rem(me + offset, count)
-            pl.semaphore_signal(barrier, inc=1, device_id={"tensor": peer}, device_id_type=MESH)
+            pl.semaphore_signal(barrier, inc=1, device_id={axis: peer}, device_id_type=MESH)
         pl.semaphore_wait(barrier, count - 1)
 
         def send(offset):
@@ -391,7 +391,7 @@
                 dst_ref=slots.at[offset - 1],
                 send_sem=send_sems.at[offset - 1],
                 recv_sem=recv_sems.at[offset - 1],
-                device_id={"tensor": lax.rem(me + offset, count)},
+                device_id={axis: lax.rem(me + offset, count)},
                 device_id_type=MESH,
             )
 
@@ -547,8 +547,114 @@
     return grad_source.reshape(rows, width), grad_gain[0]
 
 
+def expert_kernel(x_ref, c_ref, gates_ref, wg_ref, wu_ref, wd_ref, hg_ref, dg_ref, du_ref, gd_ref):
+    expert = pl.program_id(0)
+    rows_in = x_ref[...]
+    gate_part = jnp.dot(rows_in, wg_ref[...], preferred_element_type=jnp.float32)
+    up_part = jnp.dot(rows_in, wu_ref[...], preferred_element_type=jnp.float32)
+    back_hidden = jnp.dot(c_ref[...], wd_ref[...], preferred_element_type=jnp.float32)
+    mine = lax.broadcasted_iota(jnp.int32, gates_ref.shape, 1) == expert
+    gates = jnp.sum(jnp.where(mine, gates_ref[...], 0.0), axis=1, keepdims=True)
+    sigmoid_gate = jax.nn.sigmoid(gate_part)
+    silu_gate = gate_part * sigmoid_gate
+    hidden = silu_gate * up_part
+    gate_dot = jnp.sum(hidden * back_hidden, axis=1, keepdims=True)
+
+    @pl.when(expert == 0)
+    def _():
+        gd_ref[...] = jnp.zeros_like(gd_ref)
+
+    gd_ref[...] = gd_ref[...] + jnp.where(mine, gate_dot, 0.0)
+    hg_ref[...] = (hidden * gates).astype(jnp.bfloat16)
+    grad_hidden = back_hidden * gates
+    dg_ref[...] = (
+        grad_hidden * up_part * sigmoid_gate * (1.0 + gate_part * (1.0 - sigmoid_gate))
+    ).astype(jnp.bfloat16)
+    du_ref[...] = (grad_hidden * silu_gate).astype(jnp.bfloat16)
+
+
+def expert_parts(rows_in, rows_grad, gates, weights, ff_here):
+    seq_len, width = rows_in.shape
+    hidden_cols = EXPERTS * ff_here
+    whole = pl.BlockSpec(memory_space=pltpu.VMEM)
+    part = jax.ShapeDtypeStruct((seq_len, hidden_cols), jnp.bfloat16)
+    column = pl.BlockSpec((seq_len, ff_here), lambda e: (0, e))
+    flops = 6 * seq_len * width * hidden_cols
+    return pl.pallas_call(
+        expert_kernel,
+        grid=(EXPERTS,),
+        out_shape=(part, part, part, jax.ShapeDtypeStruct((seq_len, EXPERTS), jnp.float32)),
+        in_specs=[
+            whole,
+            whole,
+            whole,
+            pl.BlockSpec((width, ff_here), lambda e: (0, e)),
+            pl.BlockSpec((width, ff_here), lambda e: (0, EXPERTS + e)),
+            pl.BlockSpec((width, ff_here), lambda e: (0, 2 * EXPERTS + e)),
+        ],
+        out_specs=(
+            column,
+            column,
+            column,
+            pl.BlockSpec((seq_len, EXPERTS), lambda e: (0, 0)),
+        ),
+        compiler_params=pltpu.CompilerParams(vmem_limit_bytes=56 * 1024 * 1024),
+        cost_estimate=pl.CostEstimate(
+            flops=flops, bytes_accessed=weights.size * 2, transcendentals=0
+        ),
+    )(rows_in, rows_grad, gates, weights, weights, weights)
+
+
+def product_kernel(hg_ref, dg_ref, du_ref, x_ref, c_ref, w_ref, out_ref, dx_ref, dw_ref):
+    cols = hg_ref.shape[1]
+
+    def times_weight(left, which):
+        right = w_ref[:, which * cols : (which + 1) * cols]
+        return lax.dot_general(
+            left, right, (((1,), (1,)), ((), ())), preferred_element_type=jnp.float32
+        )
+
+    def weight_grad(rows, grad):
+        return lax.dot_general(
+            rows, grad, (((0,), (0,)), ((), ())), preferred_element_type=jnp.float32
+        ).astype(jnp.bfloat16)
+
+    out_ref[...] = times_weight(hg_ref[...], 2).astype(jnp.bfloat16)
+    dx_ref[...] = (times_weight(dg_ref[...], 0) + times_weight(du_ref[...], 1)).astype(
+        jnp.bfloat16
+    )
+    dw_ref[:, :cols] = weight_grad(x_ref[...], dg_ref[...])
+    dw_ref[:, cols : 2 * cols] = weight_grad(x_ref[...], du_ref[...])
+    dw_ref[:, 2 * cols :] = weight_grad(c_ref[...], hg_ref[...])
+
+
+def expert_products(hg, dg, du, rows_in, rows_grad, weights):
+    seq_len, width = rows_in.shape
+    cols = hg.shape[1]
+    tile = 256
+    whole = pl.BlockSpec(memory_space=pltpu.VMEM)
+    column = pl.BlockSpec((seq_len, tile), lambda i: (0, i))
+    row = pl.BlockSpec((tile, 3 * cols), lambda i: (i, 0))
+    flat = jax.ShapeDtypeStruct((seq_len, width), jnp.bfloat16)
+    return pl.pallas_call(
+        product_kernel,
+        grid=(width // tile,),
+        out_shape=(flat, flat, jax.ShapeDtypeStruct((width, 3 * cols), jnp.bfloat16)),
+        in_specs=[whole, whole, whole, column, column, row],
+        out_specs=(column, column, row),
+        compiler_params=pltpu.CompilerParams(vmem_limit_bytes=56 * 1024 * 1024),
+        cost_estimate=pl.CostEstimate(
+            flops=12 * seq_len * width * cols, bytes_accessed=weights.size * 4, transcendentals=0
+        ),
+    )(hg, dg, du, rows_in, rows_grad, weights)
+
+
 def after(value, *others):
-    zero = sum(other[0, 0].astype(jnp.float32) * 0.0 for other in others)
+    product = 0.0
+    for other in others:
+        corner = jnp.clip(other[0, 0].astype(jnp.float32), -1.0, 1.0)
+        product = corner if other is others[0] else product * corner
+    zero = product * 0.0
     return value + zero.astype(value.dtype)
 
 
@@ -582,8 +688,14 @@
         jnp.concatenate([w_query, w_key, w_value], axis=1), "dp", axis=0, tiled=True
     )
     w_o_t = lax.all_gather(w_out.T, "dp", axis=0, tiled=True)
-    gate_local = w_gate.transpose(1, 0, 2).reshape(shard_width, hidden_cols)
-    full_gate = lax.all_gather(gate_local, "dp", axis=0, tiled=True)
+    expert_local = jnp.concatenate(
+        [
+            w_gate.transpose(1, 0, 2).reshape(shard_width, hidden_cols),
+            w_up.transpose(1, 0, 2).reshape(shard_width, hidden_cols),
+            w_down.transpose(2, 0, 1).reshape(shard_width, hidden_cols),
+        ],
+        axis=1,
+    )
     full_router = small[:, 4:]
     model_width = tokens.shape[1]
     local_rows = tokens.shape[0]
@@ -609,10 +721,9 @@
         [jnp.sum(query_proj * query_proj, axis=1), jnp.sum(key_proj * key_proj, axis=1)]
     )
     query_sq, key_sq = small_sum(count, squares, 5)
-    up_local = after(w_up, query_sq[None]).transpose(1, 0, 2).reshape(shard_width, hidden_cols)
-    down_local = after(w_down, query_sq[None]).transpose(2, 0, 1).reshape(shard_width, hidden_cols)
-    full_up = lax.all_gather(up_local, "dp", axis=0, tiled=True)
-    full_down = lax.all_gather(down_local, "dp", axis=0, tiled=True)
+    full_experts = lax.all_gather(
+        after(expert_local, query_sq[None]), "dp", axis=0, tiled=True
+    )
     query_inv = lax.rsqrt(query_sq / model_width + EPSILON)[:, None]
     key_inv = lax.rsqrt(key_sq / model_width + EPSILON)[:, None]
     query_normed = query_proj * query_inv
@@ -632,45 +743,16 @@
         "sf,df->sd", mixed_low, w_o_t, preferred_element_type=jnp.float32
     ).astype(jnp.bfloat16)
     normed_two, middle = middle_exchange(count, branch_part, tokens, ffn_scale[None, :])
-    full_router = after(full_router, grad_rows, normed_two)
     logits = jnp.dot(normed_two, full_router, preferred_element_type=jnp.float32)
     router_probs = jax.nn.softmax(logits, axis=-1)
     kept = kept_mask(routes)
     gate_values = router_probs * kept
-    gates = jnp.repeat(gate_values, ff_here, axis=1)
-
-    gate_part = jnp.dot(normed_two, full_gate, preferred_element_type=jnp.float32)
-    up_part = jnp.dot(normed_two, full_up, preferred_element_type=jnp.float32)
-    sigmoid_gate = jax.nn.sigmoid(gate_part)
-    silu_gate = gate_part * sigmoid_gate
-    hidden = silu_gate * up_part
-    hidden_gated = (hidden * gates).astype(jnp.bfloat16)
-    combined = jnp.einsum(
-        "sk,dk->sd", hidden_gated, full_down, preferred_element_type=jnp.float32
-    ).astype(jnp.bfloat16)
-    back_hidden = jnp.dot(grad_rows, full_down, preferred_element_type=jnp.float32)
-    gate_dot = jnp.sum((hidden * back_hidden).reshape(seq_len, EXPERTS, ff_here), axis=2)
-    grad_hidden = back_hidden * gates
-    grad_gate_part = (
-        grad_hidden * up_part * sigmoid_gate * (1.0 + gate_part * (1.0 - sigmoid_gate))
-    ).astype(jnp.bfloat16)
-    grad_up_part = (grad_hidden * silu_gate).astype(jnp.bfloat16)
-    grad_gate_w = jnp.einsum(
-        "sd,sk->dk", normed_two, grad_gate_part, preferred_element_type=jnp.float32
-    ).astype(jnp.bfloat16)
-    grad_up_w = jnp.einsum(
-        "sd,sk->dk", normed_two, grad_up_part, preferred_element_type=jnp.float32
-    ).astype(jnp.bfloat16)
-    grad_down_w = jnp.einsum(
-        "sd,sk->dk", grad_rows, hidden_gated, preferred_element_type=jnp.float32
-    ).astype(jnp.bfloat16)
-    grad_two_part = after(
-        jnp.einsum("sk,dk->sd", grad_gate_part, full_gate, preferred_element_type=jnp.float32)
-        + jnp.einsum("sk,dk->sd", grad_up_part, full_up, preferred_element_type=jnp.float32),
-        grad_gate_w,
-        grad_up_w,
-        grad_down_w,
-    ).astype(jnp.bfloat16)
+    hidden_gated, grad_gate_part, grad_up_part, gate_dot = expert_parts(
+        normed_two, grad_rows, gate_values, full_experts, ff_here
+    )
+    combined, grad_two_part, grad_experts_w = expert_products(
+        hidden_gated, grad_gate_part, grad_up_part, normed_two, grad_rows, full_experts
+    )
     ffn_branch = lax.psum_scatter(
         combined, "tensor", scatter_dimension=0, tiled=True
     ).astype(jnp.float32)
@@ -684,9 +766,7 @@
         "sd,se->de", normed_two, logits_low, preferred_element_type=jnp.float32
     )
     own_logits = lax.dynamic_slice_in_dim(logits_low, tensor_rank * local_rows, local_rows)
-    sum_gate = lax.psum_scatter(grad_gate_w, "dp", scatter_dimension=0, tiled=True)
-    sum_up = lax.psum_scatter(grad_up_w, "dp", scatter_dimension=0, tiled=True)
-    sum_down = lax.psum_scatter(grad_down_w, "dp", scatter_dimension=0, tiled=True)
+    sum_experts = lax.psum_scatter(grad_experts_w, "dp", scatter_dimension=0, tiled=True)
     router_part = jnp.einsum(
         "se,de->sd", own_logits, full_router, preferred_element_type=jnp.float32
     )
@@ -711,7 +791,7 @@
         k_rot,
         value_heads,
         block_row,
-        after(log_totals, ffn_branch),
+        log_totals,
         grad_mixed.reshape(seq_len, heads_here, HEAD_DIM),
     )
     grad_query_normed = rotate_back(grad_q_rot, cosine_table, sine_table).reshape(
@@ -725,7 +805,7 @@
     dots = jnp.stack(
         [jnp.sum(query_scaled * query_normed, axis=1), jnp.sum(key_scaled * key_normed, axis=1)]
     )
-    query_dot, key_dot = small_sum(count, after(dots, sum_gate, sum_up), 7)
+    query_dot, key_dot = small_sum(count, after(dots, sum_experts), 7)
     grad_query_proj = (
         query_inv * (query_scaled - query_normed * (query_dot / model_width)[:, None])
     ).astype(jnp.bfloat16)
@@ -741,7 +821,7 @@
         "sf,df->sd", grad_qkv, w_qkv, preferred_element_type=jnp.float32
     ).astype(jnp.bfloat16)
     grad_source, grad_attn_gain = end_exchange(
-        count, grad_normed_part, grad_middle, tokens, after(attn_scale[None, :], sum_down)
+        count, grad_normed_part, grad_middle, tokens, after(attn_scale[None, :], ffn_branch)
     )
     sum_out_router = after(sum_out_router, grad_attn_gain[None])
     sum_out = sum_out_router[:, :head_cols]
@@ -750,21 +830,26 @@
     query_gain_full = lax.dynamic_update_slice_in_dim(zero_cols, grad_query_gain, col_start, 0)
     key_gain_full = lax.dynamic_update_slice_in_dim(zero_cols, grad_key_gain, col_start, 0)
     gain_stack = jnp.stack([grad_attn_gain, query_gain_full, key_gain_full, grad_ffn_gain])
-    total_rows = lax.psum(
-        gain_stack,
-        ("dp", "tensor"),
-    )
+    dp_count = lax.axis_size("dp")
+    total_rows = small_sum(count, gain_stack, 8)
+    total_rows = small_sum(dp_count, total_rows, 9, "dp")
     dp_rank = lax.axis_index("dp")
-    gain_width = model_width // (lax.axis_size("dp") * count)
+    gain_width = model_width // (dp_count * count)
     gain_sums = lax.dynamic_slice_in_dim(
         total_rows, (dp_rank * count + tensor_rank) * gain_width, gain_width, 1
     )
     sum_qkv = lax.psum_scatter(grad_qkv_w, "dp", scatter_dimension=0, tiled=True).astype(
         jnp.float32
     )
-    grad_gate = sum_gate.reshape(shard_width, EXPERTS, ff_here).transpose(1, 0, 2)
-    grad_up = sum_up.reshape(shard_width, EXPERTS, ff_here).transpose(1, 0, 2)
-    grad_down = sum_down.reshape(shard_width, EXPERTS, ff_here).transpose(1, 2, 0)
+    grad_gate, grad_up, grad_down = (
+        sum_experts[:, k * hidden_cols : (k + 1) * hidden_cols].reshape(
+            shard_width, EXPERTS, ff_here
+        )
+        for k in range(3)
+    )
+    grad_gate = grad_gate.transpose(1, 0, 2)
+    grad_up = grad_up.transpose(1, 0, 2)
+    grad_down = grad_down.transpose(1, 2, 0)
     return (
         output,
         grad_source,

time: 951 us -> 808 us (0.85)
  matrix products: 233 us -> 90 us
  Pallas kernels: 414 us -> 529 us
  blocking collectives: 52.9 us -> 10.6 us
  waiting for transfers between devices: 39.1 us -> 0.88 us
  local copies, waits for them, and re-layouts: 107 us -> 80.9 us
    dot_general x9 -> x0, matrix products: 138 us -> none  [the longest x1 26.5 us: local(): jnp.dot(grad_rows, full_down, preferred_element_type=jnp.float32)]
    pallas_call x0 -> x2, Pallas kernels: none -> 101 us  [the longest x1 61.7 us: expert_products(): pl.pallas_call(product_kernel, grid=(width // tile,), out_shape=(flat, fl...]
    psum x1 -> x0, blocking collectives: 42.4 us -> none  [local(): total_rows = lax.psum(gain_stack, ('dp', 'tensor'))]
    all_gather x1, waiting for transfers between devices: 38.1 us -> 0.01 us  [local(): lax.all_gather(after(cotangent, normed), 'tensor', axis=0, tiled=True)]
    unnamed x142 -> x105, local copies, waits for them, and re-layouts: 36.7 us -> 16.6 us
    pallas_call x3 -> x5, Pallas kernels: 24.7 us -> 38.6 us  [small_sum(): pl.pallas_call(kernel, out_shape=jax.ShapeDtypeStruct(values.shape, jnp.f...]
  transfers between devices with their start and end apart: 12 -> 8, of which waited for: 1 -> 0; matrix products, arithmetic and copies ran while one was open for 37% -> 27% of each run, Pallas kernels for 44% -> 53%
where the time goes in v4:
time: 808 us; the launch traced here: 802 us
  Pallas kernels  529 us (65%)
  matrix products  90 us (11%)
  local copies, waits for them, and re-layouts  80.9 us (10%)
  other arithmetic  69.8 us (9%)
  between operations  18.7 us (2%)
  blocking collectives  10.6 us (1%)
    pallas_call x4, Pallas kernels, line_exchange(): pl.pallas_call(kernel, out_shape=tuple(shapes), in_specs=[pl.BlockSpec(me...  390 us
    pallas_call x1, Pallas kernels, expert_products(): pl.pallas_call(product_kernel, grid=(width // tile,), out_shape=(flat, fl...  61.7 us
    pallas_call x1, Pallas kernels, expert_parts(): pl.pallas_call(expert_kernel, grid=(EXPERTS,), out_shape=(part, part, par...  39.5 us
    pallas_call x5, Pallas kernels, small_sum(): pl.pallas_call(kernel, out_shape=jax.ShapeDtypeStruct(values.shape, jnp.f...  38.6 us
    unnamed x105, local copies, waits for them, and re-layouts  16.6 us
  transfers between devices with their start and end apart: 8, of which 0 were waited for; matrix products, arithmetic and copies ran while one was open for 27% of the time, Pallas kernels for 53%

profile of v4, /device:TPU:0, one launch (start us, length us, event | category | flops | bytes accessed | tf_op | source)
XLA Modules:
  0.0 801.7 jit_solution(4837296791182792367)
XLA Ops:
  7.3 2.0 pad_maximum_fusion.3
  10.4 10.6 %all_gather.15 = bf16[2048,12]{0,1:T(8,128)(2,1)S(1)} all-gather(bf16[256,12]{0,1:T(8,128)(2,1)S(1)} %concatenate.46), channel_id=1, replica_groups=mesh['dp'=8,'tensor'=4] {'dp'}, dimensions={0}, use_global_device_ids=true | all-gather | bytes 55296 | tf_op jit(solution)/shard_map/all_gather | solution.py:686
  21.6 77.9 %shard_map.263 = bf16[4,16,16,2048]{3,2,1,0:T(8,128)(2,1)} custom-call(bf16[16,16,2048]{2,1,0:T(8,128)(2,1)} %bitcast.267, f32[1,2048]{1,0:T(1,128)} %get-tuple-element.301.refs_1_), custom_call_target="tpu_custom_call" | custom-call | bytes 188743680 | tf_op jit(solution)/shard_map/pallas_call | solution.py:361
  104.7 10.1 %fusion.69 = f32[1024,1536]{1,0:T(8,128)S(1)} fusion(bf16[1024,2048]{1,0:T(8,128)(2,1)} %bitcast.277, bf16[2048,1536]{1,0:T(8,128)(2,1)} %all-gather.5.cloned.1.call-done), kind=kOutput, calls=%fused_computation.170 | convolution fusion | flops 6442450944 | bytes 16777216 | tf_op jit(solution)/shard_map/dot_general | solution.py:716
  114.8 2.7 copy-done.6
  118.4 7.9 shard_map.264
  128.2 2.0 maximum_add_fusion
  131.8 2.3 reduce-window.6
  134.6 4.0 multiply_cosine_fusion
  139.8 1.9 fusion.42
  142.3 4.2 multiply_bitcast_fusion
  146.5 1.8 copy.89
  150.0 2.9 slice.223
  153.1 1.9 concatenate.50
  155.0 1.9 concatenate.49
  156.8 3.1 copy.56
  160.0 3.8 fusion.35
  163.7 2.5 copy.62
  166.3 3.1 copy.140
  170.8 3.0 slice_negate_fusion.2
  174.6 16.8 %while.27 = (s32[]{:T(128)}, bf16[2,512,512]{2,1,0:T(8,128)(2,1)}, f32[2,4,512]{2,1,0:T(4,128)S(1)}, s32[1,1024]{1,0:T(1,128)S(1)}, s32[2,512]{1,0:T(2,128)S(1)}...) while((s32[]{:T(128)}, bf16[2,512,512]{2,1,0:T(8,128)(2,1)}, ...), condition=%wide.region_5.6_spmd, body=%wide.region_2.5_spmd.sunk | while | flops 1097332736 | bytes 36776080 | solution.py:85
  177.1 2.5 exponential_reduce_fusion.2
  179.6 2.6 fusion.109
  185.3 2.5 exponential_reduce_fusion.2
  187.8 2.6 fusion.109
  191.4 7.1 convolution_convert_fusion.2
  198.6 115.6 %shard_map.265 = (bf16[4,16,16,2048]{3,2,1,0:T(8,128)(2,1)}, f32[16,16,2048]{2,1,0:T(8,128)}) custom-call(bf16[4,16,16,2048]{3,2,1,0:T(8,128)(2,1)} %bitcast.279, bf16[16,16,2048]{2,1,0:T(8,128)(2,1)} %bitcast.268, f32[1,2048]{1,0:T(1,128)} %get-tuple-element.298.refs_2_.refs_4_), custom_call_target="tpu_custom_call" | custom-call | bytes 251658240 | tf_op jit(solution)/shard_map/pallas_call | solution.py:361
  314.2 3.4 fusion.68
  318.6 39.5 %shard_map.266 = (bf16[1024,2048]{1,0:T(8,128)(2,1)}, bf16[1024,2048]{1,0:T(8,128)(2,1)}, bf16[1024,2048]{1,0:T(8,128)(2,1)}, f32[1024,8]{1,0:T(8,128)}) custom-call(bf16[1024,2048]{1,0:T(8,128)(2,1)} %bitcast.262, bf16[1024,2048]{1,0:T(8,128)(2,1)} %all-gather.9.cloned.1.call-done.c_ref, f32[1024,8]{1,0:T(8,128)} %copy.68.gates_ref, ...), custom_call_target="tpu_custom_call" | custom-call | flops 25769803776 | bytes 25165824 | tf_op jit(solution)/shard_map/pallas_call | solution.py:583
  358.1 61.7 %shard_map.267 = (bf16[1024,2048]{1,0:T(8,128)(2,1)}, bf16[1024,2048]{1,0:T(8,128)(2,1)}, bf16[2048,6144]{1,0:T(8,128)(2,1)}) custom-call(bf16[1024,2048]{1,0:T(8,128)(2,1)} %get-tuple-element.133.hg_ref, bf16[1024,2048]{1,0:T(8,128)(2,1)} %get-tuple-element.134.dg_ref, bf16[1024,2048]{1,0:T(8,128)(2,1)} %get-tuple-element.135.du_ref, ...), custom_call_target="tpu_custom_call" | custom-call | flops 51539607552 | bytes 50331648 | tf_op jit(solution)/shard_map/pallas_call | solution.py:639
  420.0 2.7 copy_bitcast_fusion.4
  424.6 7.1 shard_map.268
  435.1 118.9 %shard_map.269 = (bf16[4,16,16,2048]{3,2,1,0:T(8,128)(2,1)}, f32[16,16,2048]{2,1,0:T(8,128)}, f32[1,2048]{1,0:T(1,128)}) custom-call(bf16[4,16,16,2048]{3,2,1,0:T(8,128)(2,1)} %bitcast.284, f32[16,16,2048]{2,1,0:T(8,128)} %bitcast.271, f32[16,16,2048]{2,1,0:T(8,128)} %get-tuple-element.131.refs_2_, bf16[16,16,2048]{2,1,0:T(8,128)(2,1)} %bitcast.285, ...), custom_call_target="tpu_custom_call" | custom-call | bytes 251658240 | tf_op jit(solution)/shard_map/pallas_call | solution.py:361
  554.0 5.7 convolution_convert_fusion.5
  559.7 2.2 reshape_reshape.3
  562.0 46.0 %while.28 = (s32[]{:T(128)}, f32[1024,4,128]{0,2,1:T(8,128)S(1)}, f32[1024,4,128]{0,2,1:T(8,128)}, f32[2,512,4,128]{3,1,2,0:T(8,128)}, bf16[2,512,4,128]{3,1,2,0...) while((s32[]{:T(128)}, f32[1024,4,128]{0,2,1:T(8,128)S(1)}, ...), condition=%wide.region_14.15_spmd.clone, body=%wide.region_12.14_spmd.clone.sunk | while | flops 2719217664 | bytes 215026224 | solution.py:129
  562.0 2.4 fusion.118
  566.4 3.5 multiply_reduce_fusion.7
  569.9 3.7 multiply_convert_fusion.4
  573.6 3.9 bitcast_add_fusion.5
  579.5 2.7 bitcast_add_fusion.6
  584.9 2.4 fusion.118
  589.3 3.5 multiply_reduce_fusion.7
  592.8 3.7 multiply_convert_fusion.4
  596.6 3.8 bitcast_add_fusion.5
  602.4 2.7 bitcast_add_fusion.6
  607.9 4.4 copy.73
  616.2 2.0 copy.77
  618.2 3.0 convolution_convert_fusion.4
  621.9 2.5 convolution_convert_fusion.3
  624.4 1.8 fusion.31
  628.0 1.9 bitcast_multiply_fusion.3
  635.2 3.9 multiply_reduce_fusion.1
  641.6 7.2 shard_map.270
  649.6 5.0 multiply_convert_fusion.2
  655.9 9.5 %convolution_convert_fusion = bf16[2048,1536]{1,0:T(8,128)(2,1)} fusion(bf16[1024,2048]{1,0:T(8,128)(2,1)S(1)} %bitcast.278, bf16[1024,512]{1,0:T(8,128)(2,1)S(1)} %copy-done.39, bf16[1024,512]{1,0:T(8,128)(2,1)S(1)} %get-tuple-element.279, bf16[1024,512]{1,0:T(8,128)(2,1)S(1)} %get-tuple-element.278), kind=kOutput, calls=%fused_computation.46 | convolution fusion | flops 6455033856 | bytes 13631488 | tf_op jit(solution)/shard_map/sd,sf->df/dot_general | solution.py:817
  668.8 2.9 fusion.39
  671.7 11.0 %convolution_convert_fusion.1 = bf16[1024,2048]{1,0:T(8,128)(2,1)} fusion(bf16[2048,1536]{1,0:T(8,128)(2,1)} %all-gather.5.cloned.1.call-done, bf16[1024,512]{1,0:T(8,128)(2,1)S(1)} %copy-done.40, bf16[1024,512]{1,0:T(8,128)(2,1)S(1)} %copy-done.35, bf16[1024,512]{1,0:T(8,128)(2,1)S(1)} %copy-done.33), kind=kOutput, calls=%fused_computation.49 | convolution fusion | flops 6453985280 | bytes 13631488 | tf_op jit(solution)/shard_map/sf,df->sd/dot_general | solution.py:820
  682.7 77.3 %shard_map.271 = (f32[16,16,2048]{2,1,0:T(8,128)}, f32[1,2048]{1,0:T(1,128)}) custom-call(bf16[4,16,16,2048]{3,2,1,0:T(8,128)(2,1)} %bitcast.283, f32[16,16,2048]{2,1,0:T(8,128)} %get-tuple-element.145.refs_1_, bf16[16,16,2048]{2,1,0:T(8,128)(2,1)} %bitcast.269, f32[1,2048]{1,0:T(1,128)} %broadcast_add_fusion.1.refs_3_), custom_call_target="tpu_custom_call" | custom-call | bytes 188743680 | tf_op jit(solution)/shard_map/pallas_call | solution.py:361
  762.6 7.2 shard_map.272.in_ref
  769.7 9.2 %shard_map.273 = f32[4,2048]{1,0:T(4,128)} custom-call(f32[4,2048]{1,0:T(4,128)} %shard_map.272.in_ref), custom_call_target="tpu_custom_call" | custom-call | tf_op jit(solution)/shard_map/pallas_call | solution.py:408
  781.2 2.7 slice_convert_fusion.1
  786.9 1.8 copy.88
  790.8 2.3 fusion.65
  (275 shorter events, 71.1 us)
Async XLA Ops:
  7.2 3.0 copy-start.59
  7.2 3.0 copy-start.60
  7.2 3.0 copy-start.61
  7.2 3.0 copy-start.62
  7.2 3.0 copy-start.55
  7.2 97.5 %all-gather.5.cloned.1.call-start = ((), (), s32[]{:S(2)}) async-start(), calls=%async_computation.4 | async-start | bytes 7077888 | tf_op jit(solution)/shard_map/all_gather | solution.py:687
  9.3 182.1 %all-gather.7.cloned.1.call-start = ((), (), s32[]{:S(2)}) async-start(), calls=%async_computation.5 | async-start | bytes 2359296 | tf_op jit(solution)/shard_map/all_gather | solution.py:690
  10.1 308.5 %all-gather.9.cloned.1.call-start = ((), (), s32[]{:S(2)}) async-start(), calls=%async_computation.6 | async-start | bytes 5242880 | tf_op jit(solution)/shard_map/all_gather | solution.py:712
  21.6 79.9 %copy-start.27 = (bf16[256,2048]{1,0:T(8,128)(2,1)S(1)}, bf16[256,2048]{1,0:T(8,128)(2,1)}, u32[]{:S(2)}) copy-start(bf16[256,2048]{1,0:T(8,128)(2,1)} %param.21) | copy-start | bytes 3145732
  99.5 3.1 copy-start.36
  102.5 216.1 %all-gather.11.cloned.1.call-start = ((), (), s32[]{:S(2)}) async-start(), calls=%async_computation.7 | async-start | bytes 28311552 | tf_op jit(solution)/shard_map/all_gather | solution.py:724
  130.2 508.9 %reduce-scatter.7.cloned.1.call-start = ((), (), s32[]{:S(2)}) async-start(), calls=%async_computation.9 | async-start | bytes 28311552 | tf_op jit(solution)/shard_map/reduce_scatter | solution.py:769
  134.5 7.8 copy-start.48
  134.5 7.8 copy-start.50
  138.6 3.7 copy-start.52
  142.1 31.7 %copy-start.14 = (f32[1024,128]{1,0:T(8,128)}, f32[1024,128]{1,0:T(8,128)S(1)}, u32[]{:S(2)}) copy-start(f32[1024,128]{1,0:T(8,128)S(1)} %get-tuple-element.322) | copy-start | bytes 1572868
  142.1 31.7 %copy-start.23 = (f32[1024,128]{1,0:T(8,128)}, f32[1024,128]{1,0:T(8,128)S(1)}, u32[]{:S(2)}) copy-start(f32[1024,128]{1,0:T(8,128)S(1)} %get-tuple-element.323) | copy-start | bytes 1572868
  142.3 4.2 copy-start.44
  142.3 4.2 copy-start.46
  150.0 2.9 copy-start.20
  166.3 3.1 copy-start.26
  170.8 3.1 copy-start.11
  191.4 7.1 copy-start.5
  419.8 245.7 %reduce-scatter.5.cloned.1.call-start = ((), (), s32[]{:S(2)}) async-start(), calls=%async_computation.8 | async-start | bytes 5242880 | tf_op jit(solution)/shard_map/reduce_scatter | solution.py:756
  435.1 118.9 %copy-start.57 = (bf16[2048,512]{0,1:T(8,128)(2,1)S(1)}, bf16[2048,512]{0,1:T(8,128)(2,1)}, u32[]{:S(2)}) copy-start(bf16[2048,512]{0,1:T(8,128)(2,1)} %all-gather.7.cloned.1.call-done) | copy-start | bytes 6291460
  561.9 217.6 %reduce-scatter.11.cloned.1.call-start = ((), (), s32[]{:S(2)}) async-start(), calls=%async_computation.11 | async-start | bytes 2949120 | tf_op jit(solution)/shard_map/reduce_scatter | solution.py:780
  562.0 2.9 copy-start.16
  564.4 5.5 copy-start
  564.8 5.1 copy-start.3
  566.4 3.5 copy-start.7
  573.6 4.9 copy-start.1
  573.6 5.0 copy-start.4
  573.6 5.1 copy-start.8
  573.6 5.8 copy-start.28
  579.5 2.9 copy-start.17
  584.9 2.8 copy-start.16
  587.3 5.5 copy-start
  587.7 5.1 copy-start.3
  589.3 3.5 copy-start.7
  596.6 4.9 copy-start.1
  596.6 4.9 copy-start.4
  596.6 5.1 copy-start.8
  596.6 5.8 copy-start.28
  602.4 2.7 copy-start.2
  602.4 3.0 copy-start.17
  607.9 4.4 copy-start.19
  618.2 3.5 copy-start.56
  618.2 3.7 copy-start.58
  626.3 164.5 %reduce-scatter.9.cloned.1.call-start = ((), (), s32[]{:S(2)}) async-start(), calls=%async_computation.10 | async-start | bytes 7077888 | tf_op jit(solution)/shard_map/reduce_scatter | solution.py:841
  629.8 4.2 slice-start
  630.6 3.5 slice-start.1
  632.0 3.3 copy-start.22
  632.0 3.3 copy-start.45
  632.0 3.3 copy-start.47
  632.0 3.2 copy-start.49
  632.0 3.2 copy-start.51
  649.5 6.3 copy-start.25
  649.6 6.3 copy-start.39
  665.3 3.5 copy-start.21
  668.8 2.9 copy-start.33
  668.8 2.9 copy-start.35
  668.8 2.9 copy-start.40
  682.7 78.5 %copy-start.54 = (f32[1,2048]{1,0:T(1,128)S(1)}, f32[1,2048]{1,0:T(1,128)}, u32[]{:S(2)}) copy-start(f32[1,2048]{1,0:T(1,128)} %get-tuple-element.148) | copy-start | bytes 24580
  790.0 3.1 copy-start.31
  (23 other events, 38.2 us)
Sparse Core Ops, SparseCore 0:
  10.5 48.1 all-gather.4
  60.5 28.0 all-gather.6
  102.7 79.9 all-gather.8
  184.4 123.5 all-gather.10
  419.9 155.2 reduce-scatter.6
  577.3 77.2 reduce-scatter.4
  658.0 43.9 reduce-scatter.10
  705.4 61.8 reduce-scatter.8

commit v5 on v4

--- a/solution.py
+++ b/solution.py
@@ -2,6 +2,7 @@
 
 import jax
 import jax.numpy as jnp
+import numpy as np
 from jax import lax
 from jax.experimental import pallas as pl
 from jax.experimental.pallas import tpu as pltpu
@@ -10,7 +11,7 @@
 HEAD_DIM = 128
 EXPERTS = 8
 TOPK = 2
-QROWS = 512
+BLOCK = 256
 CAP = 320
 
 
@@ -24,112 +25,219 @@
     return source * lax.rsqrt(jnp.mean(source * source, axis=-1, keepdims=True) + EPSILON)
 
 
-def norm_back(source, gain_vec, grad_out):
-    inverse = lax.rsqrt(jnp.mean(source * source, axis=-1, keepdims=True) + EPSILON)
-    normed = source * inverse
-    grad_gain = jnp.sum(grad_out * normed, axis=0)
-    scaled = grad_out * gain_vec
-    grad_in = inverse * (scaled - normed * jnp.mean(scaled * normed, axis=-1, keepdims=True))
-    return (grad_in, grad_gain)
-
-
-def rope_tables(seq_len, head_dim):
-    half_dim = head_dim // 2
-    frequency = jnp.exp(
-        -math.log(10000.0) * 2.0 * jnp.arange(half_dim, dtype=jnp.float32) / head_dim
-    )
-    angles = jnp.arange(seq_len, dtype=jnp.float32)[:, None] * frequency[None, :]
-    return (
-        jnp.concatenate([jnp.cos(angles)] * 2, axis=1),
-        jnp.concatenate([jnp.sin(angles)] * 2, axis=1),
-    )
-
-
-def rotate(heads_in, cosine_table, sine_table):
-    half_dim = heads_in.shape[-1] // 2
-    turned = jnp.concatenate([-heads_in[..., half_dim:], heads_in[..., :half_dim]], axis=-1)
-    return heads_in * cosine_table[:, None, :] + turned * sine_table[:, None, :]
-
-
-def rotate_back(grad_in, cosine_table, sine_table):
-    half_dim = grad_in.shape[-1] // 2
-    sined = grad_in * sine_table[:, None, :]
-    turned = jnp.concatenate([sined[..., half_dim:], -sined[..., :half_dim]], axis=-1)
-    return grad_in * cosine_table[:, None, :] + turned
-
-
-def attend(q_rot, k_rot, value_heads, block_row):
-    seq_len, heads_here, head_dim = q_rot.shape
-    blocks = seq_len // QROWS
-    score_scale = head_dim ** (-0.5)
-    q_blocks = q_rot.reshape(blocks, QROWS, heads_here, head_dim)
-    id_blocks = block_row.reshape(blocks, QROWS)
-
-    def per_block(block_item):
-        q_block, id_block = block_item
-        scores = (
-            jnp.einsum("qhd,khd->hqk", q_block, k_rot, preferred_element_type=jnp.float32)
-            * score_scale
+def rope_constants(seq_len):
+    half_dim = HEAD_DIM // 2
+    frequency = np.exp(-math.log(10000.0) * 2.0 * np.arange(half_dim) / HEAD_DIM)
+    angles = np.arange(seq_len)[:, None] * frequency[None, :]
+    cosine = np.concatenate([np.cos(angles)] * 2, axis=1).astype(np.float32)
+    sine = np.concatenate([-np.sin(angles), np.sin(angles)], axis=1).astype(np.float32)
+    return jnp.asarray(cosine), jnp.asarray(sine)
+
+
+def masked_scores(q_rows, k_rows, ids_col, ids_row):
+    scores = lax.dot_general(
+        q_rows, k_rows, (((1,), (1,)), ((), ())), preferred_element_type=jnp.float32
+    ) * (HEAD_DIM ** (-0.5))
+    return jnp.where(ids_row <= ids_col, scores, MASKED)
+
+
+def key_limit(start, seq_len):
+    return min(seq_len, start + 2 * BLOCK)
+
+
+def attend_kernel(
+    q_ref, k_ref, v_ref, inv_ref, qg_ref, kg_ref, cos_ref, sin_ref, col_ref, row_ref,
+    q_out, k_out, v_out, mixed_out, log_out,
+):
+    head = pl.program_id(0)
+    seq_len = q_ref.shape[0]
+    cosine, sine = cos_ref[...], sin_ref[...]
+
+    def turn(rows):
+        return (rows * cosine + pltpu.roll(rows, HEAD_DIM // 2, 1) * sine).astype(jnp.bfloat16)
+
+    q_out[...] = turn(q_ref[...] * inv_ref[:, 0:1] * qg_ref[...])
+    k_out[...] = turn(k_ref[...] * inv_ref[:, 1:2] * kg_ref[...])
+    v_out[...] = v_ref[...].astype(jnp.bfloat16)
+
+    @pl.when(head == 0)
+    def _():
+        log_out[...] = jnp.zeros_like(log_out)
+
+    for start in range(0, seq_len, BLOCK):
+        rows = pl.ds(start, BLOCK)
+        keys = pl.ds(0, key_limit(start, seq_len))
+        scores = masked_scores(q_out[rows, :], k_out[keys, :], col_ref[rows, :], row_ref[:, keys])
+        top = jnp.max(scores, axis=-1, keepdims=True)
+        powers = jnp.exp(scores - top)
+        total = jnp.sum(powers, axis=-1, keepdims=True)
+        weights = (powers * (1.0 / total)).astype(jnp.bfloat16)
+        mixed_out[rows, :] = jnp.dot(
+            weights, v_out[keys, :], preferred_element_type=jnp.float32
+        ).astype(jnp.bfloat16)
+        lane = lax.broadcasted_iota(jnp.int32, (BLOCK, log_out.shape[1]), 1)
+        log_out[rows, :] = log_out[rows, :] + jnp.where(
+            lane == head, top + jnp.log(total), 0.0
         )
-        allowed = block_row[None, None, :] <= id_block[None, :, None]
-        scores = jnp.where(allowed, scores, MASKED)
-        row_top = jnp.max(scores, axis=-1, keepdims=True)
-        row_sum = jnp.sum(jnp.exp(scores - row_top), axis=-1, keepdims=True)
-        log_total = row_top + jnp.log(row_sum)
-        weights_low = jnp.exp(scores - log_total).astype(jnp.bfloat16)
-        mixed_block = jnp.einsum(
-            "hqk,khd->qhd", weights_low, value_heads, preferred_element_type=jnp.float32
+
+
+def attend(projected, inverses, q_gain_row, k_gain_row, tables, ids_col, ids_row):
+    seq_len = projected.shape[0]
+    heads = projected.shape[1] // (3 * HEAD_DIM)
+    cols = heads * HEAD_DIM
+    whole = pl.BlockSpec(memory_space=pltpu.VMEM)
+    gain = pl.BlockSpec((1, HEAD_DIM), lambda h: (0, h))
+    column = pl.BlockSpec((seq_len, HEAD_DIM), lambda h: (0, h))
+    flat = jax.ShapeDtypeStruct((seq_len, cols), jnp.bfloat16)
+    return pl.pallas_call(
+        attend_kernel,
+        grid=(heads,),
+        out_shape=(flat, flat, flat, flat, jax.ShapeDtypeStruct((seq_len, heads), jnp.float32)),
+        in_specs=[
+            column,
+            pl.BlockSpec((seq_len, HEAD_DIM), lambda h: (0, heads + h)),
+            pl.BlockSpec((seq_len, HEAD_DIM), lambda h: (0, 2 * heads + h)),
+            whole,
+            gain,
+            gain,
+            whole,
+            whole,
+            whole,
+            whole,
+        ],
+        out_specs=(
+            column,
+            column,
+            column,
+            column,
+            pl.BlockSpec((seq_len, heads), lambda h: (0, 0)),
+        ),
+        compiler_params=pltpu.CompilerParams(vmem_limit_bytes=48 * 1024 * 1024),
+        cost_estimate=pl.CostEstimate(
+            flops=20 * seq_len * seq_len * cols, bytes_accessed=projected.size * 4, transcendentals=0
+        ),
+    )(
+        projected, projected, projected, inverses, q_gain_row, k_gain_row, tables[0], tables[1],
+        ids_col, ids_row,
+    )
+
+
+def attend_back_kernel(
+    q_ref, k_ref, v_ref, g_ref, log_ref, qp_ref, kp_ref, inv_ref, qg_ref, kg_ref, cos_ref, sin_ref,
+    col_ref, row_ref, gq_out, gk_out, gv_out, dot_out, qgain_out, kgain_out, dq_acc, dk_acc, dv_acc,
+):
+    head = pl.program_id(0)
+    seq_len = q_ref.shape[0]
+    scale = HEAD_DIM ** (-0.5)
+    dk_acc[...] = jnp.zeros_like(dk_acc)
+    dv_acc[...] = jnp.zeros_like(dv_acc)
+
+    def down(left, right):
+        return lax.dot_general(
+            left, right, (((0,), (0,)), ((), ())), preferred_element_type=jnp.float32
         )
-        return (mixed_block.reshape(QROWS, heads_here * head_dim), log_total[..., 0])
-
-    mixed_blocks, log_totals = lax.map(per_block, (q_blocks, id_blocks))
-    return (mixed_blocks.reshape(seq_len, heads_here * head_dim), log_totals)
-
-
-def attend_back(q_rot, k_rot, value_heads, block_row, log_totals, grad_mixed):
-    seq_len, heads_here, head_dim = q_rot.shape
-    blocks = seq_len // QROWS
-    score_scale = head_dim ** (-0.5)
-    q_blocks = q_rot.reshape(blocks, QROWS, heads_here, head_dim)
-    g_blocks = grad_mixed.reshape(blocks, QROWS, heads_here, head_dim)
-    id_blocks = block_row.reshape(blocks, QROWS)
-
-    def back_block(running, block_item):
-        q_block, g_block, id_block, log_block = block_item
-        scores = (
-            jnp.einsum("qhd,khd->hqk", q_block, k_rot, preferred_element_type=jnp.float32)
-            * score_scale
+
+    for start in range(0, seq_len, BLOCK):
+        rows = pl.ds(start, BLOCK)
+        keys = pl.ds(0, key_limit(start, seq_len))
+        scores = masked_scores(q_ref[rows, :], k_ref[keys, :], col_ref[rows, :], row_ref[:, keys])
+        lane = lax.broadcasted_iota(jnp.int32, (BLOCK, log_ref.shape[1]), 1)
+        log_total = jnp.sum(jnp.where(lane == head, log_ref[rows, :], 0.0), axis=1, keepdims=True)
+        weights = jnp.exp(scores - log_total)
+        grad_weights = lax.dot_general(
+            g_ref[rows, :],
+            v_ref[keys, :],
+            (((1,), (1,)), ((), ())),
+            preferred_element_type=jnp.float32,
         )
-        allowed = block_row[None, None, :] <= id_block[None, :, None]
-        scores = jnp.where(allowed, scores, MASKED)
-        weights = jnp.exp(scores - log_block[..., None])
-        weights_low = weights.astype(jnp.bfloat16)
-        grad_weights = jnp.einsum(
-            "qhd,khd->hqk", g_block, value_heads, preferred_element_type=jnp.float32
+        grad_scores = (
+            weights * (grad_weights - jnp.sum(weights * grad_weights, axis=-1, keepdims=True))
+        ).astype(jnp.bfloat16)
+        dq_acc[rows, :] = (
+            jnp.dot(grad_scores, k_ref[keys, :], preferred_element_type=jnp.float32) * scale
         )
-        grad_scores = weights * (
-            grad_weights - jnp.sum(weights * grad_weights, axis=-1, keepdims=True)
+        dk_acc[keys, :] = dk_acc[keys, :] + down(grad_scores, q_ref[rows, :]) * scale
+        dv_acc[keys, :] = dv_acc[keys, :] + down(weights.astype(jnp.bfloat16), g_ref[rows, :])
+    gv_out[...] = dv_acc[...].astype(jnp.bfloat16)
+    cosine, sine = cos_ref[...], sin_ref[...]
+
+    @pl.when(head == 0)
+    def _():
+        dot_out[...] = jnp.zeros_like(dot_out)
+
+    def turn_back(rows):
+        return rows * cosine - pltpu.roll(rows, HEAD_DIM // 2, 1) * sine
+
+    lane = lax.broadcasted_iota(jnp.int32, dot_out.shape, 1)
+    for which, acc, proj, gain, out, gain_out in (
+        (0, dq_acc, qp_ref, qg_ref, gq_out, qgain_out),
+        (1, dk_acc, kp_ref, kg_ref, gk_out, kgain_out),
+    ):
+        grad = turn_back(acc[...])
+        normed = proj[...] * inv_ref[:, which : which + 1]
+        gain_out[...] = jnp.sum(grad * normed, axis=0, keepdims=True)
+        scaled = grad * gain[...]
+        out[...] = scaled
+        dot_out[...] = dot_out[...] + jnp.where(
+            lane == which, jnp.sum(scaled * normed, axis=1, keepdims=True), 0.0
         )
-        grad_low = grad_scores.astype(jnp.bfloat16)
-        grad_query = (
-            jnp.einsum("hqk,khd->qhd", grad_low, k_rot, preferred_element_type=jnp.float32)
-            * score_scale
-        )
-        grad_key = (
-            running[0]
-            + jnp.einsum("hqk,qhd->khd", grad_low, q_block, preferred_element_type=jnp.float32)
-            * score_scale
-        )
-        grad_value = running[1] + jnp.einsum(
-            "hqk,qhd->khd", weights_low, g_block, preferred_element_type=jnp.float32
-        )
-        return ((grad_key, grad_value), grad_query)
-
-    zero_heads = jnp.zeros(k_rot.shape, jnp.float32)
-    sums_out, grad_query = lax.scan(
-        back_block, (zero_heads, zero_heads), (q_blocks, g_blocks, id_blocks, log_totals)
-    )
-    return (grad_query.reshape(seq_len, heads_here, head_dim), sums_out[0], sums_out[1])
+
+
+def attend_back(
+    q_rot, k_rot, value_low, grad_mixed, log_totals, projected, inverses, q_gain_row, k_gain_row,
+    tables, ids_col, ids_row,
+):
+    seq_len, cols = q_rot.shape
+    heads = cols // HEAD_DIM
+    whole = pl.BlockSpec(memory_space=pltpu.VMEM)
+    gain = pl.BlockSpec((1, HEAD_DIM), lambda h: (0, h))
+    column = pl.BlockSpec((seq_len, HEAD_DIM), lambda h: (0, h))
+    wide = jax.ShapeDtypeStruct((seq_len, cols), jnp.float32)
+    gain_shape = jax.ShapeDtypeStruct((1, cols), jnp.float32)
+    return pl.pallas_call(
+        attend_back_kernel,
+        grid=(heads,),
+        out_shape=(
+            wide,
+            wide,
+            jax.ShapeDtypeStruct((seq_len, cols), jnp.bfloat16),
+            jax.ShapeDtypeStruct((seq_len, 2), jnp.float32),
+            gain_shape,
+            gain_shape,
+        ),
+        in_specs=[
+            column,
+            column,
+            column,
+            column,
+            whole,
+            column,
+            pl.BlockSpec((seq_len, HEAD_DIM), lambda h: (0, heads + h)),
+            whole,
+            gain,
+            gain,
+            whole,
+            whole,
+            whole,
+            whole,
+        ],
+        out_specs=(
+            column,
+            column,
+            column,
+            pl.BlockSpec((seq_len, 2), lambda h: (0, 0)),
+            gain,
+            gain,
+        ),
+        scratch_shapes=[pltpu.VMEM((seq_len, HEAD_DIM), jnp.float32)] * 3,
+        compiler_params=pltpu.CompilerParams(vmem_limit_bytes=48 * 1024 * 1024),
+        cost_estimate=pl.CostEstimate(
+            flops=60 * seq_len * seq_len * cols, bytes_accessed=projected.size * 4, transcendentals=0
+        ),
+    )(
+        q_rot, k_rot, value_low, grad_mixed, log_totals, projected, projected, inverses,
+        q_gain_row, k_gain_row, tables[0], tables[1], ids_col, ids_row,
+    )
 
 
 def kept_mask(route_rows):
@@ -605,7 +713,7 @@
     )(rows_in, rows_grad, gates, weights, weights, weights)
 
 
-def product_kernel(hg_ref, dg_ref, du_ref, x_ref, c_ref, w_ref, out_ref, dx_ref, dw_ref):
+def product_kernel(hg_ref, dg_ref, du_ref, x_ref, c_ref, w_ref, dx_ref, dw_ref):
     cols = hg_ref.shape[1]
 
     def times_weight(left, which):
@@ -619,7 +727,6 @@
             rows, grad, (((0,), (0,)), ((), ())), preferred_element_type=jnp.float32
         ).astype(jnp.bfloat16)
 
-    out_ref[...] = times_weight(hg_ref[...], 2).astype(jnp.bfloat16)
     dx_ref[...] = (times_weight(dg_ref[...], 0) + times_weight(du_ref[...], 1)).astype(
         jnp.bfloat16
     )
@@ -639,14 +746,40 @@
     return pl.pallas_call(
         product_kernel,
         grid=(width // tile,),
-        out_shape=(flat, flat, jax.ShapeDtypeStruct((width, 3 * cols), jnp.bfloat16)),
+        out_shape=(flat, jax.ShapeDtypeStruct((width, 3 * cols), jnp.bfloat16)),
         in_specs=[whole, whole, whole, column, column, row],
-        out_specs=(column, column, row),
+        out_specs=(column, row),
         compiler_params=pltpu.CompilerParams(vmem_limit_bytes=56 * 1024 * 1024),
         cost_estimate=pl.CostEstimate(
-            flops=12 * seq_len * width * cols, bytes_accessed=weights.size * 4, transcendentals=0
+            flops=10 * seq_len * width * cols, bytes_accessed=weights.size * 4, transcendentals=0
         ),
     )(hg, dg, du, rows_in, rows_grad, weights)
+
+
+def output_kernel(hg_ref, w_ref, out_ref):
+    out_ref[...] = lax.dot_general(
+        hg_ref[...], w_ref[...], (((1,), (1,)), ((), ())), preferred_element_type=jnp.float32
+    ).astype(jnp.bfloat16)
+
+
+def expert_output(hg, weights):
+    seq_len, cols = hg.shape
+    width = weights.shape[0]
+    tile = 256
+    return pl.pallas_call(
+        output_kernel,
+        grid=(width // tile,),
+        out_shape=jax.ShapeDtypeStruct((seq_len, width), jnp.bfloat16),
+        in_specs=[
+            pl.BlockSpec(memory_space=pltpu.VMEM),
+            pl.BlockSpec((tile, cols), lambda i: (i, 2)),
+        ],
+        out_specs=pl.BlockSpec((seq_len, tile), lambda i: (0, i)),
+        compiler_params=pltpu.CompilerParams(vmem_limit_bytes=40 * 1024 * 1024),
+        cost_estimate=pl.CostEstimate(
+            flops=2 * seq_len * width * cols, bytes_accessed=width * cols * 2, transcendentals=0
+        ),
+    )(hg, weights)
 
 
 def after(value, *others):
@@ -684,10 +817,11 @@
         [attn_gain[:, None], q_gain[:, None], k_gain[:, None], ffn_gain[:, None], w_router], axis=1
     )
     small = lax.all_gather(small, "dp", axis=0, tiled=True)
-    w_qkv = lax.all_gather(
-        jnp.concatenate([w_query, w_key, w_value], axis=1), "dp", axis=0, tiled=True
-    )
-    w_o_t = lax.all_gather(w_out.T, "dp", axis=0, tiled=True)
+    w_heads = lax.all_gather(
+        jnp.concatenate([w_query, w_key, w_value, w_out.T], axis=1), "dp", axis=0, tiled=True
+    )
+    w_qkv = w_heads[:, : 3 * head_cols]
+    w_o_t = w_heads[:, 3 * head_cols :]
     expert_local = jnp.concatenate(
         [
             w_gate.transpose(1, 0, 2).reshape(shard_width, hidden_cols),
@@ -700,7 +834,6 @@
     model_width = tokens.shape[1]
     local_rows = tokens.shape[0]
     tensor_rank = lax.axis_index("tensor")
-    heads_here = head_cols // HEAD_DIM
     col_start = tensor_rank * head_cols
     gains = small[:, :4].astype(jnp.float32).T
     attn_scale = gains[0]
@@ -711,34 +844,23 @@
     normed = start_gather(count, tokens, attn_scale[None, :])
     grad_rows = lax.all_gather(after(cotangent, normed), "tensor", axis=0, tiled=True)
     seq_len = normed.shape[0]
-    block_row = block_ids[0]
-    cosine_table, sine_table = rope_tables(seq_len, HEAD_DIM)
+    ids_row, ids_col = block_ids, block_ids.T
+    tables = rope_constants(seq_len)
     projected = jnp.dot(normed, w_qkv, preferred_element_type=jnp.float32)
     query_proj = projected[:, :head_cols]
     key_proj = projected[:, head_cols : 2 * head_cols]
-    value_low = projected[:, 2 * head_cols :].astype(jnp.bfloat16)
     squares = jnp.stack(
         [jnp.sum(query_proj * query_proj, axis=1), jnp.sum(key_proj * key_proj, axis=1)]
     )
-    query_sq, key_sq = small_sum(count, squares, 5)
+    squares = small_sum(count, squares, 5)
     full_experts = lax.all_gather(
-        after(expert_local, query_sq[None]), "dp", axis=0, tiled=True
-    )
-    query_inv = lax.rsqrt(query_sq / model_width + EPSILON)[:, None]
-    key_inv = lax.rsqrt(key_sq / model_width + EPSILON)[:, None]
-    query_normed = query_proj * query_inv
-    key_normed = key_proj * key_inv
-    q_rot = rotate(
-        (query_normed * query_scale).reshape(seq_len, heads_here, HEAD_DIM),
-        cosine_table,
-        sine_table,
-    ).astype(jnp.bfloat16)
-    k_rot = rotate(
-        (key_normed * key_scale).reshape(seq_len, heads_here, HEAD_DIM), cosine_table, sine_table
-    ).astype(jnp.bfloat16)
-    value_heads = value_low.reshape(seq_len, heads_here, HEAD_DIM)
-    mixed, log_totals = attend(q_rot, k_rot, value_heads, block_row)
-    mixed_low = mixed.astype(jnp.bfloat16)
+        after(expert_local, squares), "dp", axis=0, tiled=True
+    )
+    inverses = lax.rsqrt(squares / model_width + EPSILON).T
+    query_row, key_row = query_scale[None, :], key_scale[None, :]
+    q_rot, k_rot, value_low, mixed_low, log_totals = attend(
+        projected, inverses, query_row, key_row, tables, ids_col, ids_row
+    )
     branch_part = jnp.einsum(
         "sf,df->sd", mixed_low, w_o_t, preferred_element_type=jnp.float32
     ).astype(jnp.bfloat16)
@@ -750,8 +872,14 @@
     hidden_gated, grad_gate_part, grad_up_part, gate_dot = expert_parts(
         normed_two, grad_rows, gate_values, full_experts, ff_here
     )
-    combined, grad_two_part, grad_experts_w = expert_products(
-        hidden_gated, grad_gate_part, grad_up_part, normed_two, grad_rows, full_experts
+    combined = expert_output(hidden_gated, full_experts)
+    grad_two_part, grad_experts_w = expert_products(
+        hidden_gated,
+        grad_gate_part,
+        grad_up_part,
+        normed_two,
+        grad_rows,
+        full_experts,
     )
     ffn_branch = lax.psum_scatter(
         combined, "tensor", scatter_dimension=0, tiled=True
@@ -776,59 +904,51 @@
     grad_out_w = jnp.einsum(
         "sf,sd->df", mixed_low, grad_attn_rows, preferred_element_type=jnp.float32
     ).astype(jnp.bfloat16)
+    grad_mixed = jnp.dot(grad_attn_rows, w_o_t, preferred_element_type=jnp.float32).astype(
+        jnp.bfloat16
+    )
+    query_scaled, key_scaled, grad_value_low, dots, grad_query_gain, grad_key_gain = attend_back(
+        q_rot,
+        k_rot,
+        value_low,
+        grad_mixed,
+        after(log_totals, ffn_branch),
+        projected,
+        inverses,
+        query_row,
+        key_row,
+        tables,
+        ids_col,
+        ids_row,
+    )
+    dots = small_sum(count, after(dots.T, sum_experts), 7).T / model_width
+    query_inv, key_inv = inverses[:, 0:1], inverses[:, 1:2]
+    grad_query_proj = (
+        query_inv * (query_scaled - query_proj * query_inv * dots[:, 0:1])
+    ).astype(jnp.bfloat16)
+    grad_key_proj = (key_inv * (key_scaled - key_proj * key_inv * dots[:, 1:2])).astype(
+        jnp.bfloat16
+    )
+    grad_qkv = jnp.concatenate([grad_query_proj, grad_key_proj, grad_value_low], axis=1)
+    grad_qkv_w = jnp.einsum(
+        "sd,sf->df", normed, grad_qkv, preferred_element_type=jnp.float32
+    ).astype(jnp.bfloat16)
     grad_router_wide = jnp.pad(grad_router, ((0, 0), (0, 128 - EXPERTS))).astype(jnp.bfloat16)
-    sum_out_router = lax.psum_scatter(
-        jnp.concatenate([grad_out_w, grad_router_wide], axis=1),
+    sum_heads = lax.psum_scatter(
+        jnp.concatenate([grad_qkv_w, grad_out_w, grad_router_wide], axis=1),
         "dp",
         scatter_dimension=0,
         tiled=True,
     ).astype(jnp.float32)
-    grad_mixed = jnp.dot(grad_attn_rows, w_o_t, preferred_element_type=jnp.float32).astype(
-        jnp.bfloat16
-    )
-    grad_q_rot, grad_k_rot, grad_v = attend_back(
-        q_rot,
-        k_rot,
-        value_heads,
-        block_row,
-        log_totals,
-        grad_mixed.reshape(seq_len, heads_here, HEAD_DIM),
-    )
-    grad_query_normed = rotate_back(grad_q_rot, cosine_table, sine_table).reshape(
-        seq_len, head_cols
-    )
-    grad_key_normed = rotate_back(grad_k_rot, cosine_table, sine_table).reshape(seq_len, head_cols)
-    grad_query_gain = jnp.sum(grad_query_normed * query_normed, axis=0)
-    grad_key_gain = jnp.sum(grad_key_normed * key_normed, axis=0)
-    query_scaled = grad_query_normed * query_scale
-    key_scaled = grad_key_normed * key_scale
-    dots = jnp.stack(
-        [jnp.sum(query_scaled * query_normed, axis=1), jnp.sum(key_scaled * key_normed, axis=1)]
-    )
-    query_dot, key_dot = small_sum(count, after(dots, sum_experts), 7)
-    grad_query_proj = (
-        query_inv * (query_scaled - query_normed * (query_dot / model_width)[:, None])
-    ).astype(jnp.bfloat16)
-    grad_key_proj = (key_inv * (key_scaled - key_normed * (key_dot / model_width)[:, None])).astype(
-        jnp.bfloat16
-    )
-    grad_value_low = grad_v.reshape(seq_len, head_cols).astype(jnp.bfloat16)
-    grad_qkv = jnp.concatenate([grad_query_proj, grad_key_proj, grad_value_low], axis=1)
-    grad_qkv_w = jnp.einsum(
-        "sd,sf->df", normed, grad_qkv, preferred_element_type=jnp.float32
-    ).astype(jnp.bfloat16)
     grad_normed_part = jnp.einsum(
         "sf,df->sd", grad_qkv, w_qkv, preferred_element_type=jnp.float32
     ).astype(jnp.bfloat16)
     grad_source, grad_attn_gain = end_exchange(
-        count, grad_normed_part, grad_middle, tokens, after(attn_scale[None, :], ffn_branch)
-    )
-    sum_out_router = after(sum_out_router, grad_attn_gain[None])
-    sum_out = sum_out_router[:, :head_cols]
-    sum_router = sum_out_router[:, head_cols : head_cols + EXPERTS]
+        count, grad_normed_part, grad_middle, tokens, attn_scale[None, :]
+    )
     zero_cols = jnp.zeros((model_width,), jnp.float32)
-    query_gain_full = lax.dynamic_update_slice_in_dim(zero_cols, grad_query_gain, col_start, 0)
-    key_gain_full = lax.dynamic_update_slice_in_dim(zero_cols, grad_key_gain, col_start, 0)
+    query_gain_full = lax.dynamic_update_slice_in_dim(zero_cols, grad_query_gain[0], col_start, 0)
+    key_gain_full = lax.dynamic_update_slice_in_dim(zero_cols, grad_key_gain[0], col_start, 0)
     gain_stack = jnp.stack([grad_attn_gain, query_gain_full, key_gain_full, grad_ffn_gain])
     dp_count = lax.axis_size("dp")
     total_rows = small_sum(count, gain_stack, 8)
@@ -838,9 +958,9 @@
     gain_sums = lax.dynamic_slice_in_dim(
         total_rows, (dp_rank * count + tensor_rank) * gain_width, gain_width, 1
     )
-    sum_qkv = lax.psum_scatter(grad_qkv_w, "dp", scatter_dimension=0, tiled=True).astype(
-        jnp.float32
-    )
+    sum_qkv = sum_heads[:, : 3 * head_cols]
+    sum_out = sum_heads[:, 3 * head_cols : 4 * head_cols]
+    sum_router = sum_heads[:, 4 * head_cols : 4 * head_cols + EXPERTS]
     grad_gate, grad_up, grad_down = (
         sum_experts[:, k * hidden_cols : (k + 1) * hidden_cols].reshape(
             shard_width, EXPERTS, ff_here

time: 808 us -> 806 us (level)
  Pallas kernels: 529 us -> 598 us
  waiting for transfers between devices: 0.88 us -> 43.7 us
  other arithmetic: 69.8 us -> 30.1 us
  matrix products: 90 us -> 51.9 us
  local copies, waits for them, and re-layouts: 80.9 us -> 44 us
    pallas_call x1 -> x4, Pallas kernels: 61.7 us -> 105 us  [the longest x1 53 us: expert_products(): pl.pallas_call(product_kernel, grid=(width // tile,), out_shape=(flat, ja...]
    dot_general x14 -> x0, matrix products: 36 us -> none  [the longest x2 7.73 us: back_block(): jnp.einsum('hqk,qhd->khd', grad_low, q_block, preferred_element_type=jnp....]
    all_gather x3 -> x2, waiting for transfers between devices: 0.02 us -> 30.7 us  [the longest x1 30.7 us: local(): lax.all_gather(after(expert_local, squares), 'dp', axis=0, tiled=True)]
    while x61 -> x0, local copies, waits for them, and re-layouts: 21.4 us -> none
    pallas_call x4, Pallas kernels: 390 us -> 411 us  [line_exchange(): pl.pallas_call(kernel, out_shape=tuple(shapes), in_specs=[pl.BlockSpec(me...]
    reduce_scatter x1, waiting for transfers between devices: 0.01 us -> 13 us  [local(): lax.psum_scatter(grad_experts_w, 'dp', scatter_dimension=0, tiled=True)]
    convert_element_type x6 -> x2, other arithmetic: 17.2 us -> 5.83 us  [the longest x1 4.33 us: local(): grad_query_proj = (query_inv * (query_scaled - query_proj * query_inv * d...]
    reshape x4 -> x0, local copies, waits for them, and re-layouts: 9.74 us -> none  [the longest x3 6.61 us: local(): (query_normed * query_scale).reshape(seq_len, heads_here, HEAD_DIM)]
  transfers between devices with their start and end apart: 8 -> 6, of which waited for: 0 -> 2; matrix products, arithmetic and copies ran while one was open for 27% -> 10% of each run, Pallas kernels for 53% -> 68%
where the time goes in v5:
time: 806 us; the launch traced here: 796 us
  Pallas kernels  598 us (74%)
  matrix products  51.9 us (6%)
  local copies, waits for them, and re-layouts  44 us (5%)
  waiting for transfers between devices  43.7 us (5%)
  other arithmetic  30.1 us (4%)
  between operations  17.8 us (2%)
  blocking collectives  10.6 us (1%)
    pallas_call x4, Pallas kernels, line_exchange(): pl.pallas_call(kernel, out_shape=tuple(shapes), in_specs=[pl.BlockSpec(me...  411 us
    pallas_call x1, Pallas kernels, expert_products(): pl.pallas_call(product_kernel, grid=(width // tile,), out_shape=(flat, ja...  53 us
    pallas_call x5, Pallas kernels, small_sum(): pl.pallas_call(kernel, out_shape=jax.ShapeDtypeStruct(values.shape, jnp.f...  42.9 us
    pallas_call x1, Pallas kernels, expert_parts(): pl.pallas_call(expert_kernel, grid=(EXPERTS,), out_shape=(part, part, par...  39.4 us
    all_gather x1, waiting for transfers between devices, local(): lax.all_gather(after(expert_local, squares), 'dp', axis=0, tiled=True)  30.7 us
    unnamed x68, local copies, waits for them, and re-layouts  24.3 us
    pallas_call x1, Pallas kernels, attend_back(): pl.pallas_call(attend_back_kernel, grid=(heads,), out_shape=(wide, wide,...  24.1 us
  transfers between devices with their start and end apart: 6, of which 2 were waited for; matrix products, arithmetic and copies ran while one was open for 10% of the time, Pallas kernels for 68%

profile of v5, /device:TPU:0, one launch (start us, length us, event | category | flops | bytes accessed | tf_op | source)
XLA Modules:
  0.0 796.4 jit_solution(6731851776820403467)
XLA Ops:
  7.3 1.1 copy.49
  8.4 1.1 copy.50
  9.5 1.1 copy.51
  10.6 2.1 pad_maximum_fusion.3
  12.9 10.6 %all_gather.12 = bf16[2048,12]{0,1:T(8,128)(2,1)S(1)} all-gather(bf16[256,12]{0,1:T(8,128)(2,1)S(1)} %concatenate.15), channel_id=1, replica_groups=mesh['dp'=8,'tensor'=4] {'dp'}, dimensions={0}, use_global_device_ids=true | all-gather | bytes 55296 | tf_op jit(solution)/shard_map/all_gather | solution.py:819
  24.1 78.0 %shard_map.281 = bf16[4,16,16,2048]{3,2,1,0:T(8,128)(2,1)} custom-call(bf16[16,16,2048]{2,1,0:T(8,128)(2,1)} %bitcast.119, f32[1,2048]{1,0:T(1,128)} %get-tuple-element.105.refs_1_.refs_3_), custom_call_target="tpu_custom_call" | custom-call | bytes 188743680 | tf_op jit(solution)/shard_map/pallas_call | solution.py:469
  102.1 1.2 slice.149
  104.0 1.0 broadcast_add_fusion
  105.2 1.3 copy.73
  106.6 2.3 copy.68
  108.9 10.7 %fusion.4.q_ref.k_ref.v_ref.qp_ref.kp_ref = f32[1024,1536]{1,0:T(8,128)S(1)} fusion(bf16[1024,2048]{1,0:T(8,128)(2,1)} %bitcast.126, bf16[2048,2048]{0,1:T(8,128)(2,1)} %all-gather.4.cloned.1.call-done), kind=kOutput, calls=%fused_computation.6 | convolution fusion | flops 6442450944 | bytes 16777216 | tf_op jit(solution)/shard_map/dot_general | solution.py:849
  119.6 2.7 copy-done.12
  123.2 8.8 %shard_map.282 = f32[2,1024]{1,0:T(2,128)} custom-call(f32[2,1024]{1,0:T(2,128)} %pad_maximum_fusion.5.in_ref), custom_call_target="tpu_custom_call" | custom-call | tf_op jit(solution)/shard_map/pallas_call | solution.py:516
  132.0 1.1 slice.121
  133.9 3.1 maximum_add_fusion
  137.3 2.3 reduce-window.6
  140.4 15.7 %shard_map.283 = (bf16[1024,512]{1,0:T(8,128)(2,1)S(1)}, bf16[1024,512]{1,0:T(8,128)(2,1)S(1)}, bf16[1024,512]{1,0:T(8,128)(2,1)S(1)}, bf16[1024,512]{1,0:T(8,128)(2,1)}, f32[1024,4]{1,0:T(8,128)S(1)}) custom-call(f32[1024,1536]{1,0:T(8,128)} %copy-done.12, f32[1024,1536]{1,0:T(8,128)} %copy-done.12, f32[1024,1536]{1,0:T(8,128)} %copy-done.12, ...), custom_call_target="tpu_custom_call" | custom-call | flops 10737418240 | bytes 6291456 | tf_op jit(solution)/shard_map/pallas_call | solution.py:92
  156.1 7.4 convolution_convert_fusion.1
  163.5 131.0 %shard_map.284 = (bf16[4,16,16,2048]{3,2,1,0:T(8,128)(2,1)}, f32[16,16,2048]{2,1,0:T(8,128)}) custom-call(bf16[4,16,16,2048]{3,2,1,0:T(8,128)(2,1)} %bitcast.128, bf16[16,16,2048]{2,1,0:T(8,128)(2,1)} %bitcast.120, f32[1,2048]{1,0:T(1,128)} %get-tuple-element.102.refs_2_.refs_4_), custom_call_target="tpu_custom_call" | custom-call | bytes 251658240 | tf_op jit(solution)/shard_map/pallas_call | solution.py:469
  294.4 3.4 fusion.40
  297.9 1.0 copy.57.gates_ref
  298.9 30.7 %all-gather.8.cloned.1.call-done.wg_ref.wu_ref.wd_ref.w_ref = bf16[2048,6144]{1,0:T(8,128)(2,1)} async-done(((bf16[256,6144]{1,0:T(8,128)(2,1)}), bf16[2048,6144]{1,0:T(8,128)(2,1)}) %all-gather.8.cloned.1.call-update) | async-done | bytes 25165840 | tf_op jit(solution)/shard_map/all_gather | solution.py:856
  329.6 39.4 %shard_map.285 = (bf16[1024,2048]{1,0:T(8,128)(2,1)}, bf16[1024,2048]{1,0:T(8,128)(2,1)}, bf16[1024,2048]{1,0:T(8,128)(2,1)}, f32[1024,8]{1,0:T(8,128)}) custom-call(bf16[1024,2048]{1,0:T(8,128)(2,1)} %bitcast.116, bf16[1024,2048]{1,0:T(8,128)(2,1)} %all-gather.6.cloned.1.call-done.c_ref, f32[1024,8]{1,0:T(8,128)} %copy.57.gates_ref, ...), custom_call_target="tpu_custom_call" | custom-call | flops 25769803776 | bytes 25165824 | tf_op jit(solution)/shard_map/pallas_call | solution.py:691
  369.0 2.2 copy-done.1
  371.2 12.0 %shard_map.286 = bf16[1024,2048]{1,0:T(8,128)(2,1)S(1)} custom-call(bf16[1024,2048]{1,0:T(8,128)(2,1)S(1)} %copy-done.1, bf16[2048,6144]{1,0:T(8,128)(2,1)} %all-gather.8.cloned.1.call-done.wg_ref.wu_ref.wd_ref.w_ref), custom_call_target="tpu_custom_call" | custom-call | flops 8589934592 | bytes 8388608 | tf_op jit(solution)/shard_map/pallas_call | solution.py:769
  383.2 2.1 copy-done
  385.3 53.0 %shard_map.287 = (bf16[1024,2048]{1,0:T(8,128)(2,1)}, bf16[2048,6144]{1,0:T(8,128)(2,1)}) custom-call(bf16[1024,2048]{1,0:T(8,128)(2,1)} %get-tuple-element.41.hg_ref, bf16[1024,2048]{1,0:T(8,128)(2,1)} %get-tuple-element.45.dg_ref, bf16[1024,2048]{1,0:T(8,128)(2,1)} %get-tuple-element.46.du_ref, bf16[1024,2048]{1,0:T(8,128)(2,1)} %bitcast.117, ...), custom_call_target="tpu_custom_call" | custom-call | flops 42949672960 | bytes 50331648 | tf_op jit(solution)/shard_map/pallas_call | solution.py:746
  438.5 0.9 copy-done.19
  440.2 12.1 %shard_map.288 = f32[8,1024]{1,0:T(8,128)} custom-call(f32[8,1024]{1,0:T(8,128)} %fusion.16.in_ref), custom_call_target="tpu_custom_call" | custom-call | tf_op jit(solution)/shard_map/pallas_call | solution.py:516
  452.3 0.8 fusion.19
  453.1 0.8 fusion.21
  453.9 1.8 fusion.26
  455.7 119.7 %shard_map.289 = (bf16[4,16,16,2048]{3,2,1,0:T(8,128)(2,1)}, f32[16,16,2048]{2,1,0:T(8,128)}, f32[1,2048]{1,0:T(1,128)}) custom-call(bf16[4,16,16,2048]{3,2,1,0:T(8,128)(2,1)} %bitcast.132, f32[16,16,2048]{2,1,0:T(8,128)} %bitcast.122, f32[16,16,2048]{2,1,0:T(8,128)} %get-tuple-element.39.refs_2_, bf16[16,16,2048]{2,1,0:T(8,128)(2,1)} %bitcast.133, ...), custom_call_target="tpu_custom_call" | custom-call | bytes 251658240 | tf_op jit(solution)/shard_map/pallas_call | solution.py:469
  576.0 1.6 copy-done.24
  578.0 3.8 convolution_convert_fusion.2
  581.8 5.0 fusion.13.g_ref
  586.8 1.1 slice.153
  588.6 1.2 copy-done.6
  589.8 24.1 %shard_map.290 = (f32[1024,512]{1,0:T(8,128)}, f32[1024,512]{1,0:T(8,128)}, bf16[1024,512]{1,0:T(8,128)(2,1)S(1)}, f32[1024,2]{1,0:T(8,128)S(1)}, f32[1,512]{1,0:T(1,128)S(1)}, /*index=5*/f32[1,512]{1,0:T(1,128)S(1)}) custom-call(bf16[1024,512]{1,0:T(8,128)(2,1)S(1)} %copy-done.6, bf16[1024,512]{1,0:T(8,128)(2,1)} %copy-done.7, bf16[1024,512]{1,0:T(8,128)(2,1)} %copy-done.8, ...), custom_call_target="tpu_custom_call" | custom-call | flops 32212254720 | bytes 6291456 | tf_op jit(solution)/shard_map/pallas_call | solution.py:197
  613.9 1.0 copy-done.9
  614.9 13.0 %reduce-scatter.6.cloned.1.call-done = bf16[256,6144]{1,0:T(8,128)(2,1)} async-done(((bf16[2048,6144]{1,0:T(8,128)(2,1)}), bf16[256,6144]{1,0:T(8,128)(2,1)}) %reduce-scatter.6.cloned.1.call-update) | async-done | bytes 3145744 | tf_op jit(solution)/shard_map/reduce_scatter | solution.py:897
  627.8 1.1 slice.154
  629.7 0.8 copy.75
  630.5 7.0 shard_map.291
  638.2 4.3 multiply_convert_fusion.1
  643.2 7.6 convolution_convert_fusion
  650.8 4.3 fusion.1
  655.2 3.1 fusion.9
  658.3 11.6 %fusion.6 = bf16[1024,2048]{1,0:T(8,128)(2,1)} fusion(bf16[2048,2048]{0,1:T(8,128)(2,1)} %all-gather.4.cloned.1.call-done, bf16[1024,512]{1,0:T(8,128)(2,1)S(1)} %copy-done.10, bf16[1024,512]{1,0:T(8,128)(2,1)S(1)} %get-tuple-element.95, bf16[1024,512]{1,0:T(8,128)(2,1)S(1)} %get-tuple-element.94), kind=kOutput, calls=%fused_computation.8 | convolution fusion | flops 6453985280 | bytes 13631488 | tf_op jit(solution)/shard_map/sf,df->sd/dot_general | solution.py:943
  670.0 82.4 %shard_map.292 = (f32[16,16,2048]{2,1,0:T(8,128)}, f32[1,2048]{1,0:T(1,128)}) custom-call(bf16[4,16,16,2048]{3,2,1,0:T(8,128)(2,1)} %bitcast.131, f32[16,16,2048]{2,1,0:T(8,128)} %get-tuple-element.56.refs_1_, bf16[16,16,2048]{2,1,0:T(8,128)(2,1)} %bitcast.121, f32[1,2048]{1,0:T(1,128)} %get-tuple-element.105.refs_1_.refs_3_), custom_call_target="tpu_custom_call" | custom-call | bytes 188743680 | tf_op jit(solution)/shard_map/pallas_call | solution.py:469
  752.4 1.3 pad_maximum_fusion.4.in_ref
  753.7 7.1 shard_map.293.in_ref
  760.9 7.9 shard_map.294
  768.7 2.7 slice_convert_fusion
  771.4 1.5 copy.82
  773.0 1.5 copy.83
  774.5 1.8 copy.69
  777.6 1.5 convert_element_type.111
  779.1 0.8 slice_bitcast_fusion
  779.9 1.2 fusion.35
  781.1 2.0 copy.65
  783.1 2.0 copy.66
  785.2 2.0 copy.67
  787.8 1.3 copy.87
  (105 shorter events, 8.4 us)
Async XLA Ops:
  7.2 5.5 copy-start.25
  7.2 5.5 copy-start.26
  7.2 5.6 copy-start.27
  7.2 5.6 copy-start.28
  7.2 5.6 copy-start.23
  7.2 101.6 %all-gather.4.cloned.1.call-start = ((), (), s32[]{:S(2)}) async-start(), calls=%async_computation.3 | async-start | bytes 9437184 | tf_op jit(solution)/shard_map/all_gather | solution.py:820
  10.5 93.4 %copy-start.15 = (bf16[256,2048]{1,0:T(8,128)(2,1)S(1)}, bf16[256,2048]{1,0:T(8,128)(2,1)}, u32[]{:S(2)}) copy-start(bf16[256,2048]{1,0:T(8,128)(2,1)} %param.19) | copy-start | bytes 3145732
  12.7 286.2 %all-gather.6.cloned.1.call-start = ((), (), s32[]{:S(2)}) async-start(), calls=%async_computation.4 | async-start | bytes 5242880 | tf_op jit(solution)/shard_map/all_gather | solution.py:845
  24.1 81.0 %copy-start.18 = (bf16[8,256,256]{2,1,0:T(8,128)(2,1)S(1)}, bf16[8,256,256]{2,1,0:T(8,128)(2,1)}, u32[]{:S(2)}) copy-start(bf16[8,256,256]{2,1,0:T(8,128)(2,1)} %param.31) | copy-start | bytes 3145732
  105.1 224.5 %all-gather.8.cloned.1.call-start = ((), (), s32[]{:S(2)}) async-start(), calls=%async_computation.5 | async-start | bytes 28311552 | tf_op jit(solution)/shard_map/all_gather | solution.py:856
  119.6 2.7 copy-start.12
  133.8 3.3 copy-start.2
  133.8 3.5 copy-start.21
  133.8 6.3 copy-start.20
  133.8 6.6 copy-start.3
  133.9 6.6 copy-start.4
  137.0 449.8 %reduce-scatter.4.cloned.1.call-start = ((), (), s32[]{:S(2)}) async-start(), calls=%async_computation.6 | async-start | bytes 5242880 | tf_op jit(solution)/shard_map/reduce_scatter | solution.py:884
  156.1 7.4 copy-start.5
  156.1 7.4 copy-start.7
  156.1 7.4 copy-start.8
  369.0 2.2 copy-start.1
  383.2 2.1 copy-start
  385.3 242.5 %reduce-scatter.6.cloned.1.call-start = ((), (), s32[]{:S(2)}) async-start(), calls=%async_computation.7 | async-start | bytes 28311552 | tf_op jit(solution)/shard_map/reduce_scatter | solution.py:897
  438.4 1.0 copy-start.19
  438.4 339.2 %reduce-scatter.8.cloned.1.call-start = ((), (), s32[]{:S(2)}) async-start(), calls=%async_computation.8 | async-start | bytes 10027008 | tf_op jit(solution)/shard_map/reduce_scatter | solution.py:937
  455.7 119.7 %copy-start.11 = (bf16[4,16,16,2048]{3,2,1,0:T(8,128)(2,1)S(1)}, bf16[4,16,16,2048]{3,2,1,0:T(8,128)(2,1)}, u32[]{:S(2)}) copy-start(bf16[4,16,16,2048]{3,2,1,0:T(8,128)(2,1)} %get-tuple-element.40) | copy-start | bytes 12582916
  575.4 2.3 copy-start.24
  575.4 2.6 copy-start.29
  588.6 1.2 copy-start.6
  613.9 1.0 copy-start.9
  638.2 4.4 copy-start.10
  638.2 5.0 copy-start.14
  643.2 7.6 copy-start.16
  670.0 82.4 %copy-start.22 = (f32[1,2048]{1,0:T(1,128)S(1)}, f32[1,2048]{1,0:T(1,128)}, u32[]{:S(2)}) copy-start(f32[1,2048]{1,0:T(1,128)} %get-tuple-element.61) | copy-start | bytes 24580
  777.6 2.4 copy-start.13
  779.1 8.7 %copy-start.17 = (f32[16,16,2048]{2,1,0:T(8,128)S(1)}, f32[16,16,2048]{2,1,0:T(8,128)}, u32[]{:S(2)}) copy-start(f32[16,16,2048]{2,1,0:T(8,128)} %get-tuple-element.57) | copy-start | bytes 6291460
Sparse Core Ops, SparseCore 0:
  12.8 58.5 all-gather.3
  105.2 91.6 all-gather.5
  198.7 130.7 all-gather.7
  385.4 78.8 reduce-scatter.3
  467.8 159.9 reduce-scatter.5
  655.3 73.8 reduce-scatter.7

commit v6 on v5

--- a/solution.py
+++ b/solution.py
@@ -266,7 +266,7 @@
 
 
 def line_exchange(
-    count, chunks, rows, width, part, extras, out_shapes, epilogue, gather, collective_id, prologue=None
+    count, chunks, rows, width, part, extras, out_shapes, epilogue, gather, collective_id, prologue=None, waits=()
 ):
     reduce = part is not None
     n_extra = len(extras)
@@ -279,6 +279,7 @@
         refs = list(refs)
         part_ref = refs.pop(0) if reduce else None
         extra_refs = [refs.pop(0) for _ in range(n_extra)]
+        del refs[: len(waits)]
         full_ref = refs.pop(0) if gather else None
         out_refs = [refs.pop(0) for _ in range(n_out)]
         if reduce:
@@ -469,7 +470,8 @@
     results = pl.pallas_call(
         kernel,
         out_shape=tuple(shapes),
-        in_specs=[pl.BlockSpec(memory_space=pltpu.VMEM)] * len(operands),
+        in_specs=[pl.BlockSpec(memory_space=pltpu.VMEM)] * len(operands)
+        + [pl.BlockSpec(memory_space=pl.ANY)] * len(waits),
         out_specs=tuple([pl.BlockSpec(memory_space=pltpu.VMEM)] * len(shapes)),
         scratch_shapes=scratch,
         compiler_params=pltpu.CompilerParams(
@@ -480,7 +482,7 @@
             bytes_accessed=block_bytes * (60 if reduce and gather else 45),
             transcendentals=0,
         ),
-    )(*operands)
+    )(*operands, *waits)
     return results
 
 
@@ -527,13 +529,13 @@
     )(values)
 
 
-def start_gather(count, tokens, gain_row):
+def start_gather(count, tokens):
     rows, width = tokens.shape
     step, chunks = CHUNK_ROWS, rows // CHUNK_ROWS
 
     def epilogue(chunk, total, extra_refs, out_refs):
         value = extra_refs[0][chunk].astype(jnp.float32)
-        return (rms_scale(value) * extra_refs[1][...]).astype(jnp.bfloat16)
+        return rms_scale(value).astype(jnp.bfloat16)
 
     (full,) = line_exchange(
         count,
@@ -541,7 +543,7 @@
         step,
         width,
         None,
-        [tokens.reshape(chunks, step, width), gain_row],
+        [tokens.reshape(chunks, step, width)],
         [],
         epilogue,
         True,
@@ -550,7 +552,7 @@
     return full.reshape(count * rows, width)
 
 
-def middle_exchange(count, branch_part, tokens, gain_row):
+def middle_exchange(count, branch_part, tokens, gain_row, waits):
     rows, width = tokens.shape
     step, chunks = CHUNK_ROWS, rows // CHUNK_ROWS
 
@@ -570,6 +572,8 @@
         epilogue,
         True,
         2,
+        None,
+        waits,
     )
     return full.reshape(count * rows, width), middle.reshape(rows, width)
 
@@ -681,7 +685,7 @@
     du_ref[...] = (grad_hidden * silu_gate).astype(jnp.bfloat16)
 
 
-def expert_parts(rows_in, rows_grad, gates, weights, ff_here):
+def expert_parts(rows_in, rows_grad, gates, weights, down, ff_here):
     seq_len, width = rows_in.shape
     hidden_cols = EXPERTS * ff_here
     whole = pl.BlockSpec(memory_space=pltpu.VMEM)
@@ -698,7 +702,7 @@
             whole,
             pl.BlockSpec((width, ff_here), lambda e: (0, e)),
             pl.BlockSpec((width, ff_here), lambda e: (0, EXPERTS + e)),
-            pl.BlockSpec((width, ff_here), lambda e: (0, 2 * EXPERTS + e)),
+            pl.BlockSpec((width, ff_here), lambda e: (0, e)),
         ],
         out_specs=(
             column,
@@ -710,7 +714,7 @@
         cost_estimate=pl.CostEstimate(
             flops=flops, bytes_accessed=weights.size * 2, transcendentals=0
         ),
-    )(rows_in, rows_grad, gates, weights, weights, weights)
+    )(rows_in, rows_grad, gates, weights, weights, down)
 
 
 def product_kernel(hg_ref, dg_ref, du_ref, x_ref, c_ref, w_ref, dx_ref, dw_ref):
@@ -742,12 +746,13 @@
     whole = pl.BlockSpec(memory_space=pltpu.VMEM)
     column = pl.BlockSpec((seq_len, tile), lambda i: (0, i))
     row = pl.BlockSpec((tile, 3 * cols), lambda i: (i, 0))
+    pair = pl.BlockSpec((tile, 2 * cols), lambda i: (i, 0))
     flat = jax.ShapeDtypeStruct((seq_len, width), jnp.bfloat16)
     return pl.pallas_call(
         product_kernel,
         grid=(width // tile,),
         out_shape=(flat, jax.ShapeDtypeStruct((width, 3 * cols), jnp.bfloat16)),
-        in_specs=[whole, whole, whole, column, column, row],
+        in_specs=[whole, whole, whole, column, column, pair],
         out_specs=(column, row),
         compiler_params=pltpu.CompilerParams(vmem_limit_bytes=56 * 1024 * 1024),
         cost_estimate=pl.CostEstimate(
@@ -772,7 +777,7 @@
         out_shape=jax.ShapeDtypeStruct((seq_len, width), jnp.bfloat16),
         in_specs=[
             pl.BlockSpec(memory_space=pltpu.VMEM),
-            pl.BlockSpec((tile, cols), lambda i: (i, 2)),
+            pl.BlockSpec((tile, cols), lambda i: (i, 0)),
         ],
         out_specs=pl.BlockSpec((seq_len, tile), lambda i: (0, i)),
         compiler_params=pltpu.CompilerParams(vmem_limit_bytes=40 * 1024 * 1024),
@@ -780,6 +785,96 @@
             flops=2 * seq_len * width * cols, bytes_accessed=width * cols * 2, transcendentals=0
         ),
     )(hg, weights)
+
+
+def split_kernel(gate_ref, up_ref, down_ref, gate_out, up_out, down_out):
+    gate_out[0] = gate_ref[...].astype(jnp.float32)
+    up_out[0] = up_ref[...].astype(jnp.float32)
+    down_out[0] = down_ref[...].astype(jnp.float32).T
+
+
+def split_experts(sums, ff_here):
+    width = sums.shape[0]
+
+    def part(which):
+        return pl.BlockSpec((width, ff_here), lambda e: (0, which * EXPERTS + e))
+
+    wide = jax.ShapeDtypeStruct((EXPERTS, width, ff_here), jnp.float32)
+    tall = jax.ShapeDtypeStruct((EXPERTS, ff_here, width), jnp.float32)
+    wide_spec = pl.BlockSpec((1, width, ff_here), lambda e: (e, 0, 0))
+    tall_spec = pl.BlockSpec((1, ff_here, width), lambda e: (e, 0, 0))
+    return pl.pallas_call(
+        split_kernel,
+        grid=(EXPERTS,),
+        out_shape=(wide, wide, tall),
+        in_specs=[part(0), part(1), part(2)],
+        out_specs=(wide_spec, wide_spec, tall_spec),
+    )(sums, sums, sums)
+
+
+def scatter_sum(dp_count, count, values, collective_id):
+    total_count = dp_count * count
+
+    def kernel(in_ref, out_ref, slots, send_sems, recv_sems):
+        me = lax.axis_index("dp") * count + lax.axis_index("tensor")
+
+        def peer(offset):
+            other = lax.rem(me + offset, total_count)
+            return other, {"dp": other // count, "tensor": lax.rem(other, count)}
+
+        barrier = pltpu.get_barrier_semaphore()
+
+        def greet(offset, carry):
+            pl.semaphore_signal(
+                barrier, inc=1, device_id=peer(offset)[1], device_id_type=MESH
+            )
+            return carry
+
+        lax.fori_loop(1, total_count, greet, 0)
+        pl.semaphore_wait(barrier, total_count - 1)
+
+        def send(offset):
+            other, device = peer(offset)
+            return pltpu.make_async_remote_copy(
+                src_ref=in_ref.at[other],
+                dst_ref=slots.at[offset - 1],
+                send_sem=send_sems.at[offset - 1],
+                recv_sem=recv_sems.at[offset - 1],
+                device_id=device,
+                device_id_type=MESH,
+            )
+
+        def start(offset, carry):
+            send(offset).start()
+            return carry
+
+        lax.fori_loop(1, total_count, start, 0)
+
+        def collect(offset, total):
+            send(offset).wait_recv()
+            return total + slots[offset - 1]
+
+        out_ref[...] = lax.fori_loop(1, total_count, collect, in_ref[me])
+
+        def finish(offset, carry):
+            send(offset).wait_send()
+            return carry
+
+        lax.fori_loop(1, total_count, finish, 0)
+
+    block = values.shape[1:]
+    return pl.pallas_call(
+        kernel,
+        out_shape=jax.ShapeDtypeStruct(block, jnp.float32),
+        in_specs=[pl.BlockSpec(memory_space=pltpu.VMEM)],
+        out_specs=pl.BlockSpec(memory_space=pltpu.VMEM),
+        scratch_shapes=[
+            pltpu.VMEM((total_count - 1,) + block, jnp.float32),
+            pltpu.SemaphoreType.DMA((total_count - 1,)),
+            pltpu.SemaphoreType.DMA((total_count - 1,)),
+        ],
+        compiler_params=pltpu.CompilerParams(collective_id=collective_id, has_side_effects=True),
+    )(values)
 
 
 def after(value, *others):
@@ -813,20 +908,23 @@
     head_cols = w_query.shape[1]
     ff_here = w_gate.shape[2]
     hidden_cols = EXPERTS * ff_here
-    small = jnp.concatenate(
+    small_cols = jnp.concatenate(
         [attn_gain[:, None], q_gain[:, None], k_gain[:, None], ffn_gain[:, None], w_router], axis=1
     )
-    small = lax.all_gather(small, "dp", axis=0, tiled=True)
+    small_cols = jnp.pad(small_cols, ((0, 0), (0, 128 - small_cols.shape[1])))
     w_heads = lax.all_gather(
-        jnp.concatenate([w_query, w_key, w_value, w_out.T], axis=1), "dp", axis=0, tiled=True
+        jnp.concatenate([w_query, w_key, w_value, w_out.T, small_cols], axis=1), "dp", axis=0, tiled=True
     )
     w_qkv = w_heads[:, : 3 * head_cols]
-    w_o_t = w_heads[:, 3 * head_cols :]
+    w_o_t = w_heads[:, 3 * head_cols : 4 * head_cols]
+    small = w_heads[:, 4 * head_cols : 4 * head_cols + 4 + EXPERTS]
+    full_down = lax.all_gather(
+        w_down.transpose(2, 0, 1).reshape(shard_width, hidden_cols), "dp", axis=0, tiled=True
+    )
     expert_local = jnp.concatenate(
         [
             w_gate.transpose(1, 0, 2).reshape(shard_width, hidden_cols),
             w_up.transpose(1, 0, 2).reshape(shard_width, hidden_cols),
-            w_down.transpose(2, 0, 1).reshape(shard_width, hidden_cols),
         ],
         axis=1,
     )
@@ -841,8 +939,9 @@
     key_scale = lax.dynamic_slice_in_dim(gains[2], col_start, head_cols)
     ffn_scale = gains[3]
     count = lax.axis_size("tensor")
-    normed = start_gather(count, tokens, attn_scale[None, :])
-    grad_rows = lax.all_gather(after(cotangent, normed), "tensor", axis=0, tiled=True)
+    unit_rows = start_gather(count, tokens)
+    normed = (unit_rows.astype(jnp.float32) * attn_scale[None, :]).astype(jnp.bfloat16)
+    grad_rows = lax.all_gather(after(cotangent, unit_rows), "tensor", axis=0, tiled=True)
     seq_len = normed.shape[0]
     ids_row, ids_col = block_ids, block_ids.T
     tables = rope_constants(seq_len)
@@ -853,7 +952,7 @@
         [jnp.sum(query_proj * query_proj, axis=1), jnp.sum(key_proj * key_proj, axis=1)]
     )
     squares = small_sum(count, squares, 5)
-    full_experts = lax.all_gather(
+    full_gate_up = lax.all_gather(
         after(expert_local, squares), "dp", axis=0, tiled=True
     )
     inverses = lax.rsqrt(squares / model_width + EPSILON).T
@@ -864,22 +963,24 @@
     branch_part = jnp.einsum(
         "sf,df->sd", mixed_low, w_o_t, preferred_element_type=jnp.float32
     ).astype(jnp.bfloat16)
-    normed_two, middle = middle_exchange(count, branch_part, tokens, ffn_scale[None, :])
+    normed_two, middle = middle_exchange(
+        count, branch_part, tokens, ffn_scale[None, :], (full_down,)
+    )
     logits = jnp.dot(normed_two, full_router, preferred_element_type=jnp.float32)
     router_probs = jax.nn.softmax(logits, axis=-1)
     kept = kept_mask(routes)
     gate_values = router_probs * kept
     hidden_gated, grad_gate_part, grad_up_part, gate_dot = expert_parts(
-        normed_two, grad_rows, gate_values, full_experts, ff_here
-    )
-    combined = expert_output(hidden_gated, full_experts)
+        normed_two, grad_rows, gate_values, full_gate_up, full_down, ff_here
+    )
+    combined = expert_output(hidden_gated, full_down)
     grad_two_part, grad_experts_w = expert_products(
         hidden_gated,
         grad_gate_part,
         grad_up_part,
         normed_two,
         grad_rows,
-        full_experts,
+        full_gate_up,
     )
     ffn_branch = lax.psum_scatter(
         combined, "tensor", scatter_dimension=0, tiled=True
@@ -930,8 +1031,9 @@
         jnp.bfloat16
     )
     grad_qkv = jnp.concatenate([grad_query_proj, grad_key_proj, grad_value_low], axis=1)
-    grad_qkv_w = jnp.einsum(
-        "sd,sf->df", normed, grad_qkv, preferred_element_type=jnp.float32
+    grad_qkv_w = (
+        jnp.einsum("sd,sf->df", unit_rows, grad_qkv, preferred_element_type=jnp.float32)
+        * attn_scale[:, None]
     ).astype(jnp.bfloat16)
     grad_router_wide = jnp.pad(grad_router, ((0, 0), (0, 128 - EXPERTS))).astype(jnp.bfloat16)
     sum_heads = lax.psum_scatter(
@@ -951,25 +1053,14 @@
     key_gain_full = lax.dynamic_update_slice_in_dim(zero_cols, grad_key_gain[0], col_start, 0)
     gain_stack = jnp.stack([grad_attn_gain, query_gain_full, key_gain_full, grad_ffn_gain])
     dp_count = lax.axis_size("dp")
-    total_rows = small_sum(count, gain_stack, 8)
-    total_rows = small_sum(dp_count, total_rows, 9, "dp")
-    dp_rank = lax.axis_index("dp")
     gain_width = model_width // (dp_count * count)
-    gain_sums = lax.dynamic_slice_in_dim(
-        total_rows, (dp_rank * count + tensor_rank) * gain_width, gain_width, 1
-    )
+    gain_blocks = gain_stack.reshape(4, dp_count * count, gain_width).transpose(1, 0, 2)
+    gain_blocks = jnp.pad(gain_blocks, ((0, 0), (0, 4), (0, 128 - gain_width)))
+    gain_sums = scatter_sum(dp_count, count, gain_blocks, 8)[:4, :gain_width]
     sum_qkv = sum_heads[:, : 3 * head_cols]
     sum_out = sum_heads[:, 3 * head_cols : 4 * head_cols]
     sum_router = sum_heads[:, 4 * head_cols : 4 * head_cols + EXPERTS]
-    grad_gate, grad_up, grad_down = (
-        sum_experts[:, k * hidden_cols : (k + 1) * hidden_cols].reshape(
-            shard_width, EXPERTS, ff_here
-        )
-        for k in range(3)
-    )
-    grad_gate = grad_gate.transpose(1, 0, 2)
-    grad_up = grad_up.transpose(1, 0, 2)
-    grad_down = grad_down.transpose(1, 2, 0)
+    grad_gate, grad_up, grad_down = split_experts(sum_experts, ff_here)
     return (
         output,
         grad_source,
@@ -982,9 +1073,9 @@
         sum_out.T.astype(jnp.float32),
         gain_sums[3],
         sum_router,
-        grad_gate.astype(jnp.float32),
-        grad_up.astype(jnp.float32),
-        grad_down.astype(jnp.float32),
+        grad_gate,
+        grad_up,
+        grad_down,
     )
 
 

time: 806 us -> 835 us (1.036)
  Pallas kernels: 598 us -> 639 us
  blocking collectives: 10.6 us -> 0 us
    pallas_call x4, Pallas kernels: 411 us -> 452 us  [line_exchange(): pl.pallas_call(kernel, out_shape=tuple(shapes), in_specs=[pl.BlockSpec(me...]
    pallas_call x0 -> x2, Pallas kernels: none -> 18 us  [the longest x1 11 us: scatter_sum(): pl.pallas_call(kernel, out_shape=jax.ShapeDtypeStruct(block, jnp.float32)...]
    pallas_call x5 -> x3, Pallas kernels: 42.9 us -> 26.1 us  [small_sum(): pl.pallas_call(kernel, out_shape=jax.ShapeDtypeStruct(values.shape, jnp.f...]
    all_gather x1 -> x0, blocking collectives: 10.6 us -> none  [local(): small = lax.all_gather(small, 'dp', axis=0, tiled=True)]
    unnamed x68 -> x72, local copies, waits for them, and re-layouts: 24.3 us -> 29.4 us
  transfers between devices with their start and end apart: 6 -> 7, of which waited for: 2 -> 2; matrix products, arithmetic and copies ran while one was open for 10% -> 8% of each run, Pallas kernels for 68% -> 70%
where the time goes in v6:
time: 835 us; the launch traced here: 826 us
  Pallas kernels  639 us (77%)
  matrix products  51.3 us (6%)
  local copies, waits for them, and re-layouts  48.2 us (6%)
  waiting for transfers between devices  46.3 us (6%)
  other arithmetic  22.6 us (3%)
  between operations  17.8 us (2%)
    pallas_call x4, Pallas kernels, line_exchange(): pl.pallas_call(kernel, out_shape=tuple(shapes), in_specs=[pl.BlockSpec(me...  452 us
    pallas_call x1, Pallas kernels, expert_products(): pl.pallas_call(product_kernel, grid=(width // tile,), out_shape=(flat, ja...  52.7 us
    pallas_call x1, Pallas kernels, expert_parts(): pl.pallas_call(expert_kernel, grid=(EXPERTS,), out_shape=(part, part, par...  39.3 us
    all_gather x1, waiting for transfers between devices, local(): lax.all_gather(after(expert_local, squares), 'dp', axis=0, tiled=True)  33.6 us
    unnamed x72, local copies, waits for them, and re-layouts  29.4 us
    pallas_call x3, Pallas kernels, small_sum(): pl.pallas_call(kernel, out_shape=jax.ShapeDtypeStruct(values.shape, jnp.f...  26.1 us
    pallas_call x1, Pallas kernels, attend_back(): pl.pallas_call(attend_back_kernel, grid=(heads,), out_shape=(wide, wide,...  23.5 us
  transfers between devices with their start and end apart: 7, of which 2 were waited for; matrix products, arithmetic and copies ran while one was open for 8% of the time, Pallas kernels for 70%

profile of v6, /device:TPU:0, one launch (start us, length us, event | category | flops | bytes accessed | tf_op | source)
XLA Modules:
  0.0 825.9 jit_solution(8799673558020425086)
XLA Ops:
  7.2 1.2 copy.46
  8.4 1.1 copy.47
  9.5 1.1 copy.48
  13.3 1.0 bitcast_dynamic-update-slice_fusion
  14.3 0.8 concatenate.15
  15.1 1.0 copy-done.18
  16.2 1.4 copy.63
  17.7 78.3 %shard_map.281 = bf16[4,16,16,2048]{3,2,1,0:T(8,128)(2,1)} custom-call(bf16[16,16,2048]{2,1,0:T(8,128)(2,1)} %bitcast.108), custom_call_target="tpu_custom_call" | custom-call | bytes 188743680 | tf_op jit(solution)/shard_map/pallas_call | solution.py:470
  96.0 1.2 slice.145
  97.9 1.0 broadcast_add_fusion
  99.1 1.3 copy.64
  100.5 0.8 convert_bitcast_fusion
  101.9 10.1 %fusion.5.q_ref.k_ref.v_ref.qp_ref.kp_ref = f32[1024,1536]{1,0:T(8,128)S(1)} fusion(bf16[2048,2176]{0,1:T(8,128)(2,1)} %all-gather.5.cloned.1.call-done, bf16[1024,2048]{1,0:T(8,128)(2,1)} %bitcast.114, f32[2048]{0:T(1024)S(1)} %bitcast.131), kind=kOutput, calls=%fused_computation.8 | convolution fusion | flops 6448742400 | bytes 16785408 | tf_op jit(solution)/shard_map/dot_general | solution.py:948
  112.0 2.6 copy-done.12
  115.6 6.8 shard_map.282
  122.4 1.2 slice.120
  124.3 1.7 maximum_add_fusion
  126.4 2.3 reduce-window.6
  129.5 15.7 %shard_map.283 = (bf16[1024,512]{1,0:T(8,128)(2,1)S(1)}, bf16[1024,512]{1,0:T(8,128)(2,1)S(1)}, bf16[1024,512]{1,0:T(8,128)(2,1)S(1)}, bf16[1024,512]{1,0:T(8,128)(2,1)}, f32[1024,4]{1,0:T(8,128)S(1)}) custom-call(f32[1024,1536]{1,0:T(8,128)} %copy-done.12, f32[1024,1536]{1,0:T(8,128)} %copy-done.12, f32[1024,1536]{1,0:T(8,128)} %copy-done.12, ...), custom_call_target="tpu_custom_call" | custom-call | flops 10737418240 | bytes 6291456 | tf_op jit(solution)/shard_map/pallas_call | solution.py:92
  145.2 1.0 copy-done.5
  146.2 1.0 copy-done.7
  147.2 1.0 copy-done.8
  148.2 6.3 convolution_convert_fusion
  154.5 171.6 %shard_map.284 = (bf16[4,16,16,2048]{3,2,1,0:T(8,128)(2,1)}, f32[16,16,2048]{2,1,0:T(8,128)}) custom-call(bf16[4,16,16,2048]{3,2,1,0:T(8,128)(2,1)} %bitcast.112, bf16[16,16,2048]{2,1,0:T(8,128)(2,1)} %bitcast.109, f32[1,2048]{1,0:T(1,128)} %get-tuple-element.105.refs_2_.refs_4_, bf16[2048,2048]{1,0:T(8,128)(2,1)} %all-gather.7.cloned.1.call-done.refs_3_.wd_ref.w_ref), custom_call_target="tpu_custom_call" | custom-call | bytes 251658240 | tf_op jit(solution)/shard_map/pallas_call | solution.py:470
  326.0 3.4 fusion.42
  329.5 1.0 copy.54.gates_ref
  330.5 33.6 %all-gather.11.cloned.1.call-done.wg_ref.wu_ref.w_ref = bf16[2048,4096]{1,0:T(8,128)(2,1)} async-done(((bf16[256,4096]{1,0:T(8,128)(2,1)}), bf16[2048,4096]{1,0:T(8,128)(2,1)}) %all-gather.11.cloned.1.call-update) | async-done | bytes 16777232 | tf_op jit(solution)/shard_map/all_gather | solution.py:955
  364.1 39.3 %shard_map.285 = (bf16[1024,2048]{1,0:T(8,128)(2,1)}, bf16[1024,2048]{1,0:T(8,128)(2,1)}, bf16[1024,2048]{1,0:T(8,128)(2,1)}, f32[1024,8]{1,0:T(8,128)}) custom-call(bf16[1024,2048]{1,0:T(8,128)(2,1)} %bitcast.105, bf16[1024,2048]{1,0:T(8,128)(2,1)} %all-gather.9.cloned.1.call-done.c_ref, f32[1024,8]{1,0:T(8,128)} %copy.54.gates_ref, ...), custom_call_target="tpu_custom_call" | custom-call | flops 25769803776 | bytes 16777216 | tf_op jit(solution)/shard_map/pallas_call | solution.py:695
  403.4 2.2 copy-done.4
  405.6 12.0 %shard_map.286 = bf16[1024,2048]{1,0:T(8,128)(2,1)S(1)} custom-call(bf16[1024,2048]{1,0:T(8,128)(2,1)S(1)} %copy-done.4, bf16[2048,2048]{1,0:T(8,128)(2,1)} %all-gather.7.cloned.1.call-done.refs_3_.wd_ref.w_ref), custom_call_target="tpu_custom_call" | custom-call | flops 8589934592 | bytes 8388608 | tf_op jit(solution)/shard_map/pallas_call | solution.py:774
  417.6 2.0 copy-done
  419.7 52.7 %shard_map.287 = (bf16[1024,2048]{1,0:T(8,128)(2,1)}, bf16[2048,6144]{1,0:T(8,128)(2,1)}) custom-call(bf16[1024,2048]{1,0:T(8,128)(2,1)} %get-tuple-element.44.hg_ref, bf16[1024,2048]{1,0:T(8,128)(2,1)} %get-tuple-element.48.dg_ref, bf16[1024,2048]{1,0:T(8,128)(2,1)} %get-tuple-element.49.du_ref, bf16[1024,2048]{1,0:T(8,128)(2,1)} %bitcast.106, ...), custom_call_target="tpu_custom_call" | custom-call | flops 42949672960 | bytes 33554432 | tf_op jit(solution)/shard_map/pallas_call | solution.py:751
  472.5 0.9 copy-done.21
  474.2 12.3 %shard_map.288 = f32[8,1024]{1,0:T(8,128)} custom-call(f32[8,1024]{1,0:T(8,128)} %fusion.18.in_ref), custom_call_target="tpu_custom_call" | custom-call | tf_op jit(solution)/shard_map/pallas_call | solution.py:518
  486.5 0.8 fusion.21
  487.3 0.8 fusion.23
  488.0 2.6 fusion.28
  490.7 119.7 %shard_map.289 = (bf16[4,16,16,2048]{3,2,1,0:T(8,128)(2,1)}, f32[16,16,2048]{2,1,0:T(8,128)}, f32[1,2048]{1,0:T(1,128)}) custom-call(bf16[4,16,16,2048]{3,2,1,0:T(8,128)(2,1)} %bitcast.119, f32[16,16,2048]{2,1,0:T(8,128)} %bitcast.111, f32[16,16,2048]{2,1,0:T(8,128)} %get-tuple-element.42.refs_2_, bf16[16,16,2048]{2,1,0:T(8,128)(2,1)} %bitcast.120, ...), custom_call_target="tpu_custom_call" | custom-call | bytes 251658240 | tf_op jit(solution)/shard_map/pallas_call | solution.py:470
  611.1 1.6 copy-done.28
  613.0 3.8 convolution_convert_fusion.1
  616.9 5.0 fusion.15.g_ref
  621.8 1.1 slice.149
  623.7 1.4 copy-done.6
  625.1 23.5 %shard_map.290 = (f32[1024,512]{1,0:T(8,128)}, f32[1024,512]{1,0:T(8,128)}, bf16[1024,512]{1,0:T(8,128)(2,1)S(1)}, f32[1024,2]{1,0:T(8,128)S(1)}, f32[1,512]{1,0:T(1,128)S(1)}, /*index=5*/f32[1,512]{1,0:T(1,128)S(1)}) custom-call(bf16[1024,512]{1,0:T(8,128)(2,1)S(1)} %copy-done.6, bf16[1024,512]{1,0:T(8,128)(2,1)} %copy-done.7, bf16[1024,512]{1,0:T(8,128)(2,1)} %copy-done.8, ...), custom_call_target="tpu_custom_call" | custom-call | flops 32212254720 | bytes 6291456 | tf_op jit(solution)/shard_map/pallas_call | solution.py:197
  648.6 1.0 copy-done.9
  649.6 12.6 %reduce-scatter.6.cloned.1.call-done.gate_ref.up_ref.down_ref = bf16[256,6144]{1,0:T(8,128)(2,1)} async-done(((bf16[2048,6144]{1,0:T(8,128)(2,1)}), bf16[256,6144]{1,0:T(8,128)(2,1)}) %reduce-scatter.6.cloned.1.call-update) | async-done | bytes 3145744 | tf_op jit(solution)/shard_map/reduce_scatter | solution.py:998
  662.2 1.1 slice.150
  664.1 0.8 copy.67
  664.9 7.0 shard_map.291
  672.7 4.3 multiply_convert_fusion.4
  677.6 7.9 fusion.2
  685.5 4.2 fusion.1
  689.8 3.1 fusion.11
  692.9 11.6 %fusion.8 = bf16[1024,2048]{1,0:T(8,128)(2,1)} fusion(bf16[2048,2176]{0,1:T(8,128)(2,1)} %all-gather.5.cloned.1.call-done, bf16[1024,512]{1,0:T(8,128)(2,1)S(1)} %copy-done.10, bf16[1024,512]{1,0:T(8,128)(2,1)S(1)} %get-tuple-element.101, bf16[1024,512]{1,0:T(8,128)(2,1)S(1)} %get-tuple-element.100), kind=kOutput, calls=%fused_computation.11 | convolution fusion | flops 6453985280 | bytes 13631488 | tf_op jit(solution)/shard_map/sf,df->sd/dot_general | solution.py:1045
  704.5 82.4 %shard_map.292 = (f32[16,16,2048]{2,1,0:T(8,128)}, f32[1,2048]{1,0:T(1,128)}) custom-call(bf16[4,16,16,2048]{3,2,1,0:T(8,128)(2,1)} %bitcast.118, f32[16,16,2048]{2,1,0:T(8,128)} %get-tuple-element.59.refs_1_, bf16[16,16,2048]{2,1,0:T(8,128)(2,1)} %bitcast.110, f32[1,2048]{1,0:T(1,128)} %copy-done.23), custom_call_target="tpu_custom_call" | custom-call | bytes 188743680 | tf_op jit(solution)/shard_map/pallas_call | solution.py:470
  786.9 0.7 pad_maximum_fusion.3
  788.5 11.0 %shard_map.293 = f32[8,128]{1,0:T(8,128)} custom-call(f32[32,8,128]{2,1,0:T(8,128)} %pad.14.in_ref), custom_call_target="tpu_custom_call" | custom-call | tf_op jit(solution)/shard_map/pallas_call | solution.py:866
  799.4 7.0 shard_map.294
  807.0 2.4 fusion.37
  809.4 2.2 copy.60
  811.6 2.0 copy.61
  813.6 2.0 copy.62
  815.8 0.8 slice_bitcast_fusion
  817.2 1.3 copy.82
  (109 shorter events, 11.3 us)
Async XLA Ops:
  7.2 9.0 %copy-start.19 = (bf16[8,256,256]{2,1,0:T(8,128)(2,1)S(1)}, bf16[8,256,256]{2,1,0:T(8,128)(2,1)}, u32[]{:S(2)}) copy-start(bf16[8,256,256]{2,1,0:T(8,128)(2,1)} %param.33) | copy-start | bytes 3145732
  7.2 93.3 %all-gather.5.cloned.1.call-start = ((), (), s32[]{:S(2)}) async-start(), calls=%async_computation.3 | async-start | bytes 10027008 | tf_op jit(solution)/shard_map/all_gather | solution.py:915
  15.1 1.0 copy-start.18
  16.1 138.3 %all-gather.7.cloned.1.call-start = ((), (), s32[]{:S(2)}) async-start(), calls=%async_computation.4 | async-start | bytes 9437184 | tf_op jit(solution)/shard_map/all_gather | solution.py:921
  16.2 81.7 %copy-start.15 = (bf16[256,2048]{1,0:T(8,128)(2,1)S(1)}, bf16[256,2048]{1,0:T(8,128)(2,1)}, u32[]{:S(2)}) copy-start(bf16[256,2048]{1,0:T(8,128)(2,1)} %param.19) | copy-start | bytes 3145732
  17.6 312.9 %all-gather.9.cloned.1.call-start = ((), (), s32[]{:S(2)}) async-start(), calls=%async_computation.5 | async-start | bytes 5242880 | tf_op jit(solution)/shard_map/all_gather | solution.py:944
  17.7 81.3 %copy-start.20 = (bf16[8,256,256]{2,1,0:T(8,128)(2,1)S(1)}, bf16[8,256,256]{2,1,0:T(8,128)(2,1)}, u32[]{:S(2)}) copy-start(bf16[8,256,256]{2,1,0:T(8,128)(2,1)} %param.32) | copy-start | bytes 3145732
  98.9 265.2 %all-gather.11.cloned.1.call-start = ((), (), s32[]{:S(2)}) async-start(), calls=%async_computation.6 | async-start | bytes 18874368 | tf_op jit(solution)/shard_map/all_gather | solution.py:955
  101.9 10.1 %copy-start.23 = (f32[1,2048]{1,0:T(1,128)}, f32[1,2048]{1,0:T(1,128)S(1)}, u32[]{:S(2)}) copy-start(f32[1,2048]{1,0:T(1,128)S(1)} %get-tuple-element.108.refs_3_) | copy-start | bytes 24580
  112.0 2.6 copy-start.12
  114.9 11.2 %copy-start.1 = (s32[1,1024]{1,0:T(1,128)S(1)}, s32[1,1024]{1,0:T(1,128)}, u32[]{:S(2)}) copy-start(s32[1,1024]{1,0:T(1,128)} %row_ref.3) | copy-start | bytes 12292
  114.9 11.4 %copy-start.26 = (s32[1024,2]{0,1:T(2,128)S(1)}, s32[1024,2]{0,1:T(2,128)}, u32[]{:S(2)}) copy-start(s32[1024,2]{0,1:T(2,128)} %param.20) | copy-start | bytes 24580
  115.0 14.5 %copy-start.2 = (f32[1024,128]{1,0:T(8,128)S(1)}, f32[1024,128]{1,0:T(8,128)}, u32[]{:S(2)}) copy-start(f32[1024,128]{1,0:T(8,128)} %constant.63.clone.cos_ref) | copy-start | bytes 1572868
  115.0 14.5 %copy-start.3 = (f32[1024,128]{1,0:T(8,128)S(1)}, f32[1024,128]{1,0:T(8,128)}, u32[]{:S(2)}) copy-start(f32[1024,128]{1,0:T(8,128)} %constant.64.clone.sin_ref) | copy-start | bytes 1572868
  122.4 6.8 copy-start.22
  126.1 495.7 %reduce-scatter.4.cloned.1.call-start = ((), (), s32[]{:S(2)}) async-start(), calls=%async_computation.7 | async-start | bytes 5242880 | tf_op jit(solution)/shard_map/reduce_scatter | solution.py:985
  145.2 1.0 copy-start.5
  146.2 1.0 copy-start.7
  147.2 1.0 copy-start.8
  403.4 2.2 copy-start.4
  417.6 2.0 copy-start
  419.6 242.6 %reduce-scatter.6.cloned.1.call-start = ((), (), s32[]{:S(2)}) async-start(), calls=%async_computation.8 | async-start | bytes 28311552 | tf_op jit(solution)/shard_map/reduce_scatter | solution.py:998
  472.4 1.0 copy-start.21
  472.4 334.6 %reduce-scatter.8.cloned.1.call-start = ((), (), s32[]{:S(2)}) async-start(), calls=%async_computation.9 | async-start | bytes 10027008 | tf_op jit(solution)/shard_map/reduce_scatter | solution.py:1039
  490.7 119.8 %copy-start.11 = (bf16[4,16,16,2048]{3,2,1,0:T(8,128)(2,1)S(1)}, bf16[4,16,16,2048]{3,2,1,0:T(8,128)(2,1)}, u32[]{:S(2)}) copy-start(bf16[4,16,16,2048]{3,2,1,0:T(8,128)(2,1)} %get-tuple-element.43) | copy-start | bytes 12582916
  610.4 2.3 copy-start.28
  610.5 2.6 copy-start.29
  623.7 1.5 copy-start.6
  648.6 1.0 copy-start.9
  672.6 4.3 copy-start.10
  672.6 5.0 copy-start.14
  672.6 5.0 copy-start.24
  677.6 7.9 copy-start.16
  704.5 82.4 %copy-start.27 = (f32[1,2048]{1,0:T(1,128)S(1)}, f32[1,2048]{1,0:T(1,128)}, u32[]{:S(2)}) copy-start(f32[1,2048]{1,0:T(1,128)} %get-tuple-element.64) | copy-start | bytes 24580
  799.4 7.0 copy-start.25
  807.0 8.6 %copy-start.13 = (bf16[256,2176]{0,1:T(8,128)(2,1)S(1)}, bf16[256,2176]{0,1:T(8,128)(2,1)}, u32[]{:S(2)}) copy-start(bf16[256,2176]{0,1:T(8,128)(2,1)} %reduce-scatter.8.cloned.1.call-done) | copy-start | bytes 3342340
  809.4 7.9 copy-start.17
Sparse Core Ops, SparseCore 0:
  16.2 60.9 all-gather.4
  79.7 54.2 all-gather.6
  136.2 131.9 all-gather.8
  270.5 93.5 all-gather.10
  419.7 78.8 reduce-scatter.3
  502.2 160.0 reduce-scatter.5
  689.9 73.8 reduce-scatter.7
